TPU v7x, 256 devices: a whole 4x4x8 slice. The times are simulated.
256 devices in a mesh: rep: 8 (over x, z_lo), mp: 32 (over z_hi, y, core).
Axes of the slice: x: 4, y: 4, z: 8 (z_hi: 4, z_lo: 2; z = z_hi * 2 + z_lo), core: 2. Of those that a mesh axis runs over, the one named last changes fastest.
Arguments:
- tokens: bfloat16 [8, 2048, 5120], P('rep', 'mp'), may hold values from -6 to 6
- prompt_ids: int32 [8, 2048], P('rep', 'mp'), may hold values from 0 to 11, never falling along the last dimension, each value on 1 to 512 neighbouring positions
- modulation: float32 [8, 12, 3, 5120], P('rep'), may hold values from -4 to 4
- trainer_up: float32 [5120, 13824], P('mp', 'rep'), may hold values from -0.078125 to 0.078125
- trainer_down: float32 [13824, 5120], P('rep', 'mp'), may hold values from -0.0546875 to 0.0546875
Outputs:
- result: bfloat16 [8, 2048, 5120], P('rep', 'mp')
Inputs may be any that keep to these rules, and one draw needn't show every extreme that they name: `prompt_ids`: along each replica's 2048 tokens the prompt number never falls; each of the 12 prompts has at least one token, and one prompt has exactly a quarter of 2048.
All inputs are finite; a program needn't handle non-finite values.
Results may differ from a plain program's by a relative error of at most 0.023.
Values may be sent and summed in bfloat16 or wider, within the bound.
A program may use at most 192 MiB of HBM per device.

v0:
```python
import jax
import jax.numpy as jnp
from jax import lax
from jax.sharding import PartitionSpec as P


def local(tokens, prompt_ids, modulation, trainer_up, trainer_down):
    as_float = tokens[0].astype(jnp.float32)
    average = jnp.mean(as_float, axis=-1, keepdims=True)
    centred = as_float - average
    variance = jnp.mean(centred * centred, axis=-1, keepdims=True)
    normed = centred / jnp.sqrt(variance + 1e-06)
    prompts_here = modulation.shape[1]
    onehot = (prompt_ids[0][:, None] == jnp.arange(prompts_here, dtype=jnp.int32)[None, :]).astype(
        jnp.float32
    )
    chosen = jnp.einsum("tp,pkd->tkd", onehot, modulation[0], precision=lax.Precision.HIGHEST)
    shift = chosen[:, 0]
    scale = chosen[:, 1]
    gate = chosen[:, 2]
    xin = (normed * (1.0 + scale) + shift).astype(jnp.bfloat16)
    up_half = trainer_up.astype(jnp.bfloat16)
    down_half = trainer_down.astype(jnp.bfloat16)
    up_rows = lax.all_gather(up_half, "rep", axis=1, tiled=True)
    w_up = lax.all_to_all(up_rows, "mp", split_axis=1, concat_axis=0, tiled=True)
    down_columns = lax.all_gather(down_half, "rep", axis=0, tiled=True)
    w_down = lax.all_to_all(down_columns, "mp", split_axis=0, concat_axis=1, tiled=True)
    hidden = jax.nn.gelu(
        jnp.dot(
            lax.all_gather(xin, "mp", axis=0, tiled=True), w_up, preferred_element_type=jnp.float32
        ),
        approximate=True,
    ).astype(jnp.bfloat16)
    mlp = lax.psum_scatter(
        jnp.dot(hidden, w_down, preferred_element_type=jnp.float32).astype(jnp.bfloat16),
        "mp",
        scatter_dimension=0,
        tiled=True,
    ).astype(jnp.float32)
    result = as_float + gate * mlp
    return result.astype(jnp.bfloat16)[None]


def solution(mesh):
    in_specs = (
        P("rep", "mp", None),
        P("rep", "mp"),
        P("rep", None, None, None),
        P("mp", "rep"),
        P("rep", "mp"),
    )
    out_specs = P("rep", "mp", None)
    return jax.shard_map(local, mesh=mesh, in_specs=in_specs, out_specs=out_specs, check_vma=False)
```

profile of v0, /device:TPU:1, one launch (start us, length us, event | category | flops | bytes accessed | tf_op | source)
XLA Modules:
  0.0 793.0 jit_solution(6808156185871499909)
XLA Ops:
  6.5 2.2 convert_bitcast_fusion.2
  8.8 0.0 all-gather.8.cloned.1.call-update
  8.8 0.0 all-gather.10.cloned.1.call-start
  8.8 2.1 convert_bitcast_fusion.1
  11.0 0.0 all-gather.10.cloned.1.call-update
  11.0 0.0 all-gather.6.cloned.1.call-start
  11.1 0.2 convert_reduce_fusion
  11.3 0.3 fusion.17
  11.6 1.8 fusion.24
  13.4 1.9 copy-done
  15.3 1.2 fusion.23
  16.5 0.0 all-gather.6.cloned.1.call-update
  16.5 96.8 %all-gather.8.cloned.1.call-done = bf16[8,1728,160]{1,2,0:T(8,128)(2,1)} async-done(((bf16[1,1728,160]{1,2,0:T(8,128)(2,1)}), bf16[8,1728,160]{1,2,0:T(8,128)(2,1)}) %all-gather.8.cloned.1.call-update) | async-done | bytes 4423696 | tf_op jit(solution)/shard_map/all_gather | solution.py:24
  113.3 7.0 copy.13
  120.3 8.6 %reshape.23 = bf16[13824,160]{0,1:T(8,128)(2,1)} reshape(bf16[8,1728,160]{1,0,2:T(8,128)(2,1)} %copy.13) | data formatting | bytes 8847360
  128.9 13.7 %all_to_all.28 = bf16[160,32,432]{2,1,0:T(8,128)(2,1)} reshape(bf16[160,13824]{1,0:T(8,128)(2,1)} %bitcast.79) | data formatting | bytes 8847360 | tf_op jit(solution)/shard_map/all_to_all | solution.py:25
  142.6 7.8 copy.14
  150.4 9.7 %all-to-all-start = ((bf16[160,32,432]{2,0,1:T(8,128)(2,1)}), bf16[160,32,432]{2,0,1:T(8,128)(2,1)}, u32[]{:S(2)}, u32[]{:S(2)}) async-start(bf16[160,32,432]{2,0,1:T(8,128)(2,1)} %copy.14), calls=%async_computation | async-start | bytes 10485760 | tf_op jit(solution)/shard_map/all_to_all | solution.py:25
  160.1 158.4 %all-gather.10.cloned.1.call-done = bf16[8,1728,160]{1,2,0:T(8,128)(2,1)} async-done(((bf16[1,1728,160]{1,2,0:T(8,128)(2,1)}), bf16[8,1728,160]{1,2,0:T(8,128)(2,1)}) %all-gather.10.cloned.1.call-update) | async-done | bytes 4423696 | tf_op jit(solution)/shard_map/all_gather | solution.py:26
  318.6 6.9 copy.15
  325.4 10.6 %all_to_all.32 = bf16[32,432,160]{1,0,2:T(8,128)(2,1)} reshape(bf16[8,1728,160]{1,0,2:T(8,128)(2,1)} %copy.15) | data formatting | bytes 8847360 | tf_op jit(solution)/shard_map/all_to_all | solution.py:27
  336.0 7.9 %copy.16 = bf16[32,432,160]{1,2,0:T(8,128)(2,1)} copy(bf16[32,432,160]{1,0,2:T(8,128)(2,1)} %all_to_all.32) | data formatting | bytes 8847360 | tf_op jit(solution)/shard_map/all_to_all | solution.py:27
  344.0 0.0 all-to-all-done
  344.0 11.5 %all-to-all-start.1 = ((bf16[32,432,160]{1,2,0:T(8,128)(2,1)}), bf16[32,432,160]{1,2,0:T(8,128)(2,1)}, u32[]{:S(2)}, u32[]{:S(2)}) async-start(bf16[32,432,160]{1,2,0:T(8,128)(2,1)} %copy.16), calls=%async_computation.1 | async-start | bytes 10485760 | tf_op jit(solution)/shard_map/all_to_all | solution.py:27
  355.5 0.3 reduce-scatter.2.cloned.1.call-start
  355.8 208.1 %all-gather.6.cloned.1.call-done = bf16[2048,5120]{1,0:T(8,128)(2,1)} async-done(((bf16[64,5120]{1,0:T(8,128)(2,1)}), bf16[2048,5120]{1,0:T(8,128)(2,1)}) %all-gather.6.cloned.1.call-update) | async-done | bytes 20971536 | tf_op jit(solution)/shard_map/all_gather | solution.py:30
  563.9 15.8 %fusion.49 = bf16[2048,432]{0,1:T(8,128)(2,1)S(1)} fusion(bf16[2048,5120]{1,0:T(8,128)(2,1)} %all-gather.6.cloned.1.call-done, bf16[5120,432]{1,0:T(8,128)(2,1)} %bitcast.11), kind=kOutput, calls=%fused_computation.9.clone.clone.1 | convolution fusion | flops 9067659264 | bytes 27164672 | tf_op jit(solution)/shard_map/dot_general | solution.py:29
  579.7 0.0 all-to-all-done.1
  579.7 16.8 %convolution_convert_fusion = bf16[2048,5120]{1,0:T(8,128)(2,1)} fusion(bf16[432,5120]{0,1:T(8,128)(2,1)} %bitcast.14, bf16[2048,432]{0,1:T(8,128)(2,1)S(1)} %fusion.49), kind=kOutput, calls=%fused_computation | convolution fusion | flops 9070182400 | bytes 27164672 | tf_op jit(solution)/shard_map/dot_general | solution.py:35
  596.5 0.0 reduce-scatter.2.cloned.1.call-update
  596.5 187.5 %reduce-scatter.2.cloned.1.call-done = bf16[64,5120]{1,0:T(8,128)(2,1)} async-done(((bf16[2048,5120]{1,0:T(8,128)(2,1)}), bf16[64,5120]{1,0:T(8,128)(2,1)}) %reduce-scatter.2.cloned.1.call-update) | async-done | bytes 655376 | tf_op jit(solution)/shard_map/reduce_scatter | solution.py:34
  783.9 2.6 fusion.27
  (10 shorter events, 0.0 us)
Async XLA Ops:
  6.5 4.5 copy-start.1
  6.5 5.1 copy-start.3
  6.5 5.1 copy-start.2
  6.5 106.8 %all-gather.8.cloned.1.call-start = ((), (), s32[]{:S(2)}) async-start(), calls=%async_computation.5 | async-start | bytes 5160960 | tf_op jit(solution)/shard_map/all_gather | solution.py:24
  8.8 309.8 %all-gather.10.cloned.1.call-start = ((), (), s32[]{:S(2)}) async-start(), calls=%async_computation.6 | async-start | bytes 5160960 | tf_op jit(solution)/shard_map/all_gather | solution.py:26
  11.0 552.9 %all-gather.6.cloned.1.call-start = ((), (), s32[]{:S(2)}) async-start(), calls=%async_computation.3 | async-start | bytes 21626880 | tf_op jit(solution)/shard_map/all_gather | solution.py:30
  13.4 1.9 copy-start
  150.4 193.6 %all-to-all-start = ((bf16[160,32,432]{2,0,1:T(8,128)(2,1)}), bf16[160,32,432]{2,0,1:T(8,128)(2,1)}, u32[]{:S(2)}, u32[]{:S(2)}) async-start(bf16[160,32,432]{2,0,1:T(8,128)(2,1)} %copy.14), calls=%async_computation | async-start | bytes 10485760 | tf_op jit(solution)/shard_map/all_to_all | solution.py:25
  344.0 235.7 %all-to-all-start.1 = ((bf16[32,432,160]{1,2,0:T(8,128)(2,1)}), bf16[32,432,160]{1,2,0:T(8,128)(2,1)}, u32[]{:S(2)}, u32[]{:S(2)}) async-start(bf16[32,432,160]{1,2,0:T(8,128)(2,1)} %copy.16), calls=%async_computation.1 | async-start | bytes 10485760 | tf_op jit(solution)/shard_map/all_to_all | solution.py:27
  355.5 428.4 %reduce-scatter.2.cloned.1.call-start = ((), (), s32[]{:S(2)}) async-start(), calls=%async_computation.4 | async-start | bytes 21626880 | tf_op jit(solution)/shard_map/reduce_scatter | solution.py:34
Sparse Core Ops, SparseCore 0:
  9.2 104.0 all-gather.7
  115.1 203.4 all-gather.9
  321.1 242.7 all-gather.5
  596.6 187.2 reduce-scatter.1
where the time goes:
time: 794 us; the launch traced here: 793 us
  waiting for transfers between devices  651 us (82%)
  local copies, waits for them, and re-layouts  64.4 us (8%)
  matrix products  34.3 us (4%)
  starting transfers between devices  21.5 us (3%)
  between operations  13.2 us (2%)
  other arithmetic  8.68 us (1%)
    all_gather x1, waiting for transfers between devices, local(): lax.all_gather(xin, 'mp', axis=0, tiled=True)  208 us
    reduce_scatter x1, waiting for transfers between devices, local(): lax.psum_scatter(jnp.dot(hidden, w_down, preferred_element_type=jnp.float...  187 us
    all_gather x1, waiting for transfers between devices, local(): down_columns = lax.all_gather(down_half, 'rep', axis=0, tiled=True)  158 us
    all_gather x1, waiting for transfers between devices, local(): up_rows = lax.all_gather(up_half, 'rep', axis=1, tiled=True)  96.8 us
    all_to_all x2, local copies, waits for them, and re-layouts, local(): lax.all_to_all(up_rows, 'mp', split_axis=1, concat_axis=0, tiled=True)  21.5 us
    all_to_all x2, local copies, waits for them, and re-layouts, local(): lax.all_to_all(down_columns, 'mp', split_axis=0, concat_axis=1, tiled=True)  18.6 us
    dot_general x1, matrix products, local(): jnp.dot(hidden, w_down, preferred_element_type=jnp.float32)  16.8 us
  transfers between devices with their start and end apart: 6, of which 4 were waited for; matrix products, arithmetic and copies ran while one was open for 8% of the time, Pallas kernels for 0%

commit v1 on v0

v1 whole, which is shorter than its diff:
```python
import jax
import jax.numpy as jnp
import numpy as np
from jax import lax
from jax.sharding import Mesh, PartitionSpec as P

MP = ("mc", "core")


def local(tokens, prompt_ids, modulation, trainer_up, trainer_down):
    as_float = tokens[0].astype(jnp.float32)
    average = jnp.mean(as_float, axis=-1, keepdims=True)
    centred = as_float - average
    variance = jnp.mean(centred * centred, axis=-1, keepdims=True)
    normed = centred / jnp.sqrt(variance + 1e-06)
    prompts_here = modulation.shape[1]
    onehot = (prompt_ids[0][:, None] == jnp.arange(prompts_here, dtype=jnp.int32)[None, :]).astype(
        jnp.float32
    )
    chosen = jnp.einsum("tp,pkd->tkd", onehot, modulation[0], precision=lax.Precision.HIGHEST)
    shift = chosen[:, 0]
    scale = chosen[:, 1]
    gate = chosen[:, 2]
    xin = (normed * (1.0 + scale) + shift).astype(jnp.bfloat16)

    n_mp = lax.psum(1, MP)
    rows, cols = trainer_up.shape
    piece = cols // n_mp
    up_half = trainer_up.astype(jnp.bfloat16).reshape(rows, n_mp, piece).transpose(1, 0, 2)
    up_cols = lax.all_to_all(up_half, MP, 0, 0, tiled=True).reshape(n_mp * rows, piece)
    up_mine = lax.all_gather(up_cols, "rep", axis=1, tiled=True)
    up_other = lax.ppermute(up_mine, "core", [(0, 1), (1, 0)])
    w_up = jnp.concatenate([up_mine, up_other], axis=1)

    frows, dcols = trainer_down.shape
    down_half = trainer_down.astype(jnp.bfloat16).reshape(n_mp, piece, dcols)
    down_rows = lax.all_to_all(down_half, MP, 0, 0, tiled=True)
    down_rows = down_rows.reshape(n_mp, piece, dcols).transpose(1, 0, 2).reshape(piece, n_mp * dcols)
    down_mine = lax.all_gather(down_rows, "rep", axis=0, tiled=True)
    down_other = lax.ppermute(down_mine, "core", [(0, 1), (1, 0)])
    w_down = jnp.concatenate([down_mine, down_other], axis=0)

    x_all = lax.all_gather(xin, "mc", axis=0, tiled=True)
    hidden = jax.nn.gelu(
        jnp.dot(x_all, w_up, preferred_element_type=jnp.float32), approximate=True
    ).astype(jnp.bfloat16)
    mlp = lax.psum_scatter(
        jnp.dot(hidden, w_down, preferred_element_type=jnp.float32).astype(jnp.bfloat16),
        "mc",
        scatter_dimension=0,
        tiled=True,
    ).astype(jnp.float32)
    result = as_float + gate * mlp
    return result.astype(jnp.bfloat16)[None]


def solution(mesh):
    n_rep, n_mp = mesh.devices.shape
    chips = Mesh(mesh.devices.reshape(n_rep, n_mp // 2, 2), ("rep", "mc", "core"))
    in_specs = (
        P("rep", MP, None),
        P("rep", MP),
        P("rep", None, None, None),
        P(MP, "rep"),
        P("rep", MP),
    )
    out_specs = P("rep", MP, None)
    return jax.shard_map(local, mesh=chips, in_specs=in_specs, out_specs=out_specs, check_vma=False)
```

time: 794 us -> 586 us (0.74)
  waiting for transfers between devices: 651 us -> 436 us
  blocking collectives: 0 us -> 78.6 us
  local copies, waits for them, and re-layouts: 64.4 us -> 16.9 us
  starting transfers between devices: 21.5 us -> 1.52 us
    all_gather x3, waiting for transfers between devices: 463 us -> 294 us  [the longest x1 131 us: local(): x_all = lax.all_gather(xin, 'mc', axis=0, tiled=True)]
    all_to_all x0 -> x2, blocking collectives: none -> 78.6 us  [the longest x1 41 us: local(): down_rows = lax.all_to_all(down_half, MP, 0, 0, tiled=True)]
    reduce_scatter x1, waiting for transfers between devices: 187 us -> 142 us  [local(): lax.psum_scatter(jnp.dot(hidden, w_down, preferred_element_type=jnp.float...]
    all_to_all x4 -> x1, local copies, waits for them, and re-layouts: 40 us -> 0.19 us  [local(): lax.all_to_all(up_half, MP, 0, 0, tiled=True).reshape(n_mp * rows, piece)]
    all_to_all x2 -> x0, starting transfers between devices: 21.2 us -> none  [the longest x1 11.5 us: local(): lax.all_to_all(down_columns, 'mp', split_axis=0, concat_axis=1, tiled=True)]
    all_gather x2 -> x0, local copies, waits for them, and re-layouts: 13.9 us -> none  [the longest x1 6.98 us: local(): up_rows = lax.all_gather(up_half, 'rep', axis=1, tiled=True)]
  transfers between devices with their start and end apart: 6 -> 6, of which waited for: 4 -> 4; matrix products, arithmetic and copies ran while one was open for 8% -> 5% of each run, Pallas kernels for 0% -> 0%
where the time goes in v1:
time: 586 us; the launch traced here: 585 us
  waiting for transfers between devices  436 us (74%)
  blocking collectives  78.6 us (13%)
  matrix products  33.4 us (6%)
  local copies, waits for them, and re-layouts  16.9 us (3%)
  between operations  13.3 us (2%)
    reduce_scatter x1, waiting for transfers between devices, local(): lax.psum_scatter(jnp.dot(hidden, w_down, preferred_element_type=jnp.float...  142 us
    all_gather x1, waiting for transfers between devices, local(): x_all = lax.all_gather(xin, 'mc', axis=0, tiled=True)  131 us
    all_gather x1, waiting for transfers between devices, local(): down_mine = lax.all_gather(down_rows, 'rep', axis=0, tiled=True)  97.5 us
    all_gather x1, waiting for transfers between devices, local(): up_mine = lax.all_gather(up_cols, 'rep', axis=1, tiled=True)  65.6 us
    all_to_all x1, blocking collectives, local(): down_rows = lax.all_to_all(down_half, MP, 0, 0, tiled=True)  41 us
    all_to_all x1, blocking collectives, local(): lax.all_to_all(up_half, MP, 0, 0, tiled=True).reshape(n_mp * rows, piece)  37.6 us
    dot_general x1, matrix products, local(): jnp.dot(hidden, w_down, preferred_element_type=jnp.float32)  16.2 us
    dot_general x1, matrix products, local(): jnp.dot(x_all, w_up, preferred_element_type=jnp.float32)  15.4 us
  transfers between devices with their start and end apart: 6, of which 4 were waited for; matrix products, arithmetic and copies ran while one was open for 5% of the time, Pallas kernels for 0%

profile of v1, /device:TPU:1, one launch (start us, length us, event | category | flops | bytes accessed | tf_op | source)
XLA Modules:
  0.0 585.3 jit_solution(13966599562315707756)
XLA Ops:
  6.5 1.3 convert_element_type.31
  7.9 0.3 copy.13
  8.2 0.3 reshape.28
  8.5 37.6 %all_to_all.10 = bf16[32,160,54]{1,2,0:T(8,128)(2,1)S(1)} all-to-all(bf16[32,160,54]{1,2,0:T(8,128)(2,1)S(1)} %bitcast.65), channel_id=1, replica_groups=mesh['rep'=8,'mc'=16,'core'=2] {'mc','core'}, dimensions={0} | all-to-all | bytes 1105920 | tf_op jit(solution)/shard_map/all_to_all | solution.py:30
  46.1 0.2 copy.14
  46.3 2.3 reshape.29
  48.6 0.0 all-gather.8.cloned.1.call-update
  48.7 0.0 all-gather.10.cloned.1.call-start
  48.7 0.1 convert_element_type.33
  48.8 0.3 copy.15
  49.1 0.3 reshape.30
  49.4 41.0 %all_to_all.11 = bf16[32,54,160]{2,1,0:T(8,128)(2,1)S(1)} all-to-all(bf16[32,54,160]{2,1,0:T(8,128)(2,1)S(1)} %reshape.30), channel_id=1, replica_groups=mesh['rep'=8,'mc'=16,'core'=2] {'mc','core'}, dimensions={0} | all-to-all | bytes 1105920 | tf_op jit(solution)/shard_map/all_to_all | solution.py:37
  90.4 0.2 copy.16
  90.6 2.3 reshape.34
  92.9 0.0 all-gather.6.cloned.1.call-start
  93.0 0.2 convert_reduce_fusion
  93.2 0.3 fusion.21
  93.5 1.8 fusion.28
  95.3 1.9 copy-done
  97.3 1.2 fusion.27
  98.5 0.0 reduce-scatter.2.cloned.1.call-start
  98.5 65.6 %all-gather.8.cloned.1.call-done = bf16[8,54,5120]{2,1,0:T(8,128)(2,1)} async-done(((bf16[1,54,5120]{2,1,0:T(8,128)(2,1)}), bf16[8,54,5120]{2,1,0:T(8,128)(2,1)}) %all-gather.8.cloned.1.call-update) | async-done | bytes 4423696 | tf_op jit(solution)/shard_map/all_gather | solution.py:31
  164.2 4.3 reshape.33
  168.5 0.5 collective-permute-start
  169.0 97.5 %all-gather.10.cloned.1.call-done = bf16[8,54,5120]{2,1,0:T(8,128)(2,1)} async-done(((bf16[1,54,5120]{2,1,0:T(8,128)(2,1)}), bf16[8,54,5120]{2,1,0:T(8,128)(2,1)}) %all-gather.10.cloned.1.call-update) | async-done | bytes 4423696 | tf_op jit(solution)/shard_map/all_gather | solution.py:39
  266.5 4.4 reshape.35
  270.9 0.9 collective-permute-start.1
  271.8 131.1 %all-gather.6.cloned.1.call-done = bf16[1024,5120]{1,0:T(8,128)(2,1)} async-done(((bf16[64,5120]{1,0:T(8,128)(2,1)}), bf16[1024,5120]{1,0:T(8,128)(2,1)}) %all-gather.6.cloned.1.call-update) | async-done | bytes 10485776 | tf_op jit(solution)/shard_map/all_gather | solution.py:43
  402.9 15.4 %fusion.14 = bf16[1024,864]{0,1:T(8,128)(2,1)S(1)} fusion(bf16[1024,5120]{1,0:T(8,128)(2,1)} %all-gather.6.cloned.1.call-done, bf16[5120,432]{0,1:T(8,128)(2,1)} %collective-permute-done, bf16[5120,432]{0,1:T(8,128)(2,1)} %bitcast.64), kind=kOutput, calls=%fused_computation.16 | convolution fusion | flops 9085353984 | bytes 21102592 | tf_op jit(solution)/shard_map/dot_general | solution.py:45
  418.4 16.2 %convolution_convert_fusion = bf16[1024,5120]{1,0:T(8,128)(2,1)} fusion(bf16[1024,864]{0,1:T(8,128)(2,1)S(1)} %fusion.14, bf16[432,5120]{1,0:T(8,128)(2,1)} %collective-permute-done.1, bf16[432,5120]{1,0:T(8,128)(2,1)S(1)} %copy-done.2), kind=kOutput, calls=%fused_computation | convolution fusion | flops 9082634240 | bytes 21102592 | tf_op jit(solution)/shard_map/dot_general | solution.py:48
  434.6 141.7 %reduce-scatter.2.cloned.1.call-done = bf16[64,5120]{1,0:T(8,128)(2,1)} async-done(((bf16[1024,5120]{1,0:T(8,128)(2,1)}), bf16[64,5120]{1,0:T(8,128)(2,1)}) %reduce-scatter.2.cloned.1.call-update) | async-done | bytes 655376 | tf_op jit(solution)/shard_map/reduce_scatter | solution.py:47
  576.2 2.6 fusion.31
  (19 shorter events, 0.1 us)
Async XLA Ops:
  6.5 157.6 %all-gather.8.cloned.1.call-start = ((), (), s32[]{:S(2)}) async-start(), calls=%async_computation.5 | async-start | bytes 5160960 | tf_op jit(solution)/shard_map/all_gather | solution.py:31
  8.4 40.3 %copy-start.4 = (f32[1728,160]{0,1:T(8,128)S(1)}, f32[1728,160]{0,1:T(8,128)}, u32[]{:S(2)}) copy-start(f32[1728,160]{0,1:T(8,128)} %param.9) | copy-start | bytes 3317764
  48.7 217.8 %all-gather.10.cloned.1.call-start = ((), (), s32[]{:S(2)}) async-start(), calls=%async_computation.6 | async-start | bytes 5160960 | tf_op jit(solution)/shard_map/all_gather | solution.py:39
  49.1 43.8 %copy-start.1 = (bf16[1,64,5120]{2,1,0:T(8,128)(2,1)S(1)}, bf16[1,64,5120]{2,1,0:T(8,128)(2,1)}, u32[]{:S(2)}) copy-start(bf16[1,64,5120]{2,1,0:T(8,128)(2,1)} %param.5) | copy-start | bytes 1966084
  49.4 44.1 %copy-start.3 = (f32[1,12,3,5120]{3,0,2,1:T(1,128)S(1)}, f32[1,12,3,5120]{3,0,2,1:T(1,128)}, u32[]{:S(2)}) copy-start(f32[1,12,3,5120]{3,0,2,1:T(1,128)} %param.7) | copy-start | bytes 2211844
  49.4 44.1 %copy-start.5 = (s32[1,64]{1,0:T(1,128)S(1)}, s32[1,64]{1,0:T(1,128)}, u32[]{:S(2)}) copy-start(s32[1,64]{1,0:T(1,128)} %param.6) | copy-start | bytes 772
  92.9 310.0 %all-gather.6.cloned.1.call-start = ((), (), s32[]{:S(2)}) async-start(), calls=%async_computation.3 | async-start | bytes 11141120 | tf_op jit(solution)/shard_map/all_gather | solution.py:43
  95.3 1.9 copy-start
  98.5 477.7 %reduce-scatter.2.cloned.1.call-start = ((), (), s32[]{:S(2)}) async-start(), calls=%async_computation.4 | async-start | bytes 11141120 | tf_op jit(solution)/shard_map/reduce_scatter | solution.py:47
  168.5 103.3 %collective-permute-start = (bf16[5120,432]{0,1:T(8,128)(2,1)}, bf16[5120,432]{0,1:T(8,128)(2,1)}, u32[]{:S(2)}, u32[]{:S(2)}) collective-permute-start(bf16[5120,432]{0,1:T(8,128)(2,1)} %bitcast.63), channel_id=1, source_target_pairs={{0,1},{1,0},{2,3},{3,2},{4,5},{5,4},{6,7},{7,6},{8,9},{9,8},{10,11... | collective-permute-start | bytes 13271048 | tf_op jit(solution)/shard_map/ppermute | solution.py:32
  270.9 147.5 %collective-permute-start.1 = (bf16[432,5120]{1,0:T(8,128)(2,1)}, bf16[432,5120]{1,0:T(8,128)(2,1)}, u32[]{:S(2)}, u32[]{:S(2)}) collective-permute-start(bf16[432,5120]{1,0:T(8,128)(2,1)} %reshape.35), channel_id=1, source_target_pairs={{0,1},{1,0},{2,3},{3,2},{4,5},{5,4},{6,7},{7,6},{8,9},{9,8},{10,11... | collective-permute-start | bytes 13271048 | tf_op jit(solution)/shard_map/ppermute | solution.py:40
  402.9 15.5 %copy-start.2 = (bf16[432,5120]{1,0:T(8,128)(2,1)S(1)}, bf16[432,5120]{1,0:T(8,128)(2,1)}, u32[]{:S(2)}) copy-start(bf16[432,5120]{1,0:T(8,128)(2,1)} %reshape.35) | copy-start | bytes 13271044
Sparse Core Ops, SparseCore 0:
  48.8 115.3 all-gather.7
  166.0 100.4 all-gather.9
  268.9 133.9 all-gather.5
  434.7 141.4 reduce-scatter.1

commit v2 on v1

v2 whole, which is shorter than its diff:
```python
import functools

import jax
import jax.numpy as jnp
from jax import lax
from jax.experimental import pallas as pl
from jax.experimental.pallas import tpu as pltpu
from jax.sharding import Mesh, PartitionSpec as P

MP = ("mc", "core")
MESH_ID = pl.DeviceIdType.MESH


def handover_kernel(up_ref, dn_ref, up_out, dn_out, send_sem, recv_sem, fwd_send, fwd_recv, local_sem):
    n_rep = up_out.shape[1]
    me = lax.axis_index("rep")
    mc = lax.axis_index("mc")
    c = lax.axis_index("core")
    other = 1 - c

    barrier = pltpu.get_barrier_semaphore()
    for k in range(1, n_rep):
        pl.semaphore_signal(barrier, 1, device_id=(lax.rem(me + k, n_rep), mc, c), device_id_type=MESH_ID)
    pl.semaphore_signal(barrier, 1, device_id=(me, mc, other), device_id_type=MESH_ID)
    pl.semaphore_wait(barrier, n_rep)

    pairs = ((up_ref, up_out), (dn_ref, dn_out))
    locals_ = []
    sends = []
    for i, (src, dst) in enumerate(pairs):
        cp = pltpu.make_async_copy(src, dst.at[c, me], local_sem.at[i])
        cp.start()
        locals_.append(cp)
        for k in range(1, n_rep):
            cp = pltpu.make_async_remote_copy(
                src_ref=src,
                dst_ref=dst.at[c, me],
                send_sem=send_sem.at[i, k],
                recv_sem=recv_sem.at[i, k],
                device_id=(lax.rem(me + k, n_rep), mc, c),
                device_id_type=MESH_ID,
            )
            cp.start()
            sends.append(cp)

    forwards = []
    for i, (src, dst) in enumerate(pairs):
        for k in range(n_rep):
            slot = lax.rem(me + n_rep - k, n_rep)
            if k == 0:
                locals_[i].wait()
            else:
                pltpu.make_async_remote_copy(
                    src_ref=src,
                    dst_ref=dst.at[c, slot],
                    send_sem=send_sem.at[i, k],
                    recv_sem=recv_sem.at[i, k],
                    device_id=(slot, mc, c),
                    device_id_type=MESH_ID,
                ).wait_recv()
            fw = pltpu.make_async_remote_copy(
                src_ref=dst.at[c, slot],
                dst_ref=dst.at[c, slot],
                send_sem=fwd_send.at[i, k],
                recv_sem=fwd_recv.at[i, k],
                device_id=(me, mc, other),
                device_id_type=MESH_ID,
            )
            fw.start()
            forwards.append(fw)

    for cp in sends:
        cp.wait_send()
    for i, (src, dst) in enumerate(pairs):
        for k in range(n_rep):
            slot = lax.rem(me + n_rep - k, n_rep)
            pltpu.make_async_remote_copy(
                src_ref=dst.at[other, slot],
                dst_ref=dst.at[other, slot],
                send_sem=fwd_send.at[i, k],
                recv_sem=fwd_recv.at[i, k],
                device_id=(me, mc, other),
                device_id_type=MESH_ID,
            ).wait_recv()
    for fw in forwards:
        fw.wait_send()


def handover(up_blk, dn_blk, n_rep):
    units, width = up_blk.shape
    shape = jax.ShapeDtypeStruct((2, n_rep, units, width), up_blk.dtype)
    return pl.pallas_call(
        handover_kernel,
        out_shape=(shape, shape),
        in_specs=[pl.BlockSpec(memory_space=pl.ANY)] * 2,
        out_specs=(pl.BlockSpec(memory_space=pl.ANY),) * 2,
        scratch_shapes=[
            pltpu.SemaphoreType.DMA((2, n_rep)),
            pltpu.SemaphoreType.DMA((2, n_rep)),
            pltpu.SemaphoreType.DMA((2, n_rep)),
            pltpu.SemaphoreType.DMA((2, n_rep)),
            pltpu.SemaphoreType.DMA((2,)),
        ],
        compiler_params=pltpu.CompilerParams(collective_id=0, has_side_effects=True),
    )(up_blk, dn_blk)


def local(tokens, prompt_ids, modulation, trainer_up, trainer_down):
    as_float = tokens[0].astype(jnp.float32)
    average = jnp.mean(as_float, axis=-1, keepdims=True)
    centred = as_float - average
    variance = jnp.mean(centred * centred, axis=-1, keepdims=True)
    normed = centred / jnp.sqrt(variance + 1e-06)
    prompts_here = modulation.shape[1]
    onehot = (prompt_ids[0][:, None] == jnp.arange(prompts_here, dtype=jnp.int32)[None, :]).astype(
        jnp.float32
    )
    chosen = jnp.einsum("tp,pkd->tkd", onehot, modulation[0], precision=lax.Precision.HIGHEST)
    shift = chosen[:, 0]
    scale = chosen[:, 1]
    gate = chosen[:, 2]
    xin = (normed * (1.0 + scale) + shift).astype(jnp.bfloat16)
    x_all = lax.all_gather(xin, "mc", axis=0, tiled=True)

    n_mp = lax.psum(1, MP)
    n_rep = lax.psum(1, "rep")
    rows, cols = trainer_up.shape
    piece = cols // n_mp
    both = jnp.stack([trainer_up.astype(jnp.bfloat16).T, trainer_down.astype(jnp.bfloat16)])
    both = lax.all_to_all(both.reshape(2, n_mp, piece, rows), MP, 1, 1, tiled=True)
    both = both.transpose(0, 2, 1, 3).reshape(2, piece, n_mp * rows)
    up_all, dn_all = handover(both[0], both[1], n_rep)
    units = 2 * n_rep * piece
    w_up_t = up_all.reshape(units, n_mp * rows)
    w_down = dn_all.reshape(units, n_mp * rows)

    hidden = jax.nn.gelu(
        lax.dot_general(x_all, w_up_t, (((1,), (1,)), ((), ())), preferred_element_type=jnp.float32),
        approximate=True,
    ).astype(jnp.bfloat16)
    mlp = lax.psum_scatter(
        jnp.dot(hidden, w_down, preferred_element_type=jnp.float32).astype(jnp.bfloat16),
        "mc",
        scatter_dimension=0,
        tiled=True,
    ).astype(jnp.float32)
    result = as_float + gate * mlp
    return result.astype(jnp.bfloat16)[None]


def solution(mesh):
    n_rep, n_mp = mesh.devices.shape
    chips = Mesh(mesh.devices.reshape(n_rep, n_mp // 2, 2), ("rep", "mc", "core"))
    in_specs = (
        P("rep", MP, None),
        P("rep", MP),
        P("rep", None, None, None),
        P(MP, "rep"),
        P("rep", MP),
    )
    out_specs = P("rep", MP, None)
    return jax.shard_map(local, mesh=chips, in_specs=in_specs, out_specs=out_specs, check_vma=False)
```

time: 586 us -> 484 us (0.83)
  waiting for transfers between devices: 436 us -> 135 us
  Pallas kernels: 0 us -> 189 us
  local copies, waits for them, and re-layouts: 16.9 us -> 28.8 us
    pallas_call x0 -> x1, Pallas kernels: none -> 189 us  [handover(): pl.pallas_call(handover_kernel, out_shape=(shape, shape), in_specs=[pl.Bl...]
    all_gather x2 -> x0, waiting for transfers between devices: 163 us -> none  [the longest x1 97.5 us: local(): down_mine = lax.all_gather(down_rows, 'rep', axis=0, tiled=True)]
    all_gather x1, waiting for transfers between devices: 131 us -> 0.01 us  [local(): x_all = lax.all_gather(xin, 'mc', axis=0, tiled=True)]
    reshape x3 -> x2, local copies, waits for them, and re-layouts: 2.9 us -> 16.6 us  [the longest x1 8.3 us: local(): w_down = dn_all.reshape(units, n_mp * rows)]
    unnamed x15 -> x8, local copies, waits for them, and re-layouts: 13 us -> 1.84 us
    reduce_scatter x1, waiting for transfers between devices: 142 us -> 135 us  [local(): lax.psum_scatter(jnp.dot(hidden, w_down, preferred_element_type=jnp.float...]
    all_to_all x2 -> x1, blocking collectives: 78.6 us -> 77.4 us  [local(): lax.all_to_all(both.reshape(2, n_mp, piece, rows), MP, 1, 1, tiled=True)]
  transfers between devices with their start and end apart: 6 -> 2, of which waited for: 4 -> 1; matrix products, arithmetic and copies ran while one was open for 5% -> 6% of each run, Pallas kernels for 0% -> 39%
where the time goes in v2:
time: 484 us; the launch traced here: 483 us
  Pallas kernels  189 us (39%)
  waiting for transfers between devices  135 us (28%)
  blocking collectives  77.4 us (16%)
  matrix products  30.9 us (6%)
  local copies, waits for them, and re-layouts  28.8 us (6%)
  between operations  13.5 us (3%)
  other arithmetic  8.3 us (2%)
    pallas_call x1, Pallas kernels, handover(): pl.pallas_call(handover_kernel, out_shape=(shape, shape), in_specs=[pl.Bl...  189 us
    reduce_scatter x1, waiting for transfers between devices, local(): lax.psum_scatter(jnp.dot(hidden, w_down, preferred_element_type=jnp.float...  135 us
    all_to_all x1, blocking collectives, local(): lax.all_to_all(both.reshape(2, n_mp, piece, rows), MP, 1, 1, tiled=True)  77.4 us
    dot_general x1, matrix products, local(): jnp.dot(hidden, w_down, preferred_element_type=jnp.float32)  14.3 us
    dot_general x1, matrix products, local(): lax.dot_general(x_all, w_up_t, (((1,), (1,)), ((), ())), preferred_elemen...  13.6 us
  transfers between devices with their start and end apart: 2, of which 1 were waited for; matrix products, arithmetic and copies ran while one was open for 6% of the time, Pallas kernels for 39%

profile of v2, /device:TPU:1, one launch (start us, length us, event | category | flops | bytes accessed | tf_op | source)
XLA Modules:
  0.0 483.2 jit_solution(2162698433530012572)
XLA Ops:
  6.5 0.0 all-gather.2.cloned.1.call-start
  6.5 1.3 convert_reduce_fusion
  7.9 1.4 fusion.17
  9.3 0.0 copy-start.3
  9.4 3.0 fusion.24
  12.3 0.0 copy-start
  12.4 1.8 copy-done
  14.2 1.2 fusion.23
  15.4 0.0 all-gather.2.cloned.1.call-update
  15.4 0.0 reduce-scatter.2.cloned.1.call-start
  15.5 0.1 convert_element_type.32
  15.6 0.3 copy.16
  15.9 0.3 stack.10
  16.1 1.3 convert_bitcast_fusion.1
  17.5 0.3 copy.15
  17.8 0.3 stack.9
  18.1 0.4 pad_maximum_fusion
  18.4 1.8 copy.17
  20.3 77.4 %all_to_all.5 = bf16[2,32,54,160]{3,0,2,1:T(2,128)(2,1)S(1)} all-to-all(bf16[2,32,54,160]{3,0,2,1:T(2,128)(2,1)S(1)} %copy.17), channel_id=1, replica_groups=mesh['rep'=8,'mc'=16,'core'=2] {'mc','core'}, dimensions={1} | all-to-all | bytes 2211840 | tf_op jit(solution)/shard_map/all_to_all | solution.py:130
  97.7 2.4 fusion.35
  100.1 0.2 copy.18
  100.3 2.3 squeeze.20.up_ref
  102.6 0.2 copy.19
  102.8 2.3 squeeze.21.dn_ref
  105.1 189.0 %shard_map.55 = (bf16[2,8,54,5120]{3,2,1,0:T(8,128)(2,1)}, bf16[2,8,54,5120]{3,2,1,0:T(8,128)(2,1)}) custom-call(bf16[54,5120]{1,0:T(8,128)(2,1)} %squeeze.20.up_ref, bf16[54,5120]{1,0:T(8,128)(2,1)} %squeeze.21.dn_ref), custom_call_target="tpu_custom_call" | custom-call | tf_op jit(solution)/shard_map/pallas_call | solution.py:92
  294.1 8.3 %reshape.32 = bf16[864,5120]{1,0:T(8,128)(2,1)} reshape(bf16[2,8,54,5120]{3,2,1,0:T(8,128)(2,1)} %get-tuple-element.7) | data formatting | bytes 17694720 | tf_op jit(solution)/shard_map/reshape | solution.py:134
  302.4 8.3 %reshape.33 = bf16[864,5120]{1,0:T(8,128)(2,1)} reshape(bf16[2,8,54,5120]{3,2,1,0:T(8,128)(2,1)} %get-tuple-element.8) | data formatting | bytes 17694720 | tf_op jit(solution)/shard_map/reshape | solution.py:135
  310.7 13.6 %fusion.36 = f32[1024,864]{0,1:T(8,128)S(1)} fusion(bf16[1024,5120]{1,0:T(8,128)(2,1)} %all-gather.2.cloned.1.call-done, bf16[864,5120]{1,0:T(8,128)(2,1)} %reshape.32), kind=kOutput, calls=%fused_computation.46 | convolution fusion | flops 9059696640 | bytes 22872064 | tf_op jit(solution)/shard_map/dot_general | solution.py:138
  324.3 14.3 %convolution_convert_fusion = bf16[1024,5120]{1,0:T(8,128)(2,1)} fusion(bf16[864,5120]{1,0:T(8,128)(2,1)S(1)} %copy-done.2, f32[1024,864]{0,1:T(8,128)S(1)} %fusion.36), kind=kOutput, calls=%fused_computation | convolution fusion | flops 9072902144 | bytes 22872064 | tf_op jit(solution)/shard_map/dot_general | solution.py:142
  338.6 0.0 reduce-scatter.2.cloned.1.call-update
  338.6 135.2 %reduce-scatter.2.cloned.1.call-done = bf16[64,5120]{1,0:T(8,128)(2,1)} async-done(((bf16[1024,5120]{1,0:T(8,128)(2,1)}), bf16[64,5120]{1,0:T(8,128)(2,1)}) %reduce-scatter.2.cloned.1.call-update) | async-done | bytes 655376 | tf_op jit(solution)/shard_map/reduce_scatter | solution.py:141
  473.8 2.6 fusion.27
  (8 shorter events, 0.0 us)
Async XLA Ops:
  6.5 7.6 %copy-start.1 = (bf16[1,64,5120]{2,1,0:T(8,128)(2,1)S(1)}, bf16[1,64,5120]{2,1,0:T(8,128)(2,1)}, u32[]{:S(2)}) copy-start(bf16[1,64,5120]{2,1,0:T(8,128)(2,1)} %param.5) | copy-start | bytes 1966084
  6.5 304.2 %all-gather.2.cloned.1.call-start = ((), (), s32[]{:S(2)}) async-start(), calls=%async_computation.2 | async-start | bytes 11141120 | tf_op jit(solution)/shard_map/all_gather | solution.py:123
  9.3 6.1 %copy-start.3 = (f32[1728,160]{0,1:T(8,128)S(1)}, f32[1728,160]{0,1:T(8,128)}, u32[]{:S(2)}) copy-start(f32[1728,160]{0,1:T(8,128)} %param.9) | copy-start | bytes 3317764
  12.3 1.8 copy-start
  15.4 458.4 %reduce-scatter.2.cloned.1.call-start = ((), (), s32[]{:S(2)}) async-start(), calls=%async_computation.3 | async-start | bytes 11141120 | tf_op jit(solution)/shard_map/reduce_scatter | solution.py:141
  310.7 13.6 %copy-start.2 = (bf16[864,5120]{1,0:T(8,128)(2,1)S(1)}, bf16[864,5120]{1,0:T(8,128)(2,1)}, u32[]{:S(2)}) copy-start(bf16[864,5120]{1,0:T(8,128)(2,1)} %reshape.33) | copy-start | bytes 26542084
Sparse Core Ops, SparseCore 0:
  15.5 220.6 all-gather.1
  338.7 134.9 reduce-scatter.1

commit v3 on v2

--- a/solution.py
+++ b/solution.py
@@ -11,58 +11,139 @@
 MESH_ID = pl.DeviceIdType.MESH
 
 
+def exchange_kernel(src, dst, send_sem, recv_sem, local_sem):
+    n = src.shape[0]
+    me = lax.axis_index("mc") * 2 + lax.axis_index("core")
+    r = lax.axis_index("rep")
+
+    def dev(i):
+        return (r, lax.div(i, 2), lax.rem(i, 2))
+
+    barrier = pltpu.get_barrier_semaphore()
+    for k in range(1, n):
+        pl.semaphore_signal(barrier, 1, device_id=dev(lax.rem(me + k, n)), device_id_type=MESH_ID)
+    pl.semaphore_wait(barrier, n - 1)
+    own = pltpu.make_async_copy(src.at[me], dst.at[me], local_sem.at[0])
+    own.start()
+    sends = []
+    for k in range(1, n):
+        t = lax.rem(me + k, n)
+        cp = pltpu.make_async_remote_copy(
+            src_ref=src.at[t],
+            dst_ref=dst.at[me],
+            send_sem=send_sem.at[k],
+            recv_sem=recv_sem.at[k],
+            device_id=dev(t),
+            device_id_type=MESH_ID,
+        )
+        cp.start()
+        sends.append(cp)
+    for k in range(1, n):
+        s = lax.rem(me + n - k, n)
+        pltpu.make_async_remote_copy(
+            src_ref=src.at[s],
+            dst_ref=dst.at[s],
+            send_sem=send_sem.at[k],
+            recv_sem=recv_sem.at[k],
+            device_id=dev(s),
+            device_id_type=MESH_ID,
+        ).wait_recv()
+    for cp in sends:
+        cp.wait_send()
+    own.wait()
+
+
+def exchange(pieces):
+    n = pieces.shape[0]
+    return pl.pallas_call(
+        exchange_kernel,
+        out_shape=jax.ShapeDtypeStruct(pieces.shape, pieces.dtype),
+        in_specs=[pl.BlockSpec(memory_space=pl.ANY)],
+        out_specs=pl.BlockSpec(memory_space=pl.ANY),
+        scratch_shapes=[
+            pltpu.SemaphoreType.DMA((n,)),
+            pltpu.SemaphoreType.DMA((n,)),
+            pltpu.SemaphoreType.DMA((1,)),
+        ],
+        compiler_params=pltpu.CompilerParams(collective_id=1, has_side_effects=True),
+    )(pieces)
+
+
 def handover_kernel(up_ref, dn_ref, up_out, dn_out, send_sem, recv_sem, fwd_send, fwd_recv, local_sem):
     n_rep = up_out.shape[1]
+    n_x = n_rep // 2
     me = lax.axis_index("rep")
     mc = lax.axis_index("mc")
     c = lax.axis_index("core")
     other = 1 - c
+    x = lax.div(me, 2)
+    zl = lax.rem(me, 2)
+    partner = me + 1 - 2 * zl
+    xs = [lax.rem(x + d, n_x) * 2 for d in range(1, n_x)]
 
     barrier = pltpu.get_barrier_semaphore()
-    for k in range(1, n_rep):
-        pl.semaphore_signal(barrier, 1, device_id=(lax.rem(me + k, n_rep), mc, c), device_id_type=MESH_ID)
+    for t in [partner] + [xo + zl for xo in xs]:
+        pl.semaphore_signal(barrier, 1, device_id=(t, mc, c), device_id_type=MESH_ID)
     pl.semaphore_signal(barrier, 1, device_id=(me, mc, other), device_id_type=MESH_ID)
-    pl.semaphore_wait(barrier, n_rep)
+    pl.semaphore_wait(barrier, n_x + 1)
 
     pairs = ((up_ref, up_out), (dn_ref, dn_out))
+
+    def recv_desc(i, slot):
+        dst = pairs[i][1]
+        return pltpu.make_async_remote_copy(
+            src_ref=dst.at[c, slot],
+            dst_ref=dst.at[c, slot],
+            send_sem=send_sem.at[i, 0],
+            recv_sem=recv_sem.at[i, slot],
+            device_id=(slot, mc, c),
+            device_id_type=MESH_ID,
+        )
+
     locals_ = []
     sends = []
     for i, (src, dst) in enumerate(pairs):
         cp = pltpu.make_async_copy(src, dst.at[c, me], local_sem.at[i])
         cp.start()
         locals_.append(cp)
-        for k in range(1, n_rep):
+        for j, t in enumerate([partner] + [xo + zl for xo in xs]):
             cp = pltpu.make_async_remote_copy(
                 src_ref=src,
                 dst_ref=dst.at[c, me],
-                send_sem=send_sem.at[i, k],
-                recv_sem=recv_sem.at[i, k],
-                device_id=(lax.rem(me + k, n_rep), mc, c),
+                send_sem=send_sem.at[i, j],
+                recv_sem=recv_sem.at[i, me],
+                device_id=(t, mc, c),
                 device_id_type=MESH_ID,
             )
             cp.start()
             sends.append(cp)
+    for i, (src, dst) in enumerate(pairs):
+        recv_desc(i, partner).wait_recv()
+        for j, xo in enumerate(xs):
+            cp = pltpu.make_async_remote_copy(
+                src_ref=dst.at[c, partner],
+                dst_ref=dst.at[c, partner],
+                send_sem=send_sem.at[i, n_x + j],
+                recv_sem=recv_sem.at[i, partner],
+                device_id=(xo + zl, mc, c),
+                device_id_type=MESH_ID,
+            )
+            cp.start()
+            sends.append(cp)
 
     forwards = []
     for i, (src, dst) in enumerate(pairs):
-        for k in range(n_rep):
-            slot = lax.rem(me + n_rep - k, n_rep)
-            if k == 0:
+        order = [me, partner] + [xo + zl for xo in xs] + [xo + 1 - zl for xo in xs]
+        for slot in order:
+            if slot is me:
                 locals_[i].wait()
-            else:
-                pltpu.make_async_remote_copy(
-                    src_ref=src,
-                    dst_ref=dst.at[c, slot],
-                    send_sem=send_sem.at[i, k],
-                    recv_sem=recv_sem.at[i, k],
-                    device_id=(slot, mc, c),
-                    device_id_type=MESH_ID,
-                ).wait_recv()
+            elif slot is not partner:
+                recv_desc(i, slot).wait_recv()
             fw = pltpu.make_async_remote_copy(
                 src_ref=dst.at[c, slot],
                 dst_ref=dst.at[c, slot],
-                send_sem=fwd_send.at[i, k],
-                recv_sem=fwd_recv.at[i, k],
+                send_sem=fwd_send.at[i, slot],
+                recv_sem=fwd_recv.at[i, slot],
                 device_id=(me, mc, other),
                 device_id_type=MESH_ID,
             )
@@ -72,13 +153,12 @@
     for cp in sends:
         cp.wait_send()
     for i, (src, dst) in enumerate(pairs):
-        for k in range(n_rep):
-            slot = lax.rem(me + n_rep - k, n_rep)
+        for slot in range(n_rep):
             pltpu.make_async_remote_copy(
                 src_ref=dst.at[other, slot],
                 dst_ref=dst.at[other, slot],
-                send_sem=fwd_send.at[i, k],
-                recv_sem=fwd_recv.at[i, k],
+                send_sem=fwd_send.at[i, slot],
+                recv_sem=fwd_recv.at[i, slot],
                 device_id=(me, mc, other),
                 device_id_type=MESH_ID,
             ).wait_recv()
@@ -127,8 +207,8 @@
     rows, cols = trainer_up.shape
     piece = cols // n_mp
     both = jnp.stack([trainer_up.astype(jnp.bfloat16).T, trainer_down.astype(jnp.bfloat16)])
-    both = lax.all_to_all(both.reshape(2, n_mp, piece, rows), MP, 1, 1, tiled=True)
-    both = both.transpose(0, 2, 1, 3).reshape(2, piece, n_mp * rows)
+    both = exchange(both.reshape(2, n_mp, piece, rows).transpose(1, 0, 2, 3))
+    both = both.transpose(1, 2, 0, 3).reshape(2, piece, n_mp * rows)
     up_all, dn_all = handover(both[0], both[1], n_rep)
     units = 2 * n_rep * piece
     w_up_t = up_all.reshape(units, n_mp * rows)

time: 484 us -> 426 us (0.88)
  blocking collectives: 77.4 us -> 0 us
  waiting for transfers between devices: 135 us -> 148 us
  local copies, waits for them, and re-layouts: 28.8 us -> 36.5 us
    all_to_all x1 -> x0, blocking collectives: 77.4 us -> none  [local(): lax.all_to_all(both.reshape(2, n_mp, piece, rows), MP, 1, 1, tiled=True)]
    pallas_call x1, Pallas kernels: 189 us -> 119 us  [handover(): pl.pallas_call(handover_kernel, out_shape=(shape, shape), in_specs=[pl.Bl...]
    pallas_call x0 -> x1, Pallas kernels: none -> 67 us  [exchange(): pl.pallas_call(exchange_kernel, out_shape=jax.ShapeDtypeStruct(pieces.sha...]
    reduce_scatter x1, waiting for transfers between devices: 135 us -> 148 us  [local(): lax.psum_scatter(jnp.dot(hidden, w_down, preferred_element_type=jnp.float...]
    another operation x3 -> x4, local copies, waits for them, and re-layouts: 2.38 us -> 11.5 us  [local(): jnp.stack([trainer_up.astype(jnp.bfloat16).T, trainer_down.astype(jnp.bfl...]
  transfers between devices with their start and end apart: 2 -> 2, of which waited for: 1 -> 1; matrix products, arithmetic and copies ran while one was open for 6% -> 9% of each run, Pallas kernels for 39% -> 44%
where the time goes in v3:
time: 426 us
  Pallas kernels  186 us (44%)
  waiting for transfers between devices  148 us (35%)
  local copies, waits for them, and re-layouts  36.5 us (9%)
  matrix products  30.9 us (7%)
  between operations  13.5 us (3%)
  other arithmetic  10.6 us (2%)
    reduce_scatter x1, waiting for transfers between devices, local(): lax.psum_scatter(jnp.dot(hidden, w_down, preferred_element_type=jnp.float...  148 us
    pallas_call x1, Pallas kernels, handover(): pl.pallas_call(handover_kernel, out_shape=(shape, shape), in_specs=[pl.Bl...  119 us
    pallas_call x1, Pallas kernels, exchange(): pl.pallas_call(exchange_kernel, out_shape=jax.ShapeDtypeStruct(pieces.sha...  67 us
    dot_general x1, matrix products, local(): jnp.dot(hidden, w_down, preferred_element_type=jnp.float32)  14.1 us
    dot_general x1, matrix products, local(): lax.dot_general(x_all, w_up_t, (((1,), (1,)), ((), ())), preferred_elemen...  13.8 us
    another operation x4, local copies, waits for them, and re-layouts, local(): jnp.stack([trainer_up.astype(jnp.bfloat16).T, trainer_down.astype(jnp.bfl...  11.5 us
  transfers between devices with their start and end apart: 2, of which 1 were waited for; matrix products, arithmetic and copies ran while one was open for 9% of the time, Pallas kernels for 44%

profile of v3, /device:TPU:1, one launch (start us, length us, event | category | flops | bytes accessed | tf_op | source)
XLA Modules:
  0.0 425.5 jit_solution(13785679237304374032)
XLA Ops:
  6.5 0.0 all-gather.2.cloned.1.call-start
  6.5 1.3 convert_reduce_fusion
  7.9 1.4 fusion.17
  9.3 0.0 copy-start.3
  9.4 3.0 fusion.24
  12.3 0.0 copy-start
  12.4 1.8 copy-done
  14.2 0.0 copy-done.1
  14.2 1.2 fusion.23
  15.4 0.0 all-gather.2.cloned.1.call-update
  15.4 0.0 reduce-scatter.2.cloned.1.call-start
  15.5 0.1 convert_bitcast_fusion.1
  15.6 4.0 reshape.35
  19.5 1.4 copy.14
  21.0 1.3 convert_element_type.32
  22.3 4.0 reshape.36
  26.3 2.1 copy.15
  28.4 2.7 maximum_bitcast_fusion.src
  31.1 67.0 %shard_map.55 = bf16[32,2,54,160]{3,2,1,0:T(8,128)(2,1)} custom-call(bf16[32,2,54,160]{3,2,1,0:T(8,128)(2,1)} %maximum_bitcast_fusion.src), custom_call_target="tpu_custom_call" | custom-call | tf_op jit(solution)/shard_map/pallas_call | solution.py:58
  98.1 1.6 fusion.35
  99.7 0.2 copy.16
  99.9 2.3 squeeze.20.up_ref
  102.2 0.2 copy.17
  102.4 2.3 squeeze.21.dn_ref
  104.7 118.8 %shard_map.56 = (bf16[2,8,54,5120]{3,2,1,0:T(8,128)(2,1)}, bf16[2,8,54,5120]{3,2,1,0:T(8,128)(2,1)}) custom-call(bf16[54,5120]{1,0:T(8,128)(2,1)} %squeeze.20.up_ref, bf16[54,5120]{1,0:T(8,128)(2,1)} %squeeze.21.dn_ref), custom_call_target="tpu_custom_call" | custom-call | tf_op jit(solution)/shard_map/pallas_call | solution.py:172
  223.5 8.3 %reshape.32 = bf16[864,5120]{1,0:T(8,128)(2,1)} reshape(bf16[2,8,54,5120]{3,2,1,0:T(8,128)(2,1)} %get-tuple-element.7) | data formatting | bytes 17694720 | tf_op jit(solution)/shard_map/reshape | solution.py:214
  231.8 8.3 %reshape.33 = bf16[864,5120]{1,0:T(8,128)(2,1)} reshape(bf16[2,8,54,5120]{3,2,1,0:T(8,128)(2,1)} %get-tuple-element.8) | data formatting | bytes 17694720 | tf_op jit(solution)/shard_map/reshape | solution.py:215
  240.1 13.8 %fusion.36 = f32[1024,864]{0,1:T(8,128)S(1)} fusion(bf16[1024,5120]{1,0:T(8,128)(2,1)} %all-gather.2.cloned.1.call-done, bf16[864,5120]{1,0:T(8,128)(2,1)} %reshape.32), kind=kOutput, calls=%fused_computation.46 | convolution fusion | flops 9059696640 | bytes 22872064 | tf_op jit(solution)/shard_map/dot_general | solution.py:218
  253.9 14.1 %convolution_convert_fusion = bf16[1024,5120]{1,0:T(8,128)(2,1)} fusion(bf16[864,5120]{1,0:T(8,128)(2,1)S(1)} %copy-done.2, f32[1024,864]{0,1:T(8,128)S(1)} %fusion.36), kind=kOutput, calls=%fused_computation | convolution fusion | flops 9072902144 | bytes 22872064 | tf_op jit(solution)/shard_map/dot_general | solution.py:222
  268.0 0.0 reduce-scatter.2.cloned.1.call-update
  268.0 148.1 %reduce-scatter.2.cloned.1.call-done = bf16[64,5120]{1,0:T(8,128)(2,1)} async-done(((bf16[1024,5120]{1,0:T(8,128)(2,1)}), bf16[64,5120]{1,0:T(8,128)(2,1)}) %reduce-scatter.2.cloned.1.call-update) | async-done | bytes 655376 | tf_op jit(solution)/shard_map/reduce_scatter | solution.py:221
  416.1 2.6 fusion.27
  (7 shorter events, 0.0 us)
Async XLA Ops:
  6.5 7.6 %copy-start.1 = (bf16[1,64,5120]{2,1,0:T(8,128)(2,1)S(1)}, bf16[1,64,5120]{2,1,0:T(8,128)(2,1)}, u32[]{:S(2)}) copy-start(bf16[1,64,5120]{2,1,0:T(8,128)(2,1)} %param.5) | copy-start | bytes 1966084
  6.5 233.6 %all-gather.2.cloned.1.call-start = ((), (), s32[]{:S(2)}) async-start(), calls=%async_computation.1 | async-start | bytes 11141120 | tf_op jit(solution)/shard_map/all_gather | solution.py:203
  9.3 6.1 %copy-start.3 = (f32[160,1728]{1,0:T(8,128)S(1)}, f32[160,1728]{1,0:T(8,128)}, u32[]{:S(2)}) copy-start(f32[160,1728]{1,0:T(8,128)} %param.8) | copy-start | bytes 3317764
  12.3 1.8 copy-start
  15.4 400.7 %reduce-scatter.2.cloned.1.call-start = ((), (), s32[]{:S(2)}) async-start(), calls=%async_computation.2 | async-start | bytes 11141120 | tf_op jit(solution)/shard_map/reduce_scatter | solution.py:221
  240.1 13.8 %copy-start.2 = (bf16[864,5120]{1,0:T(8,128)(2,1)S(1)}, bf16[864,5120]{1,0:T(8,128)(2,1)}, u32[]{:S(2)}) copy-start(bf16[864,5120]{1,0:T(8,128)(2,1)} %reshape.33) | copy-start | bytes 26542084
Sparse Core Ops, SparseCore 0:
  15.5 202.8 all-gather.1
  268.2 147.9 reduce-scatter.1

commit v4 on v3

--- a/solution.py
+++ b/solution.py
@@ -200,17 +200,20 @@
     scale = chosen[:, 1]
     gate = chosen[:, 2]
     xin = (normed * (1.0 + scale) + shift).astype(jnp.bfloat16)
-    x_all = lax.all_gather(xin, "mc", axis=0, tiled=True)
 
     n_mp = lax.psum(1, MP)
     n_rep = lax.psum(1, "rep")
     rows, cols = trainer_up.shape
     piece = cols // n_mp
     both = jnp.stack([trainer_up.astype(jnp.bfloat16).T, trainer_down.astype(jnp.bfloat16)])
-    both = exchange(both.reshape(2, n_mp, piece, rows).transpose(1, 0, 2, 3))
-    both = both.transpose(1, 2, 0, 3).reshape(2, piece, n_mp * rows)
+    padded = -(-piece // 16) * 16
+    both = jnp.pad(both.reshape(2, n_mp, piece, rows), ((0, 0), (0, 0), (0, padded - piece), (0, 0)))
+    both = exchange(both.transpose(1, 0, 2, 3))
+    xin, both = lax.optimization_barrier((xin, both))
+    x_all = lax.all_gather(xin, "mc", axis=0, tiled=True)
+    both = both.transpose(1, 2, 0, 3).reshape(2, padded, n_mp * rows)
     up_all, dn_all = handover(both[0], both[1], n_rep)
-    units = 2 * n_rep * piece
+    units = 2 * n_rep * padded
     w_up_t = up_all.reshape(units, n_mp * rows)
     w_down = dn_all.reshape(units, n_mp * rows)
 

time: 426 us -> 421 us (0.988)
  local copies, waits for them, and re-layouts: 36.5 us -> 19.7 us
  waiting for transfers between devices: 148 us -> 160 us
  Pallas kernels: 186 us -> 178 us
  matrix products: 30.9 us -> 37.8 us
    all_gather x1, waiting for transfers between devices: 0.01 us -> 18.5 us  [local(): x_all = lax.all_gather(xin, 'mc', axis=0, tiled=True)]
    pallas_call x1, Pallas kernels: 67 us -> 49.2 us  [exchange(): pl.pallas_call(exchange_kernel, out_shape=jax.ShapeDtypeStruct(pieces.sha...]
    reshape x2 -> x0, local copies, waits for them, and re-layouts: 16.6 us -> none  [the longest x1 8.3 us: local(): w_down = dn_all.reshape(units, n_mp * rows)]
    pallas_call x1, Pallas kernels: 119 us -> 129 us  [handover(): pl.pallas_call(handover_kernel, out_shape=(shape, shape), in_specs=[pl.Bl...]
    reduce_scatter x1, waiting for transfers between devices: 148 us -> 141 us  [local(): lax.psum_scatter(jnp.dot(hidden, w_down, preferred_element_type=jnp.float...]
    dot_general x1, matrix products: 14.1 us -> 18.6 us  [local(): jnp.dot(hidden, w_down, preferred_element_type=jnp.float32)]
  transfers between devices with their start and end apart: 2 -> 2, of which waited for: 1 -> 2; matrix products, arithmetic and copies ran while one was open for 9% -> 2% of each run, Pallas kernels for 44% -> 31%
where the time goes in v4:
time: 421 us; the launch traced here: 420 us
  Pallas kernels  178 us (42%)
  waiting for transfers between devices  160 us (38%)
  matrix products  37.8 us (9%)
  local copies, waits for them, and re-layouts  19.7 us (5%)
  between operations  13.5 us (3%)
  other arithmetic  10.9 us (3%)
    reduce_scatter x1, waiting for transfers between devices, local(): lax.psum_scatter(jnp.dot(hidden, w_down, preferred_element_type=jnp.float...  141 us
    pallas_call x1, Pallas kernels, handover(): pl.pallas_call(handover_kernel, out_shape=(shape, shape), in_specs=[pl.Bl...  129 us
    pallas_call x1, Pallas kernels, exchange(): pl.pallas_call(exchange_kernel, out_shape=jax.ShapeDtypeStruct(pieces.sha...  49.2 us
    dot_general x1, matrix products, local(): jnp.dot(hidden, w_down, preferred_element_type=jnp.float32)  18.6 us
    all_gather x1, waiting for transfers between devices, local(): x_all = lax.all_gather(xin, 'mc', axis=0, tiled=True)  18.5 us
    dot_general x1, matrix products, local(): lax.dot_general(x_all, w_up_t, (((1,), (1,)), ((), ())), preferred_elemen...  17.4 us
    another operation x4, local copies, waits for them, and re-layouts, local(): jnp.stack([trainer_up.astype(jnp.bfloat16).T, trainer_down.astype(jnp.bfl...  10.5 us
  transfers between devices with their start and end apart: 2, of which 2 were waited for; matrix products, arithmetic and copies ran while one was open for 2% of the time, Pallas kernels for 31%

profile of v4, /device:TPU:1, one launch (start us, length us, event | category | flops | bytes accessed | tf_op | source)
XLA Modules:
  0.0 420.3 jit_solution(17005068170419685794)
XLA Ops:
  6.5 0.0 all-gather.2.cloned.1.call-start
  6.5 1.3 convert_reduce_fusion
  7.8 1.4 fusion.21
  9.3 1.3 convert_bitcast_fusion.1
  10.6 1.3 convert_element_type.34
  11.9 4.0 reshape.36
  15.9 1.3 copy.15
  17.2 4.0 reshape.35
  21.2 1.3 copy.14
  22.4 0.0 copy-start.5
  22.4 1.8 fusion.11.src
  24.2 49.2 %shard_map.55 = bf16[32,2,64,160]{3,2,1,0:T(8,128)(2,1)} custom-call(bf16[32,2,64,160]{3,2,1,0:T(8,128)(2,1)} %fusion.11.src), custom_call_target="tpu_custom_call" | custom-call | tf_op jit(solution)/shard_map/pallas_call | solution.py:58
  73.4 0.0 copy-done.5
  73.4 0.0 copy-done.4
  73.4 0.0 copy-start.2
  73.4 1.8 fusion.28
  75.2 1.9 copy-done
  77.1 1.2 fusion.27
  78.3 0.0 all-gather.2.cloned.1.call-update
  78.3 0.2 reduce-scatter.2.cloned.1.call-start
  78.6 1.1 fusion.39
  79.7 0.6 copy.17
  80.3 2.5 squeeze.21.dn_ref
  82.8 0.6 copy.16
  83.4 2.5 squeeze.20.up_ref
  85.9 129.2 %shard_map.56 = (bf16[2,8,64,5120]{3,2,1,0:T(8,128)(2,1)}, bf16[2,8,64,5120]{3,2,1,0:T(8,128)(2,1)}) custom-call(bf16[64,5120]{1,0:T(8,128)(2,1)} %squeeze.20.up_ref, bf16[64,5120]{1,0:T(8,128)(2,1)} %squeeze.21.dn_ref), custom_call_target="tpu_custom_call" | custom-call | tf_op jit(solution)/shard_map/pallas_call | solution.py:172
  215.2 18.5 %all-gather.2.cloned.1.call-done = bf16[1024,5120]{1,0:T(8,128)(2,1)} async-done(((bf16[64,5120]{1,0:T(8,128)(2,1)}), bf16[1024,5120]{1,0:T(8,128)(2,1)}) %all-gather.2.cloned.1.call-update) | async-done | bytes 10485776 | tf_op jit(solution)/shard_map/all_gather | solution.py:213
  233.7 17.4 %fusion.40 = f32[1024,1024]{1,0:T(8,128)} fusion(bf16[1024,5120]{1,0:T(8,128)(2,1)} %all-gather.2.cloned.1.call-done, bf16[1024,5120]{1,0:T(8,128)(2,1)} %bitcast.72), kind=kOutput, calls=%fused_computation.50 | convolution fusion | flops 10737418240 | bytes 25165824 | tf_op jit(solution)/shard_map/dot_general | solution.py:221
  251.1 18.6 %convolution_convert_fusion = bf16[1024,5120]{1,0:T(8,128)(2,1)} fusion(bf16[1024,5120]{1,0:T(8,128)(2,1)S(1)} %bitcast.71, f32[1024,1024]{1,0:T(8,128)} %fusion.40), kind=kOutput, calls=%fused_computation | convolution fusion | flops 10752098304 | bytes 25165824 | tf_op jit(solution)/shard_map/dot_general | solution.py:225
  269.7 0.0 reduce-scatter.2.cloned.1.call-update
  269.7 141.2 %reduce-scatter.2.cloned.1.call-done = bf16[64,5120]{1,0:T(8,128)(2,1)} async-done(((bf16[1024,5120]{1,0:T(8,128)(2,1)}), bf16[64,5120]{1,0:T(8,128)(2,1)}) %reduce-scatter.2.cloned.1.call-update) | async-done | bytes 655376 | tf_op jit(solution)/shard_map/reduce_scatter | solution.py:224
  410.9 2.6 fusion.31
  (11 shorter events, 0.0 us)
Async XLA Ops:
  6.5 227.1 %all-gather.2.cloned.1.call-start = ((), (), s32[]{:S(2)}) async-start(), calls=%async_computation.1 | async-start | bytes 11141120 | tf_op jit(solution)/shard_map/all_gather | solution.py:213
  22.4 51.0 %copy-start.5 = (s32[1,64]{1,0:T(1,128)S(1)}, s32[1,64]{1,0:T(1,128)}, u32[]{:S(2)}) copy-start(s32[1,64]{1,0:T(1,128)} %param.6) | copy-start | bytes 772
  24.2 49.2 %copy-start.4 = (f32[1,12,3,5120]{3,0,2,1:T(1,128)S(1)}, f32[1,12,3,5120]{3,0,2,1:T(1,128)}, u32[]{:S(2)}) copy-start(f32[1,12,3,5120]{3,0,2,1:T(1,128)} %param.7) | copy-start | bytes 2211844
  24.2 52.9 %copy-start.1 = (bf16[1,64,5120]{2,1,0:T(8,128)(2,1)S(1)}, bf16[1,64,5120]{2,1,0:T(8,128)(2,1)}, u32[]{:S(2)}) copy-start(bf16[1,64,5120]{2,1,0:T(8,128)(2,1)} %param.5) | copy-start | bytes 1966084
  73.4 5.1 %copy-start.2 = (bf16[32,2,64,160]{3,2,1,0:T(8,128)(2,1)S(1)}, bf16[32,2,64,160]{3,2,1,0:T(8,128)(2,1)}, u32[]{:S(2)}) copy-start(bf16[32,2,64,160]{3,2,1,0:T(8,128)(2,1)} %shard_map.55) | copy-start | bytes 3932164
  75.2 1.9 copy-start
  78.3 332.6 %reduce-scatter.2.cloned.1.call-start = ((), (), s32[]{:S(2)}) async-start(), calls=%async_computation.2 | async-start | bytes 11141120 | tf_op jit(solution)/shard_map/reduce_scatter | solution.py:224
  79.7 3.1 copy-start.3
  233.7 17.4 %copy-start.6 = (bf16[2,8,64,5120]{3,2,1,0:T(8,128)(2,1)S(1)}, bf16[2,8,64,5120]{3,2,1,0:T(8,128)(2,1)}, u32[]{:S(2)}) copy-start(bf16[2,8,64,5120]{3,2,1,0:T(8,128)(2,1)} %get-tuple-element.12) | copy-start | bytes 31457284
Sparse Core Ops, SparseCore 0:
  78.5 155.1 all-gather.1
  269.9 141.0 reduce-scatter.1

commit v5 on v4

--- a/solution.py
+++ b/solution.py
@@ -209,24 +209,30 @@
     padded = -(-piece // 16) * 16
     both = jnp.pad(both.reshape(2, n_mp, piece, rows), ((0, 0), (0, 0), (0, padded - piece), (0, 0)))
     both = exchange(both.transpose(1, 0, 2, 3))
-    xin, both = lax.optimization_barrier((xin, both))
-    x_all = lax.all_gather(xin, "mc", axis=0, tiled=True)
     both = both.transpose(1, 2, 0, 3).reshape(2, padded, n_mp * rows)
     up_all, dn_all = handover(both[0], both[1], n_rep)
     units = 2 * n_rep * padded
     w_up_t = up_all.reshape(units, n_mp * rows)
     w_down = dn_all.reshape(units, n_mp * rows)
 
-    hidden = jax.nn.gelu(
-        lax.dot_general(x_all, w_up_t, (((1,), (1,)), ((), ())), preferred_element_type=jnp.float32),
-        approximate=True,
-    ).astype(jnp.bfloat16)
-    mlp = lax.psum_scatter(
-        jnp.dot(hidden, w_down, preferred_element_type=jnp.float32).astype(jnp.bfloat16),
-        "mc",
-        scatter_dimension=0,
-        tiled=True,
-    ).astype(jnp.float32)
+    chunks = 2
+    step = xin.shape[0] // chunks
+    parts = []
+    for h in range(chunks):
+        x_all = lax.all_gather(xin[h * step:(h + 1) * step], "mc", axis=0, tiled=True)
+        hidden = jax.nn.gelu(
+            lax.dot_general(x_all, w_up_t, (((1,), (1,)), ((), ())), preferred_element_type=jnp.float32),
+            approximate=True,
+        ).astype(jnp.bfloat16)
+        parts.append(
+            lax.psum_scatter(
+                jnp.dot(hidden, w_down, preferred_element_type=jnp.float32).astype(jnp.bfloat16),
+                "mc",
+                scatter_dimension=0,
+                tiled=True,
+            )
+        )
+    mlp = jnp.concatenate(parts, axis=0).astype(jnp.float32)
     result = as_float + gate * mlp
     return result.astype(jnp.bfloat16)[None]
 

time: 421 us -> 481 us (1.14)
  waiting for transfers between devices: 160 us -> 202 us
  Pallas kernels: 178 us -> 191 us
  matrix products: 37.8 us -> 45.1 us
    reduce_scatter x1 -> x2, waiting for transfers between devices: 141 us -> 202 us  [local(): lax.psum_scatter(jnp.dot(hidden, w_down, preferred_element_type=jnp.float...]
    dot_general x1 -> x2, matrix products: 18.6 us -> 42.1 us  [local(): jnp.dot(hidden, w_down, preferred_element_type=jnp.float32)]
    pallas_call x1, Pallas kernels: 49.2 us -> 68.6 us  [exchange(): pl.pallas_call(exchange_kernel, out_shape=jax.ShapeDtypeStruct(pieces.sha...]
    all_gather x1 -> x2, waiting for transfers between devices: 18.5 us -> 0.04 us  [local(): lax.all_gather(xin[h * step:(h + 1) * step], 'mc', axis=0, tiled=True)]
    dot_general x1 -> x0, matrix products: 17.4 us -> none  [local(): lax.dot_general(x_all, w_up_t, (((1,), (1,)), ((), ())), preferred_elemen...]
    pallas_call x1, Pallas kernels: 129 us -> 122 us  [handover(): pl.pallas_call(handover_kernel, out_shape=(shape, shape), in_specs=[pl.Bl...]
  transfers between devices with their start and end apart: 2 -> 4, of which waited for: 2 -> 2; matrix products, arithmetic and copies ran while one was open for 2% -> 13% of each run, Pallas kernels for 31% -> 40%
where the time goes in v5:
time: 481 us
  waiting for transfers between devices  202 us (42%)
  Pallas kernels  191 us (40%)
  matrix products  45.1 us (9%)
  local copies, waits for them, and re-layouts  20.3 us (4%)
  between operations  13.3 us (3%)
  other arithmetic  8.7 us (2%)
    reduce_scatter x2, waiting for transfers between devices, local(): lax.psum_scatter(jnp.dot(hidden, w_down, preferred_element_type=jnp.float...  202 us
    pallas_call x1, Pallas kernels, handover(): pl.pallas_call(handover_kernel, out_shape=(shape, shape), in_specs=[pl.Bl...  122 us
    pallas_call x1, Pallas kernels, exchange(): pl.pallas_call(exchange_kernel, out_shape=jax.ShapeDtypeStruct(pieces.sha...  68.6 us
    dot_general x2, matrix products, local(): jnp.dot(hidden, w_down, preferred_element_type=jnp.float32)  42.1 us
    another operation x4, local copies, waits for them, and re-layouts, local(): jnp.stack([trainer_up.astype(jnp.bfloat16).T, trainer_down.astype(jnp.bfl...  10.6 us
  transfers between devices with their start and end apart: 4, of which 2 were waited for; matrix products, arithmetic and copies ran while one was open for 13% of the time, Pallas kernels for 40%

profile of v5, /device:TPU:1, one launch (start us, length us, event | category | flops | bytes accessed | tf_op | source)
XLA Modules:
  0.0 480.5 jit_solution(2754222348165234189)
XLA Ops:
  6.5 1.3 convert_reduce_fusion
  7.8 1.4 fusion.23
  9.3 2.9 fusion.40
  12.3 0.4 fusion.29
  12.6 0.9 fusion.55
  13.5 0.8 copy-done
  14.3 0.0 all-gather.3.cloned.1.call-update
  14.4 0.0 all-gather.5.cloned.1.call-start
  14.4 0.7 all-gather.5.cloned.1.call-update
  15.1 0.0 reduce-scatter.3.cloned.1.call-start
  15.2 0.1 convert_bitcast_fusion.1
  15.2 4.0 reshape.74
  19.2 1.4 copy.14
  20.7 1.3 convert_element_type.49
  22.0 4.0 reshape.75
  26.0 1.3 copy.15
  27.2 1.7 fusion.19.src
  29.0 68.6 %shard_map.55 = bf16[32,2,64,160]{3,2,1,0:T(8,128)(2,1)} custom-call(bf16[32,2,64,160]{3,2,1,0:T(8,128)(2,1)} %fusion.19.src), custom_call_target="tpu_custom_call" | custom-call | tf_op jit(solution)/shard_map/pallas_call | solution.py:58
  97.6 1.7 fusion.54
  99.3 0.6 copy.16
  99.9 2.5 squeeze.20.up_ref
  102.4 0.6 copy.17
  103.0 2.5 squeeze.21.dn_ref
  105.5 122.1 %shard_map.56 = (bf16[2,8,64,5120]{3,2,1,0:T(8,128)(2,1)}, bf16[2,8,64,5120]{3,2,1,0:T(8,128)(2,1)}) custom-call(bf16[64,5120]{1,0:T(8,128)(2,1)} %squeeze.20.up_ref, bf16[64,5120]{1,0:T(8,128)(2,1)} %squeeze.21.dn_ref), custom_call_target="tpu_custom_call" | custom-call | tf_op jit(solution)/shard_map/pallas_call | solution.py:172
  227.6 0.0 all-gather.3.cloned.1.call-done
  227.7 21.2 %convolution_convert_fusion.1 = bf16[512,5120]{1,0:T(8,128)(2,1)} fusion(bf16[1024,5120]{1,0:T(8,128)(2,1)} %bitcast.70, bf16[512,5120]{1,0:T(8,128)(2,1)} %all-gather.3.cloned.1.call-done, bf16[1024,5120]{1,0:T(8,128)(2,1)} %bitcast.68), kind=kOutput, calls=%fused_computation.1 | convolution fusion | flops 10744758272 | bytes 31457280 | tf_op jit(solution)/shard_map/dot_general | solution.py:229
  248.8 0.0 reduce-scatter.5.cloned.1.call-start
  248.9 0.0 all-gather.5.cloned.1.call-done
  248.9 21.0 %convolution_convert_fusion = bf16[512,5120]{1,0:T(8,128)(2,1)} fusion(bf16[1024,5120]{1,0:T(8,128)(2,1)} %bitcast.71, bf16[512,5120]{1,0:T(8,128)(2,1)} %all-gather.5.cloned.1.call-done, bf16[1024,5120]{1,0:T(8,128)(2,1)} %bitcast.69), kind=kOutput, calls=%fused_computation | convolution fusion | flops 10744758272 | bytes 31457280 | tf_op jit(solution)/shard_map/dot_general | solution.py:229
  269.9 98.6 %reduce-scatter.3.cloned.1.call-done = bf16[32,5120]{1,0:T(8,128)(2,1)} async-done(((bf16[512,5120]{1,0:T(8,128)(2,1)}), bf16[32,5120]{1,0:T(8,128)(2,1)}) %reduce-scatter.3.cloned.1.call-update) | async-done | bytes 327696 | tf_op jit(solution)/shard_map/reduce_scatter | solution.py:228
  368.5 103.0 %reduce-scatter.5.cloned.1.call-done = bf16[32,5120]{1,0:T(8,128)(2,1)} async-done(((bf16[512,5120]{1,0:T(8,128)(2,1)}), bf16[32,5120]{1,0:T(8,128)(2,1)}) %reduce-scatter.5.cloned.1.call-update) | async-done | bytes 327696 | tf_op jit(solution)/shard_map/reduce_scatter | solution.py:228
  471.5 2.5 fusion.26
  (12 shorter events, 0.1 us)
Async XLA Ops:
  6.5 221.1 %all-gather.3.cloned.1.call-start = ((), (), s32[]{:S(2)}) async-start(), calls=%async_computation.2 | async-start | bytes 5570560 | tf_op jit(solution)/shard_map/all_gather | solution.py:222
  9.3 3.0 copy-start.1
  12.2 2.1 copy-start
  12.2 2.9 copy-start.3
  14.4 234.5 %all-gather.5.cloned.1.call-start = ((), (), s32[]{:S(2)}) async-start(), calls=%async_computation.4 | async-start | bytes 5570560 | tf_op jit(solution)/shard_map/all_gather | solution.py:222
  15.1 353.4 %reduce-scatter.3.cloned.1.call-start = ((), (), s32[]{:S(2)}) async-start(), calls=%async_computation.3 | async-start | bytes 5570560 | tf_op jit(solution)/shard_map/reduce_scatter | solution.py:228
  248.8 222.6 %reduce-scatter.5.cloned.1.call-start = ((), (), s32[]{:S(2)}) async-start(), calls=%async_computation.5 | async-start | bytes 5570560 | tf_op jit(solution)/shard_map/reduce_scatter | solution.py:228
  269.9 201.6 %copy-start.2 = (bf16[1,64,5120]{2,1,0:T(8,128)(2,1)S(1)}, bf16[1,64,5120]{2,1,0:T(8,128)(2,1)}, u32[]{:S(2)}) copy-start(bf16[1,64,5120]{2,1,0:T(8,128)(2,1)} %param.5) | copy-start | bytes 1966084
Sparse Core Ops, SparseCore 0:
  14.5 127.2 all-gather.2
  144.2 93.9 all-gather.4
  249.0 119.4 reduce-scatter.2
  372.0 99.4 reduce-scatter.4

commit v6 on v4

--- a/solution.py
+++ b/solution.py
@@ -7,17 +7,17 @@
 from jax.experimental.pallas import tpu as pltpu
 from jax.sharding import Mesh, PartitionSpec as P
 
-MP = ("mc", "core")
+MP = ("zh", "y", "core")
 MESH_ID = pl.DeviceIdType.MESH
 
 
 def exchange_kernel(src, dst, send_sem, recv_sem, local_sem):
     n = src.shape[0]
-    me = lax.axis_index("mc") * 2 + lax.axis_index("core")
+    me = (lax.axis_index("zh") * 4 + lax.axis_index("y")) * 2 + lax.axis_index("core")
     r = lax.axis_index("rep")
 
     def dev(i):
-        return (r, lax.div(i, 2), lax.rem(i, 2))
+        return (r, lax.div(i, 8), lax.rem(lax.div(i, 2), 4), lax.rem(i, 2))
 
     barrier = pltpu.get_barrier_semaphore()
     for k in range(1, n):
@@ -73,7 +73,8 @@
     n_rep = up_out.shape[1]
     n_x = n_rep // 2
     me = lax.axis_index("rep")
-    mc = lax.axis_index("mc")
+    zh = lax.axis_index("zh")
+    yy = lax.axis_index("y")
     c = lax.axis_index("core")
     other = 1 - c
     x = lax.div(me, 2)
@@ -83,8 +84,8 @@
 
     barrier = pltpu.get_barrier_semaphore()
     for t in [partner] + [xo + zl for xo in xs]:
-        pl.semaphore_signal(barrier, 1, device_id=(t, mc, c), device_id_type=MESH_ID)
-    pl.semaphore_signal(barrier, 1, device_id=(me, mc, other), device_id_type=MESH_ID)
+        pl.semaphore_signal(barrier, 1, device_id=(t, zh, yy, c), device_id_type=MESH_ID)
+    pl.semaphore_signal(barrier, 1, device_id=(me, zh, yy, other), device_id_type=MESH_ID)
     pl.semaphore_wait(barrier, n_x + 1)
 
     pairs = ((up_ref, up_out), (dn_ref, dn_out))
@@ -96,7 +97,7 @@
             dst_ref=dst.at[c, slot],
             send_sem=send_sem.at[i, 0],
             recv_sem=recv_sem.at[i, slot],
-            device_id=(slot, mc, c),
+            device_id=(slot, zh, yy, c),
             device_id_type=MESH_ID,
         )
 
@@ -112,7 +113,7 @@
                 dst_ref=dst.at[c, me],
                 send_sem=send_sem.at[i, j],
                 recv_sem=recv_sem.at[i, me],
-                device_id=(t, mc, c),
+                device_id=(t, zh, yy, c),
                 device_id_type=MESH_ID,
             )
             cp.start()
@@ -125,7 +126,7 @@
                 dst_ref=dst.at[c, partner],
                 send_sem=send_sem.at[i, n_x + j],
                 recv_sem=recv_sem.at[i, partner],
-                device_id=(xo + zl, mc, c),
+                device_id=(xo + zl, zh, yy, c),
                 device_id_type=MESH_ID,
             )
             cp.start()
@@ -144,7 +145,7 @@
                 dst_ref=dst.at[c, slot],
                 send_sem=fwd_send.at[i, slot],
                 recv_sem=fwd_recv.at[i, slot],
-                device_id=(me, mc, other),
+                device_id=(me, zh, yy, other),
                 device_id_type=MESH_ID,
             )
             fw.start()
@@ -159,7 +160,7 @@
                 dst_ref=dst.at[other, slot],
                 send_sem=fwd_send.at[i, slot],
                 recv_sem=fwd_recv.at[i, slot],
-                device_id=(me, mc, other),
+                device_id=(me, zh, yy, other),
                 device_id_type=MESH_ID,
             ).wait_recv()
     for fw in forwards:
@@ -210,7 +211,7 @@
     both = jnp.pad(both.reshape(2, n_mp, piece, rows), ((0, 0), (0, 0), (0, padded - piece), (0, 0)))
     both = exchange(both.transpose(1, 0, 2, 3))
     xin, both = lax.optimization_barrier((xin, both))
-    x_all = lax.all_gather(xin, "mc", axis=0, tiled=True)
+    x_all = lax.all_gather(lax.all_gather(xin, "zh", axis=0, tiled=True), "y", axis=0, tiled=True)
     both = both.transpose(1, 2, 0, 3).reshape(2, padded, n_mp * rows)
     up_all, dn_all = handover(both[0], both[1], n_rep)
     units = 2 * n_rep * padded
@@ -221,19 +222,16 @@
         lax.dot_general(x_all, w_up_t, (((1,), (1,)), ((), ())), preferred_element_type=jnp.float32),
         approximate=True,
     ).astype(jnp.bfloat16)
-    mlp = lax.psum_scatter(
-        jnp.dot(hidden, w_down, preferred_element_type=jnp.float32).astype(jnp.bfloat16),
-        "mc",
-        scatter_dimension=0,
-        tiled=True,
-    ).astype(jnp.float32)
+    partial = jnp.dot(hidden, w_down, preferred_element_type=jnp.float32).astype(jnp.bfloat16)
+    partial = lax.psum_scatter(partial, "y", scatter_dimension=0, tiled=True)
+    mlp = lax.psum_scatter(partial, "zh", scatter_dimension=0, tiled=True).astype(jnp.float32)
     result = as_float + gate * mlp
     return result.astype(jnp.bfloat16)[None]
 
 
 def solution(mesh):
     n_rep, n_mp = mesh.devices.shape
-    chips = Mesh(mesh.devices.reshape(n_rep, n_mp // 2, 2), ("rep", "mc", "core"))
+    chips = Mesh(mesh.devices.reshape(n_rep, 4, n_mp // 8, 2), ("rep", "zh", "y", "core"))
     in_specs = (
         P("rep", MP, None),
         P("rep", MP),

time: 421 us -> 484 us (1.15)
  waiting for transfers between devices: 160 us -> 230 us
  Pallas kernels: 178 us -> 171 us
    all_gather x1 -> x2, waiting for transfers between devices: 18.5 us -> 71.2 us  [the longest x1 71.2 us: local(): lax.all_gather(xin, 'zh', axis=0, tiled=True)]
    reduce_scatter x1 -> x2, waiting for transfers between devices: 141 us -> 159 us  [the longest x1 97.9 us: local(): partial = lax.psum_scatter(partial, 'y', scatter_dimension=0, tiled=True)]
    pallas_call x1, Pallas kernels: 129 us -> 122 us  [handover(): pl.pallas_call(handover_kernel, out_shape=(shape, shape), in_specs=[pl.Bl...]
  transfers between devices with their start and end apart: 2 -> 4, of which waited for: 2 -> 3; matrix products, arithmetic and copies ran while one was open for 2% -> 2% of each run, Pallas kernels for 31% -> 25%
where the time goes in v6:
time: 484 us
  waiting for transfers between devices  230 us (48%)
  Pallas kernels  171 us (35%)
  matrix products  37.9 us (8%)
  local copies, waits for them, and re-layouts  19.7 us (4%)
  between operations  13.3 us (3%)
  other arithmetic  10.9 us (2%)
    pallas_call x1, Pallas kernels, handover(): pl.pallas_call(handover_kernel, out_shape=(shape, shape), in_specs=[pl.Bl...  122 us
    reduce_scatter x1, waiting for transfers between devices, local(): partial = lax.psum_scatter(partial, 'y', scatter_dimension=0, tiled=True)  97.9 us
    all_gather x1, waiting for transfers between devices, local(): lax.all_gather(xin, 'zh', axis=0, tiled=True)  71.2 us
    reduce_scatter x1, waiting for transfers between devices, local(): lax.psum_scatter(partial, 'zh', scatter_dimension=0, tiled=True)  61.1 us
    pallas_call x1, Pallas kernels, exchange(): pl.pallas_call(exchange_kernel, out_shape=jax.ShapeDtypeStruct(pieces.sha...  49.2 us
    dot_general x1, matrix products, local(): jnp.dot(hidden, w_down, preferred_element_type=jnp.float32)  18.7 us
    dot_general x1, matrix products, local(): lax.dot_general(x_all, w_up_t, (((1,), (1,)), ((), ())), preferred_elemen...  17.4 us
    another operation x4, local copies, waits for them, and re-layouts, local(): jnp.stack([trainer_up.astype(jnp.bfloat16).T, trainer_down.astype(jnp.bfl...  10.5 us
  transfers between devices with their start and end apart: 4, of which 3 were waited for; matrix products, arithmetic and copies ran while one was open for 2% of the time, Pallas kernels for 25%

profile of v6, /device:TPU:1, one launch (start us, length us, event | category | flops | bytes accessed | tf_op | source)
XLA Modules:
  0.0 483.6 jit_solution(6173489903517736666)
XLA Ops:
  6.5 1.3 convert_reduce_fusion
  7.8 1.4 fusion.21
  9.3 1.3 convert_bitcast_fusion.1
  10.6 1.3 convert_element_type.34
  11.9 4.0 reshape.36
  15.9 1.3 copy.15
  17.2 4.0 reshape.35
  21.2 1.3 copy.14
  22.4 1.8 fusion.11.src
  24.2 49.2 %shard_map.55 = bf16[32,2,64,160]{3,2,1,0:T(8,128)(2,1)} custom-call(bf16[32,2,64,160]{3,2,1,0:T(8,128)(2,1)} %fusion.11.src), custom_call_target="tpu_custom_call" | custom-call | tf_op jit(solution)/shard_map/pallas_call | solution.py:58
  73.4 1.8 fusion.28
  75.2 1.9 copy-done
  77.1 1.2 fusion.27
  78.3 0.0 all-gather.3.cloned.1.call-update
  78.3 0.0 all-gather.5.cloned.1.call-start
  78.4 71.2 %all-gather.3.cloned.1.call-done = bf16[256,5120]{1,0:T(8,128)(2,1)} async-done(((bf16[64,5120]{1,0:T(8,128)(2,1)}), bf16[256,5120]{1,0:T(8,128)(2,1)}) %all-gather.3.cloned.1.call-update) | async-done | bytes 2621456 | tf_op jit(solution)/shard_map/all_gather | solution.py:214
  149.6 0.0 all-gather.5.cloned.1.call-update
  149.6 0.2 reduce-scatter.3.cloned.1.call-start
  149.8 1.1 fusion.39
  151.0 0.6 copy.17
  151.5 2.5 squeeze.21.dn_ref
  154.1 0.6 copy.16
  154.7 2.5 squeeze.20.up_ref
  157.2 122.0 %shard_map.56 = (bf16[2,8,64,5120]{3,2,1,0:T(8,128)(2,1)}, bf16[2,8,64,5120]{3,2,1,0:T(8,128)(2,1)}) custom-call(bf16[64,5120]{1,0:T(8,128)(2,1)} %squeeze.20.up_ref, bf16[64,5120]{1,0:T(8,128)(2,1)} %squeeze.21.dn_ref), custom_call_target="tpu_custom_call" | custom-call | tf_op jit(solution)/shard_map/pallas_call | solution.py:173
  279.2 0.0 all-gather.5.cloned.1.call-done
  279.2 17.4 %fusion.40 = f32[1024,1024]{1,0:T(8,128)} fusion(bf16[1024,5120]{1,0:T(8,128)(2,1)} %all-gather.5.cloned.1.call-done, bf16[1024,5120]{1,0:T(8,128)(2,1)} %bitcast.72), kind=kOutput, calls=%fused_computation.50 | convolution fusion | flops 10737418240 | bytes 25165824 | tf_op jit(solution)/shard_map/dot_general | solution.py:222
  296.7 18.7 %convolution_convert_fusion = bf16[1024,5120]{1,0:T(8,128)(2,1)} fusion(bf16[1024,5120]{1,0:T(8,128)(2,1)S(1)} %bitcast.71, f32[1024,1024]{1,0:T(8,128)} %fusion.40), kind=kOutput, calls=%fused_computation | convolution fusion | flops 10752098304 | bytes 25165824 | tf_op jit(solution)/shard_map/dot_general | solution.py:225
  315.3 0.0 reduce-scatter.3.cloned.1.call-update
  315.4 0.0 reduce-scatter.5.cloned.1.call-start
  315.4 97.9 %reduce-scatter.3.cloned.1.call-done = bf16[256,5120]{1,0:T(8,128)(2,1)} async-done(((bf16[1024,5120]{1,0:T(8,128)(2,1)}), bf16[256,5120]{1,0:T(8,128)(2,1)}) %reduce-scatter.3.cloned.1.call-update) | async-done | bytes 2621456 | tf_op jit(solution)/shard_map/reduce_scatter | solution.py:226
  413.3 61.1 %reduce-scatter.5.cloned.1.call-done = bf16[64,5120]{1,0:T(8,128)(2,1)} async-done(((bf16[256,5120]{1,0:T(8,128)(2,1)}), bf16[64,5120]{1,0:T(8,128)(2,1)}) %reduce-scatter.5.cloned.1.call-update) | async-done | bytes 655376 | tf_op jit(solution)/shard_map/reduce_scatter | solution.py:227
  474.5 2.6 fusion.31
  (17 shorter events, 0.1 us)
Async XLA Ops:
  6.5 143.0 %all-gather.3.cloned.1.call-start = ((), (), s32[]{:S(2)}) async-start(), calls=%async_computation.2 | async-start | bytes 3276800 | tf_op jit(solution)/shard_map/all_gather | solution.py:214
  22.4 51.0 %copy-start.5 = (s32[1,64]{1,0:T(1,128)S(1)}, s32[1,64]{1,0:T(1,128)}, u32[]{:S(2)}) copy-start(s32[1,64]{1,0:T(1,128)} %param.6) | copy-start | bytes 772
  24.2 49.2 %copy-start.4 = (f32[1,12,3,5120]{3,0,2,1:T(1,128)S(1)}, f32[1,12,3,5120]{3,0,2,1:T(1,128)}, u32[]{:S(2)}) copy-start(f32[1,12,3,5120]{3,0,2,1:T(1,128)} %param.7) | copy-start | bytes 2211844
  24.2 52.9 %copy-start.1 = (bf16[1,64,5120]{2,1,0:T(8,128)(2,1)S(1)}, bf16[1,64,5120]{2,1,0:T(8,128)(2,1)}, u32[]{:S(2)}) copy-start(bf16[1,64,5120]{2,1,0:T(8,128)(2,1)} %param.5) | copy-start | bytes 1966084
  75.2 1.9 copy-start
  77.1 72.7 %copy-start.2 = (bf16[32,2,64,160]{3,2,1,0:T(8,128)(2,1)S(1)}, bf16[32,2,64,160]{3,2,1,0:T(8,128)(2,1)}, u32[]{:S(2)}) copy-start(bf16[32,2,64,160]{3,2,1,0:T(8,128)(2,1)} %shard_map.55) | copy-start | bytes 3932164
  78.3 200.9 %all-gather.5.cloned.1.call-start = ((), (), s32[]{:S(2)}) async-start(), calls=%async_computation.3 | async-start | bytes 13107200 | tf_op jit(solution)/shard_map/all_gather | solution.py:214
  149.6 263.7 %reduce-scatter.3.cloned.1.call-start = ((), (), s32[]{:S(2)}) async-start(), calls=%async_computation.4 | async-start | bytes 13107200 | tf_op jit(solution)/shard_map/reduce_scatter | solution.py:226
  151.0 3.1 copy-start.3
  279.2 17.4 %copy-start.6 = (bf16[2,8,64,5120]{3,2,1,0:T(8,128)(2,1)S(1)}, bf16[2,8,64,5120]{3,2,1,0:T(8,128)(2,1)}, u32[]{:S(2)}) copy-start(bf16[2,8,64,5120]{3,2,1,0:T(8,128)(2,1)} %get-tuple-element.12) | copy-start | bytes 31457284
  315.4 159.1 %reduce-scatter.5.cloned.1.call-start = ((), (), s32[]{:S(2)}) async-start(), calls=%async_computation.5 | async-start | bytes 3276800 | tf_op jit(solution)/shard_map/reduce_scatter | solution.py:227
Sparse Core Ops, SparseCore 0:
  78.5 71.0 all-gather.2
  151.4 101.8 all-gather.4
  315.5 97.7 reduce-scatter.2
  415.7 58.7 reduce-scatter.4

commit v7 on v4

--- a/solution.py
+++ b/solution.py
@@ -200,6 +200,7 @@
     scale = chosen[:, 1]
     gate = chosen[:, 2]
     xin = (normed * (1.0 + scale) + shift).astype(jnp.bfloat16)
+    x_all = lax.all_gather(xin, "mc", axis=0, tiled=True)
 
     n_mp = lax.psum(1, MP)
     n_rep = lax.psum(1, "rep")
@@ -209,8 +210,6 @@
     padded = -(-piece // 16) * 16
     both = jnp.pad(both.reshape(2, n_mp, piece, rows), ((0, 0), (0, 0), (0, padded - piece), (0, 0)))
     both = exchange(both.transpose(1, 0, 2, 3))
-    xin, both = lax.optimization_barrier((xin, both))
-    x_all = lax.all_gather(xin, "mc", axis=0, tiled=True)
     both = both.transpose(1, 2, 0, 3).reshape(2, padded, n_mp * rows)
     up_all, dn_all = handover(both[0], both[1], n_rep)
     units = 2 * n_rep * padded

time: 421 us -> 429 us (1.019)
  Pallas kernels: 178 us -> 206 us
  waiting for transfers between devices: 160 us -> 144 us
  matrix products: 37.8 us -> 32.8 us
    pallas_call x1, Pallas kernels: 49.2 us -> 73.1 us  [exchange(): pl.pallas_call(exchange_kernel, out_shape=jax.ShapeDtypeStruct(pieces.sha...]
    all_gather x1, waiting for transfers between devices: 18.5 us -> 0.02 us  [local(): x_all = lax.all_gather(xin, 'mc', axis=0, tiled=True)]
    dot_general x1, matrix products: 18.6 us -> 14 us  [local(): jnp.dot(hidden, w_down, preferred_element_type=jnp.float32)]
  transfers between devices with their start and end apart: 2 -> 2, of which waited for: 2 -> 1; matrix products, arithmetic and copies ran while one was open for 2% -> 6% of each run, Pallas kernels for 31% -> 48%
where the time goes in v7:
time: 429 us
  Pallas kernels  206 us (48%)
  waiting for transfers between devices  144 us (34%)
  matrix products  32.8 us (8%)
  local copies, waits for them, and re-layouts  21.3 us (5%)
  between operations  13.5 us (3%)
  other arithmetic  10.9 us (3%)
    reduce_scatter x1, waiting for transfers between devices, local(): lax.psum_scatter(jnp.dot(hidden, w_down, preferred_element_type=jnp.float...  144 us
    pallas_call x1, Pallas kernels, handover(): pl.pallas_call(handover_kernel, out_shape=(shape, shape), in_specs=[pl.Bl...  133 us
    pallas_call x1, Pallas kernels, exchange(): pl.pallas_call(exchange_kernel, out_shape=jax.ShapeDtypeStruct(pieces.sha...  73.1 us
    dot_general x1, matrix products, local(): lax.dot_general(x_all, w_up_t, (((1,), (1,)), ((), ())), preferred_elemen...  15.8 us
    dot_general x1, matrix products, local(): jnp.dot(hidden, w_down, preferred_element_type=jnp.float32)  14 us
    another operation x4, local copies, waits for them, and re-layouts, local(): jnp.stack([trainer_up.astype(jnp.bfloat16).T, trainer_down.astype(jnp.bfl...  11.5 us
  transfers between devices with their start and end apart: 2, of which 1 were waited for; matrix products, arithmetic and copies ran while one was open for 6% of the time, Pallas kernels for 48%

profile of v7, /device:TPU:1, one launch (start us, length us, event | category | flops | bytes accessed | tf_op | source)
XLA Modules:
  0.0 428.8 jit_solution(5544643750349183455)
XLA Ops:
  6.5 0.0 all-gather.2.cloned.1.call-start
  6.5 1.3 convert_reduce_fusion
  7.9 1.4 fusion.21
  9.3 0.0 copy-start.2
  9.4 3.0 fusion.28
  12.3 0.0 copy-start
  12.4 1.9 copy-done
  14.2 0.0 copy-done.1
  14.2 1.2 fusion.27
  15.4 0.0 all-gather.2.cloned.1.call-update
  15.5 0.0 reduce-scatter.2.cloned.1.call-start
  15.5 0.0 copy-done.2
  15.5 0.1 convert_element_type.34
  15.6 4.0 reshape.36
  19.6 1.4 copy.15
  21.0 1.3 convert_bitcast_fusion.1
  22.4 4.0 reshape.35
  26.3 2.1 copy.14
  28.4 2.9 fusion.11.src
  31.3 73.1 %shard_map.55 = bf16[32,2,64,160]{3,2,1,0:T(8,128)(2,1)} custom-call(bf16[32,2,64,160]{3,2,1,0:T(8,128)(2,1)} %fusion.11.src), custom_call_target="tpu_custom_call" | custom-call | tf_op jit(solution)/shard_map/pallas_call | solution.py:58
  104.5 1.7 fusion.39
  106.1 0.6 copy.17
  106.7 2.5 squeeze.21.dn_ref
  109.3 0.6 copy.16
  109.9 2.5 squeeze.20.up_ref
  112.4 132.7 %shard_map.56 = (bf16[2,8,64,5120]{3,2,1,0:T(8,128)(2,1)}, bf16[2,8,64,5120]{3,2,1,0:T(8,128)(2,1)}) custom-call(bf16[64,5120]{1,0:T(8,128)(2,1)} %squeeze.20.up_ref, bf16[64,5120]{1,0:T(8,128)(2,1)} %squeeze.21.dn_ref), custom_call_target="tpu_custom_call" | custom-call | tf_op jit(solution)/shard_map/pallas_call | solution.py:172
  245.1 0.0 all-gather.2.cloned.1.call-done
  245.2 15.8 %fusion.40 = f32[1024,1024]{1,0:T(8,128)S(1)} fusion(bf16[1024,5120]{1,0:T(8,128)(2,1)} %all-gather.2.cloned.1.call-done, bf16[1024,5120]{1,0:T(8,128)(2,1)} %bitcast.72), kind=kOutput, calls=%fused_computation.50 | convolution fusion | flops 10737418240 | bytes 25165824 | tf_op jit(solution)/shard_map/dot_general | solution.py:220
  261.0 14.0 %convolution_convert_fusion = bf16[1024,5120]{1,0:T(8,128)(2,1)} fusion(bf16[1024,5120]{1,0:T(8,128)(2,1)S(1)} %bitcast.71, f32[1024,1024]{1,0:T(8,128)S(1)} %fusion.40), kind=kOutput, calls=%fused_computation | convolution fusion | flops 10752098304 | bytes 25165824 | tf_op jit(solution)/shard_map/dot_general | solution.py:224
  275.0 0.0 reduce-scatter.2.cloned.1.call-update
  275.0 144.4 %reduce-scatter.2.cloned.1.call-done = bf16[64,5120]{1,0:T(8,128)(2,1)} async-done(((bf16[1024,5120]{1,0:T(8,128)(2,1)}), bf16[64,5120]{1,0:T(8,128)(2,1)}) %reduce-scatter.2.cloned.1.call-update) | async-done | bytes 655376 | tf_op jit(solution)/shard_map/reduce_scatter | solution.py:223
  419.4 2.6 fusion.31
  (5 shorter events, 0.0 us)
Async XLA Ops:
  6.5 7.7 %copy-start.1 = (bf16[1,64,5120]{2,1,0:T(8,128)(2,1)S(1)}, bf16[1,64,5120]{2,1,0:T(8,128)(2,1)}, u32[]{:S(2)}) copy-start(bf16[1,64,5120]{2,1,0:T(8,128)(2,1)} %param.5) | copy-start | bytes 1966084
  6.5 238.6 %all-gather.2.cloned.1.call-start = ((), (), s32[]{:S(2)}) async-start(), calls=%async_computation.1 | async-start | bytes 11141120 | tf_op jit(solution)/shard_map/all_gather | solution.py:203
  9.3 6.2 %copy-start.2 = (f32[1728,160]{0,1:T(8,128)S(1)}, f32[1728,160]{0,1:T(8,128)}, u32[]{:S(2)}) copy-start(f32[1728,160]{0,1:T(8,128)} %param.9) | copy-start | bytes 3317764
  12.3 1.9 copy-start
  15.5 403.9 %reduce-scatter.2.cloned.1.call-start = ((), (), s32[]{:S(2)}) async-start(), calls=%async_computation.2 | async-start | bytes 11141120 | tf_op jit(solution)/shard_map/reduce_scatter | solution.py:223
  245.1 15.8 %copy-start.3 = (bf16[2,8,64,5120]{3,2,1,0:T(8,128)(2,1)S(1)}, bf16[2,8,64,5120]{3,2,1,0:T(8,128)(2,1)}, u32[]{:S(2)}) copy-start(bf16[2,8,64,5120]{3,2,1,0:T(8,128)(2,1)} %get-tuple-element.8) | copy-start | bytes 31457284
Sparse Core Ops, SparseCore 0:
  15.6 211.5 all-gather.1
  275.1 144.2 reduce-scatter.1

commit v8 on v4

--- a/solution.py
+++ b/solution.py
@@ -207,11 +207,12 @@
     piece = cols // n_mp
     both = jnp.stack([trainer_up.astype(jnp.bfloat16).T, trainer_down.astype(jnp.bfloat16)])
     padded = -(-piece // 16) * 16
-    both = jnp.pad(both.reshape(2, n_mp, piece, rows), ((0, 0), (0, 0), (0, padded - piece), (0, 0)))
-    both = exchange(both.transpose(1, 0, 2, 3))
+    flat = (piece * rows // 120, 120)
+    both = exchange(both.reshape(2, n_mp, *flat).transpose(1, 0, 2, 3))
     xin, both = lax.optimization_barrier((xin, both))
     x_all = lax.all_gather(xin, "mc", axis=0, tiled=True)
-    both = both.transpose(1, 2, 0, 3).reshape(2, padded, n_mp * rows)
+    both = both.reshape(n_mp, 2, piece, rows).transpose(1, 2, 0, 3)
+    both = jnp.pad(both, ((0, 0), (0, padded - piece), (0, 0), (0, 0))).reshape(2, padded, n_mp * rows)
     up_all, dn_all = handover(both[0], both[1], n_rep)
     units = 2 * n_rep * padded
     w_up_t = up_all.reshape(units, n_mp * rows)

time: 421 us -> 387 us (0.919)
  Pallas kernels: 178 us -> 159 us
  matrix products: 37.8 us -> 31.6 us
  local copies, waits for them, and re-layouts: 19.7 us -> 14.9 us
    pallas_call x1, Pallas kernels: 49.2 us -> 32.8 us  [exchange(): pl.pallas_call(exchange_kernel, out_shape=jax.ShapeDtypeStruct(pieces.sha...]
    another operation x4 -> x2, local copies, waits for them, and re-layouts: 10.5 us -> 1.85 us  [local(): jnp.stack([trainer_up.astype(jnp.bfloat16).T, trainer_down.astype(jnp.bfl...]
    dot_general x1, matrix products: 18.6 us -> 14.2 us  [local(): jnp.dot(hidden, w_down, preferred_element_type=jnp.float32)]
  transfers between devices with their start and end apart: 2 -> 2, of which waited for: 2 -> 2; matrix products, arithmetic and copies ran while one was open for 2% -> 3% of each run, Pallas kernels for 31% -> 33%
where the time goes in v8:
time: 387 us; the launch traced here: 386 us
  Pallas kernels  159 us (41%)
  waiting for transfers between devices  158 us (41%)
  matrix products  31.6 us (8%)
  local copies, waits for them, and re-layouts  14.9 us (4%)
  between operations  13.6 us (4%)
  other arithmetic  9.22 us (2%)
    reduce_scatter x1, waiting for transfers between devices, local(): lax.psum_scatter(jnp.dot(hidden, w_down, preferred_element_type=jnp.float...  140 us
    pallas_call x1, Pallas kernels, handover(): pl.pallas_call(handover_kernel, out_shape=(shape, shape), in_specs=[pl.Bl...  126 us
    pallas_call x1, Pallas kernels, exchange(): pl.pallas_call(exchange_kernel, out_shape=jax.ShapeDtypeStruct(pieces.sha...  32.8 us
    all_gather x1, waiting for transfers between devices, local(): x_all = lax.all_gather(xin, 'mc', axis=0, tiled=True)  17.8 us
    dot_general x1, matrix products, local(): lax.dot_general(x_all, w_up_t, (((1,), (1,)), ((), ())), preferred_elemen...  15.6 us
    dot_general x1, matrix products, local(): jnp.dot(hidden, w_down, preferred_element_type=jnp.float32)  14.2 us
  transfers between devices with their start and end apart: 2, of which 2 were waited for; matrix products, arithmetic and copies ran while one was open for 3% of the time, Pallas kernels for 33%

profile of v8, /device:TPU:1, one launch (start us, length us, event | category | flops | bytes accessed | tf_op | source)
XLA Modules:
  0.0 386.3 jit_solution(8323304759291775445)
XLA Ops:
  6.5 0.0 all-gather.2.cloned.1.call-start
  6.5 1.4 convert_reduce_fusion
  7.9 1.4 fusion.17
  9.4 1.3 convert_bitcast_fusion.1
  10.7 0.3 copy.11
  11.0 0.9 stack.9
  11.9 0.1 convert_element_type.34
  12.0 0.0 copy-start.2
  12.0 0.0 copy-start.4
  12.0 0.3 copy.12
  12.3 0.9 stack.10
  13.3 1.2 maximum_bitcast_fusion.src
  14.5 32.8 %shard_map.55 = bf16[32,2,72,120]{3,2,1,0:T(8,128)(2,1)} custom-call(bf16[32,2,72,120]{3,2,1,0:T(8,128)(2,1)} %maximum_bitcast_fusion.src), custom_call_target="tpu_custom_call" | custom-call | tf_op jit(solution)/shard_map/pallas_call | solution.py:58
  47.4 1.8 fusion.24
  49.2 1.8 copy-done
  51.0 1.2 fusion.23
  52.2 0.0 all-gather.2.cloned.1.call-update
  52.3 0.2 reduce-scatter.2.cloned.1.call-start
  52.5 4.0 %reshape.35 = bf16[32,2,54,160]{3,2,1,0:T(8,128)(2,1)S(1)} reshape(bf16[32,2,72,120]{3,2,1,0:T(8,128)(2,1)} %shard_map.55) | data formatting | bytes 2211840 | tf_op jit(solution)/shard_map/reshape | solution.py:214
  56.5 0.3 pad_slice_fusion
  56.9 0.6 copy.16
  57.5 2.5 squeeze.21.dn_ref
  60.0 0.6 copy.15
  60.6 2.5 squeeze.20.up_ref
  63.1 125.8 %shard_map.56 = (bf16[2,8,64,5120]{3,2,1,0:T(8,128)(2,1)}, bf16[2,8,64,5120]{3,2,1,0:T(8,128)(2,1)}) custom-call(bf16[64,5120]{1,0:T(8,128)(2,1)} %squeeze.20.up_ref, bf16[64,5120]{1,0:T(8,128)(2,1)} %squeeze.21.dn_ref), custom_call_target="tpu_custom_call" | custom-call | tf_op jit(solution)/shard_map/pallas_call | solution.py:172
  188.9 17.8 %all-gather.2.cloned.1.call-done = bf16[1024,5120]{1,0:T(8,128)(2,1)} async-done(((bf16[64,5120]{1,0:T(8,128)(2,1)}), bf16[1024,5120]{1,0:T(8,128)(2,1)}) %all-gather.2.cloned.1.call-update) | async-done | bytes 10485776 | tf_op jit(solution)/shard_map/all_gather | solution.py:213
  206.8 15.6 %fusion.35 = f32[1024,1024]{1,0:T(8,128)S(1)} fusion(bf16[1024,5120]{1,0:T(8,128)(2,1)} %all-gather.2.cloned.1.call-done, bf16[1024,5120]{1,0:T(8,128)(2,1)} %bitcast.74), kind=kOutput, calls=%fused_computation.47 | convolution fusion | flops 10737418240 | bytes 25165824 | tf_op jit(solution)/shard_map/dot_general | solution.py:222
  222.3 0.0 copy-done.5
  222.3 14.2 %convolution_convert_fusion = bf16[1024,5120]{1,0:T(8,128)(2,1)} fusion(bf16[1024,5120]{1,0:T(8,128)(2,1)S(1)} %bitcast.73, f32[1024,1024]{1,0:T(8,128)S(1)} %fusion.35), kind=kOutput, calls=%fused_computation | convolution fusion | flops 10752098304 | bytes 25165824 | tf_op jit(solution)/shard_map/dot_general | solution.py:226
  236.6 0.0 reduce-scatter.2.cloned.1.call-update
  236.6 140.3 %reduce-scatter.2.cloned.1.call-done = bf16[64,5120]{1,0:T(8,128)(2,1)} async-done(((bf16[1024,5120]{1,0:T(8,128)(2,1)}), bf16[64,5120]{1,0:T(8,128)(2,1)}) %reduce-scatter.2.cloned.1.call-update) | async-done | bytes 655376 | tf_op jit(solution)/shard_map/reduce_scatter | solution.py:225
  376.9 2.6 fusion.27
  (10 shorter events, 0.0 us)
Async XLA Ops:
  6.5 5.4 %copy-start.3 = (f32[1728,160]{0,1:T(8,128)S(1)}, f32[1728,160]{0,1:T(8,128)}, u32[]{:S(2)}) copy-start(f32[1728,160]{0,1:T(8,128)} %param.9) | copy-start | bytes 3317764
  6.5 200.2 %all-gather.2.cloned.1.call-start = ((), (), s32[]{:S(2)}) async-start(), calls=%async_computation.1 | async-start | bytes 11141120 | tf_op jit(solution)/shard_map/all_gather | solution.py:213
  12.0 35.4 %copy-start.2 = (f32[1,12,3,5120]{3,0,2,1:T(1,128)S(1)}, f32[1,12,3,5120]{3,0,2,1:T(1,128)}, u32[]{:S(2)}) copy-start(f32[1,12,3,5120]{3,0,2,1:T(1,128)} %param.7) | copy-start | bytes 2211844
  12.0 35.4 %copy-start.4 = (s32[1,64]{1,0:T(1,128)S(1)}, s32[1,64]{1,0:T(1,128)}, u32[]{:S(2)}) copy-start(s32[1,64]{1,0:T(1,128)} %param.6) | copy-start | bytes 772
  14.5 36.5 %copy-start.1 = (bf16[1,64,5120]{2,1,0:T(8,128)(2,1)S(1)}, bf16[1,64,5120]{2,1,0:T(8,128)(2,1)}, u32[]{:S(2)}) copy-start(bf16[1,64,5120]{2,1,0:T(8,128)(2,1)} %param.5) | copy-start | bytes 1966084
  49.2 1.9 copy-start
  52.3 324.7 %reduce-scatter.2.cloned.1.call-start = ((), (), s32[]{:S(2)}) async-start(), calls=%async_computation.2 | async-start | bytes 11141120 | tf_op jit(solution)/shard_map/reduce_scatter | solution.py:225
  206.8 15.6 %copy-start.5 = (bf16[2,8,64,5120]{3,2,1,0:T(8,128)(2,1)S(1)}, bf16[2,8,64,5120]{3,2,1,0:T(8,128)(2,1)}, u32[]{:S(2)}) copy-start(bf16[2,8,64,5120]{3,2,1,0:T(8,128)(2,1)} %get-tuple-element.12) | copy-start | bytes 31457284
Sparse Core Ops, SparseCore 0:
  52.4 154.3 all-gather.1
  236.7 140.1 reduce-scatter.1

commit v9 on v8

--- a/solution.py
+++ b/solution.py
@@ -200,6 +200,7 @@
     scale = chosen[:, 1]
     gate = chosen[:, 2]
     xin = (normed * (1.0 + scale) + shift).astype(jnp.bfloat16)
+    x_all = lax.all_gather(xin, "mc", axis=0, tiled=True)
 
     n_mp = lax.psum(1, MP)
     n_rep = lax.psum(1, "rep")
@@ -209,8 +210,6 @@
     padded = -(-piece // 16) * 16
     flat = (piece * rows // 120, 120)
     both = exchange(both.reshape(2, n_mp, *flat).transpose(1, 0, 2, 3))
-    xin, both = lax.optimization_barrier((xin, both))
-    x_all = lax.all_gather(xin, "mc", axis=0, tiled=True)
     both = both.reshape(n_mp, 2, piece, rows).transpose(1, 2, 0, 3)
     both = jnp.pad(both, ((0, 0), (0, padded - piece), (0, 0), (0, 0))).reshape(2, padded, n_mp * rows)
     up_all, dn_all = handover(both[0], both[1], n_rep)

time: 387 us -> 404 us (1.044)
  Pallas kernels: 159 us -> 173 us
    reduce_scatter x1, waiting for transfers between devices: 140 us -> 160 us  [local(): lax.psum_scatter(jnp.dot(hidden, w_down, preferred_element_type=jnp.float...]
    all_gather x1, waiting for transfers between devices: 17.8 us -> 0.02 us  [local(): x_all = lax.all_gather(xin, 'mc', axis=0, tiled=True)]
    pallas_call x1, Pallas kernels: 32.8 us -> 48.4 us  [exchange(): pl.pallas_call(exchange_kernel, out_shape=jax.ShapeDtypeStruct(pieces.sha...]
  transfers between devices with their start and end apart: 2 -> 2, of which waited for: 2 -> 1; matrix products, arithmetic and copies ran while one was open for 3% -> 4% of each run, Pallas kernels for 33% -> 43%
where the time goes in v9:
time: 404 us; the launch traced here: 403 us
  Pallas kernels  173 us (43%)
  waiting for transfers between devices  160 us (40%)
  matrix products  32.8 us (8%)
  local copies, waits for them, and re-layouts  15.1 us (4%)
  between operations  13.6 us (3%)
  other arithmetic  9.2 us (2%)
    reduce_scatter x1, waiting for transfers between devices, local(): lax.psum_scatter(jnp.dot(hidden, w_down, preferred_element_type=jnp.float...  160 us
    pallas_call x1, Pallas kernels, handover(): pl.pallas_call(handover_kernel, out_shape=(shape, shape), in_specs=[pl.Bl...  125 us
    pallas_call x1, Pallas kernels, exchange(): pl.pallas_call(exchange_kernel, out_shape=jax.ShapeDtypeStruct(pieces.sha...  48.4 us
    dot_general x1, matrix products, local(): lax.dot_general(x_all, w_up_t, (((1,), (1,)), ((), ())), preferred_elemen...  15.6 us
    dot_general x1, matrix products, local(): jnp.dot(hidden, w_down, preferred_element_type=jnp.float32)  14.2 us
  transfers between devices with their start and end apart: 2, of which 1 were waited for; matrix products, arithmetic and copies ran while one was open for 4% of the time, Pallas kernels for 43%

profile of v9, /device:TPU:1, one launch (start us, length us, event | category | flops | bytes accessed | tf_op | source)
XLA Modules:
  0.0 403.4 jit_solution(3717398634276677591)
XLA Ops:
  6.5 0.0 all-gather.2.cloned.1.call-start
  6.5 1.3 convert_reduce_fusion
  7.9 1.4 fusion.17
  9.3 0.0 copy-start.2
  9.4 3.0 fusion.24
  12.3 0.0 copy-start
  12.4 1.9 copy-done
  14.2 1.2 fusion.23
  15.4 0.0 all-gather.2.cloned.1.call-update
  15.5 0.0 reduce-scatter.2.cloned.1.call-start
  15.5 0.0 copy-done.2
  15.5 0.1 convert_bitcast_fusion.1
  15.6 0.3 copy.11
  15.9 0.9 stack.9
  16.8 1.3 convert_element_type.34
  18.1 0.3 copy.12
  18.4 0.9 stack.10
  19.4 1.3 maximum_bitcast_fusion.src
  20.6 48.4 %shard_map.55 = bf16[32,2,72,120]{3,2,1,0:T(8,128)(2,1)} custom-call(bf16[32,2,72,120]{3,2,1,0:T(8,128)(2,1)} %maximum_bitcast_fusion.src), custom_call_target="tpu_custom_call" | custom-call | tf_op jit(solution)/shard_map/pallas_call | solution.py:58
  69.0 4.2 %reshape.35 = bf16[32,2,54,160]{3,2,1,0:T(8,128)(2,1)S(1)} reshape(bf16[32,2,72,120]{3,2,1,0:T(8,128)(2,1)} %shard_map.55) | data formatting | bytes 2211840 | tf_op jit(solution)/shard_map/reshape | solution.py:213
  73.2 0.3 pad_slice_fusion
  73.6 0.6 copy.16
  74.2 2.5 squeeze.21.dn_ref
  76.7 0.6 copy.15
  77.3 2.5 squeeze.20.up_ref
  79.8 124.6 %shard_map.56 = (bf16[2,8,64,5120]{3,2,1,0:T(8,128)(2,1)}, bf16[2,8,64,5120]{3,2,1,0:T(8,128)(2,1)}) custom-call(bf16[64,5120]{1,0:T(8,128)(2,1)} %squeeze.20.up_ref, bf16[64,5120]{1,0:T(8,128)(2,1)} %squeeze.21.dn_ref), custom_call_target="tpu_custom_call" | custom-call | tf_op jit(solution)/shard_map/pallas_call | solution.py:172
  204.4 0.0 all-gather.2.cloned.1.call-done
  204.4 15.6 %fusion.35 = f32[1024,1024]{1,0:T(8,128)S(1)} fusion(bf16[1024,5120]{1,0:T(8,128)(2,1)} %all-gather.2.cloned.1.call-done, bf16[1024,5120]{1,0:T(8,128)(2,1)} %bitcast.74), kind=kOutput, calls=%fused_computation.47 | convolution fusion | flops 10737418240 | bytes 25165824 | tf_op jit(solution)/shard_map/dot_general | solution.py:221
  220.0 14.2 %convolution_convert_fusion = bf16[1024,5120]{1,0:T(8,128)(2,1)} fusion(bf16[1024,5120]{1,0:T(8,128)(2,1)S(1)} %bitcast.73, f32[1024,1024]{1,0:T(8,128)S(1)} %fusion.35), kind=kOutput, calls=%fused_computation | convolution fusion | flops 10752098304 | bytes 25165824 | tf_op jit(solution)/shard_map/dot_general | solution.py:225
  234.3 0.0 reduce-scatter.2.cloned.1.call-update
  234.3 159.7 %reduce-scatter.2.cloned.1.call-done = bf16[64,5120]{1,0:T(8,128)(2,1)} async-done(((bf16[1024,5120]{1,0:T(8,128)(2,1)}), bf16[64,5120]{1,0:T(8,128)(2,1)}) %reduce-scatter.2.cloned.1.call-update) | async-done | bytes 655376 | tf_op jit(solution)/shard_map/reduce_scatter | solution.py:224
  394.0 2.6 fusion.27
  (6 shorter events, 0.0 us)
Async XLA Ops:
  6.5 7.7 %copy-start.1 = (bf16[1,64,5120]{2,1,0:T(8,128)(2,1)S(1)}, bf16[1,64,5120]{2,1,0:T(8,128)(2,1)}, u32[]{:S(2)}) copy-start(bf16[1,64,5120]{2,1,0:T(8,128)(2,1)} %param.5) | copy-start | bytes 1966084
  6.5 197.9 %all-gather.2.cloned.1.call-start = ((), (), s32[]{:S(2)}) async-start(), calls=%async_computation.1 | async-start | bytes 11141120 | tf_op jit(solution)/shard_map/all_gather | solution.py:203
  9.3 6.2 %copy-start.2 = (f32[160,1728]{1,0:T(8,128)S(1)}, f32[160,1728]{1,0:T(8,128)}, u32[]{:S(2)}) copy-start(f32[160,1728]{1,0:T(8,128)} %param.8) | copy-start | bytes 3317764
  12.3 1.9 copy-start
  15.5 378.5 %reduce-scatter.2.cloned.1.call-start = ((), (), s32[]{:S(2)}) async-start(), calls=%async_computation.2 | async-start | bytes 11141120 | tf_op jit(solution)/shard_map/reduce_scatter | solution.py:224
  204.4 15.6 %copy-start.3 = (bf16[2,8,64,5120]{3,2,1,0:T(8,128)(2,1)S(1)}, bf16[2,8,64,5120]{3,2,1,0:T(8,128)(2,1)}, u32[]{:S(2)}) copy-start(bf16[2,8,64,5120]{3,2,1,0:T(8,128)(2,1)} %get-tuple-element.8) | copy-start | bytes 31457284
Sparse Core Ops, SparseCore 0:
  15.6 185.2 all-gather.1
  234.4 159.5 reduce-scatter.1

commit v10 on v8

--- a/solution.py
+++ b/solution.py
@@ -208,7 +208,8 @@
     both = jnp.stack([trainer_up.astype(jnp.bfloat16).T, trainer_down.astype(jnp.bfloat16)])
     padded = -(-piece // 16) * 16
     flat = (piece * rows // 120, 120)
-    both = exchange(both.reshape(2, n_mp, *flat).transpose(1, 0, 2, 3))
+    xin, both = lax.optimization_barrier((xin, both.reshape(2, n_mp, *flat).transpose(1, 0, 2, 3)))
+    both = exchange(both)
     xin, both = lax.optimization_barrier((xin, both))
     x_all = lax.all_gather(xin, "mc", axis=0, tiled=True)
     both = both.reshape(n_mp, 2, piece, rows).transpose(1, 2, 0, 3)

time: 387 us -> 389 us (level)
  transfers between devices with their start and end apart: 2 -> 2, of which waited for: 2 -> 2; matrix products, arithmetic and copies ran while one was open for 3% -> 3% of each run, Pallas kernels for 33% -> 32%
where the time goes in v10:
time: 389 us; the launch traced here: 388 us
  Pallas kernels  159 us (41%)
  waiting for transfers between devices  159 us (41%)
  matrix products  31.5 us (8%)
  local copies, waits for them, and re-layouts  14.9 us (4%)
  between operations  13.5 us (3%)
  other arithmetic  10.4 us (3%)
    reduce_scatter x1, waiting for transfers between devices, local(): lax.psum_scatter(jnp.dot(hidden, w_down, preferred_element_type=jnp.float...  141 us
    pallas_call x1, Pallas kernels, handover(): pl.pallas_call(handover_kernel, out_shape=(shape, shape), in_specs=[pl.Bl...  126 us
    pallas_call x1, Pallas kernels, exchange(): pl.pallas_call(exchange_kernel, out_shape=jax.ShapeDtypeStruct(pieces.sha...  32.7 us
    all_gather x1, waiting for transfers between devices, local(): x_all = lax.all_gather(xin, 'mc', axis=0, tiled=True)  17.8 us
    dot_general x1, matrix products, local(): lax.dot_general(x_all, w_up_t, (((1,), (1,)), ((), ())), preferred_elemen...  15.6 us
    dot_general x1, matrix products, local(): jnp.dot(hidden, w_down, preferred_element_type=jnp.float32)  14.2 us
  transfers between devices with their start and end apart: 2, of which 2 were waited for; matrix products, arithmetic and copies ran while one was open for 3% of the time, Pallas kernels for 32%

profile of v10, /device:TPU:1, one launch (start us, length us, event | category | flops | bytes accessed | tf_op | source)
XLA Modules:
  0.0 388.5 jit_solution(2754367703077110509)
XLA Ops:
  6.5 1.3 convert_reduce_fusion
  7.8 1.4 fusion.17
  9.3 1.3 convert_bitcast_fusion.1
  10.6 0.3 copy.11
  10.9 0.0 copy-start.2
  10.9 0.0 copy-start.3
  10.9 0.9 stack.9
  11.8 1.3 convert_element_type.34
  13.2 0.3 copy.12
  13.5 0.9 stack.10
  14.4 0.0 copy-start.1
  14.4 1.3 maximum_bitcast_fusion.src
  15.7 0.0 copy-done.3
  15.7 1.8 fusion.24
  17.4 1.9 copy-done
  19.3 1.2 fusion.23
  20.5 32.7 %shard_map.55 = bf16[32,2,72,120]{3,2,1,0:T(8,128)(2,1)} custom-call(bf16[32,2,72,120]{3,2,1,0:T(8,128)(2,1)} %maximum_bitcast_fusion.src), custom_call_target="tpu_custom_call" | custom-call | tf_op jit(solution)/shard_map/pallas_call | solution.py:58
  53.2 0.0 all-gather.2.cloned.1.call-update
  53.2 0.2 reduce-scatter.2.cloned.1.call-start
  53.5 4.0 %reshape.35 = bf16[32,2,54,160]{3,2,1,0:T(8,128)(2,1)S(1)} reshape(bf16[32,2,72,120]{3,2,1,0:T(8,128)(2,1)} %shard_map.55) | data formatting | bytes 2211840 | tf_op jit(solution)/shard_map/reshape | solution.py:215
  57.5 0.3 pad_slice_fusion
  57.8 0.6 copy.16
  58.4 2.5 squeeze.21.dn_ref
  60.9 0.6 copy.15
  61.5 2.5 squeeze.20.up_ref
  64.1 126.0 %shard_map.56 = (bf16[2,8,64,5120]{3,2,1,0:T(8,128)(2,1)}, bf16[2,8,64,5120]{3,2,1,0:T(8,128)(2,1)}) custom-call(bf16[64,5120]{1,0:T(8,128)(2,1)} %squeeze.20.up_ref, bf16[64,5120]{1,0:T(8,128)(2,1)} %squeeze.21.dn_ref), custom_call_target="tpu_custom_call" | custom-call | tf_op jit(solution)/shard_map/pallas_call | solution.py:172
  190.0 17.8 %all-gather.2.cloned.1.call-done = bf16[1024,5120]{1,0:T(8,128)(2,1)} async-done(((bf16[64,5120]{1,0:T(8,128)(2,1)}), bf16[1024,5120]{1,0:T(8,128)(2,1)}) %all-gather.2.cloned.1.call-update) | async-done | bytes 10485776 | tf_op jit(solution)/shard_map/all_gather | solution.py:214
  207.9 15.6 %fusion.35 = f32[1024,1024]{1,0:T(8,128)S(1)} fusion(bf16[1024,5120]{1,0:T(8,128)(2,1)} %all-gather.2.cloned.1.call-done, bf16[1024,5120]{1,0:T(8,128)(2,1)} %bitcast.74), kind=kOutput, calls=%fused_computation.47 | convolution fusion | flops 10737418240 | bytes 25165824 | tf_op jit(solution)/shard_map/dot_general | solution.py:223
  223.5 14.2 %convolution_convert_fusion = bf16[1024,5120]{1,0:T(8,128)(2,1)} fusion(bf16[1024,5120]{1,0:T(8,128)(2,1)S(1)} %bitcast.73, f32[1024,1024]{1,0:T(8,128)S(1)} %fusion.35), kind=kOutput, calls=%fused_computation | convolution fusion | flops 10752098304 | bytes 25165824 | tf_op jit(solution)/shard_map/dot_general | solution.py:227
  237.7 0.0 reduce-scatter.2.cloned.1.call-update
  237.7 141.4 %reduce-scatter.2.cloned.1.call-done = bf16[64,5120]{1,0:T(8,128)(2,1)} async-done(((bf16[1024,5120]{1,0:T(8,128)(2,1)}), bf16[64,5120]{1,0:T(8,128)(2,1)}) %reduce-scatter.2.cloned.1.call-update) | async-done | bytes 655376 | tf_op jit(solution)/shard_map/reduce_scatter | solution.py:226
  379.1 2.6 fusion.27
  (8 shorter events, 0.0 us)
Async XLA Ops:
  6.5 201.3 %all-gather.2.cloned.1.call-start = ((), (), s32[]{:S(2)}) async-start(), calls=%async_computation.1 | async-start | bytes 11141120 | tf_op jit(solution)/shard_map/all_gather | solution.py:214
  10.9 4.7 %copy-start.2 = (f32[1,12,3,5120]{3,0,2,1:T(1,128)S(1)}, f32[1,12,3,5120]{3,0,2,1:T(1,128)}, u32[]{:S(2)}) copy-start(f32[1,12,3,5120]{3,0,2,1:T(1,128)} %param.7) | copy-start | bytes 2211844
  10.9 4.7 %copy-start.3 = (s32[1,64]{1,0:T(1,128)S(1)}, s32[1,64]{1,0:T(1,128)}, u32[]{:S(2)}) copy-start(s32[1,64]{1,0:T(1,128)} %param.6) | copy-start | bytes 772
  14.4 4.9 %copy-start.1 = (bf16[1,64,5120]{2,1,0:T(8,128)(2,1)S(1)}, bf16[1,64,5120]{2,1,0:T(8,128)(2,1)}, u32[]{:S(2)}) copy-start(bf16[1,64,5120]{2,1,0:T(8,128)(2,1)} %param.5) | copy-start | bytes 1966084
  17.4 1.9 copy-start
  53.2 325.8 %reduce-scatter.2.cloned.1.call-start = ((), (), s32[]{:S(2)}) async-start(), calls=%async_computation.2 | async-start | bytes 11141120 | tf_op jit(solution)/shard_map/reduce_scatter | solution.py:226
  207.9 15.6 %copy-start.4 = (bf16[2,8,64,5120]{3,2,1,0:T(8,128)(2,1)S(1)}, bf16[2,8,64,5120]{3,2,1,0:T(8,128)(2,1)}, u32[]{:S(2)}) copy-start(bf16[2,8,64,5120]{3,2,1,0:T(8,128)(2,1)} %get-tuple-element.16) | copy-start | bytes 31457284
Sparse Core Ops, SparseCore 0:
  53.3 154.4 all-gather.1
  237.8 141.2 reduce-scatter.1

commit v11 on v8

--- a/solution.py
+++ b/solution.py
@@ -206,15 +206,14 @@
     rows, cols = trainer_up.shape
     piece = cols // n_mp
     both = jnp.stack([trainer_up.astype(jnp.bfloat16).T, trainer_down.astype(jnp.bfloat16)])
-    padded = -(-piece // 16) * 16
     flat = (piece * rows // 120, 120)
     both = exchange(both.reshape(2, n_mp, *flat).transpose(1, 0, 2, 3))
     xin, both = lax.optimization_barrier((xin, both))
     x_all = lax.all_gather(xin, "mc", axis=0, tiled=True)
     both = both.reshape(n_mp, 2, piece, rows).transpose(1, 2, 0, 3)
-    both = jnp.pad(both, ((0, 0), (0, padded - piece), (0, 0), (0, 0))).reshape(2, padded, n_mp * rows)
+    both = both.reshape(2, piece, n_mp * rows)
     up_all, dn_all = handover(both[0], both[1], n_rep)
-    units = 2 * n_rep * padded
+    units = 2 * n_rep * piece
     w_up_t = up_all.reshape(units, n_mp * rows)
     w_down = dn_all.reshape(units, n_mp * rows)
 

time: 387 us -> 382 us (0.987)
  local copies, waits for them, and re-layouts: 14.9 us -> 30.1 us
  Pallas kernels: 159 us -> 144 us
    reshape x0 -> x2, local copies, waits for them, and re-layouts: none -> 16.7 us  [the longest x1 8.38 us: local(): w_down = dn_all.reshape(units, n_mp * rows)]
    pallas_call x1, Pallas kernels: 126 us -> 112 us  [handover(): pl.pallas_call(handover_kernel, out_shape=(shape, shape), in_specs=[pl.Bl...]
    all_gather x1, waiting for transfers between devices: 17.8 us -> 12.7 us  [local(): x_all = lax.all_gather(xin, 'mc', axis=0, tiled=True)]
  transfers between devices with their start and end apart: 2 -> 2, of which waited for: 2 -> 2; matrix products, arithmetic and copies ran while one was open for 3% -> 7% of each run, Pallas kernels for 33% -> 29%
where the time goes in v11:
time: 382 us
  waiting for transfers between devices  155 us (41%)
  Pallas kernels  144 us (38%)
  local copies, waits for them, and re-layouts  30.1 us (8%)
  matrix products  29.6 us (8%)
  between operations  13.6 us (4%)
  other arithmetic  9.21 us (2%)
    reduce_scatter x1, waiting for transfers between devices, local(): lax.psum_scatter(jnp.dot(hidden, w_down, preferred_element_type=jnp.float...  142 us
    pallas_call x1, Pallas kernels, handover(): pl.pallas_call(handover_kernel, out_shape=(shape, shape), in_specs=[pl.Bl...  112 us
    pallas_call x1, Pallas kernels, exchange(): pl.pallas_call(exchange_kernel, out_shape=jax.ShapeDtypeStruct(pieces.sha...  32.8 us
    dot_general x1, matrix products, local(): jnp.dot(hidden, w_down, preferred_element_type=jnp.float32)  14.3 us
    dot_general x1, matrix products, local(): lax.dot_general(x_all, w_up_t, (((1,), (1,)), ((), ())), preferred_elemen...  13.6 us
    all_gather x1, waiting for transfers between devices, local(): x_all = lax.all_gather(xin, 'mc', axis=0, tiled=True)  12.7 us
    reshape x1, local copies, waits for them, and re-layouts, local(): w_down = dn_all.reshape(units, n_mp * rows)  8.38 us
    reshape x1, local copies, waits for them, and re-layouts, local(): w_up_t = up_all.reshape(units, n_mp * rows)  8.32 us
  transfers between devices with their start and end apart: 2, of which 2 were waited for; matrix products, arithmetic and copies ran while one was open for 7% of the time, Pallas kernels for 29%

profile of v11, /device:TPU:1, one launch (start us, length us, event | category | flops | bytes accessed | tf_op | source)
XLA Modules:
  0.0 382.2 jit_solution(9840931142235876968)
XLA Ops:
  6.5 1.4 convert_reduce_fusion
  7.9 1.4 fusion.17
  9.4 1.3 convert_bitcast_fusion.1
  10.7 0.3 copy.11
  11.0 0.9 stack.9
  11.9 0.1 convert_element_type.32
  12.0 0.0 copy-start.3
  12.0 0.0 copy-start.5
  12.0 0.3 copy.12
  12.3 0.9 stack.10
  13.2 1.2 maximum_bitcast_fusion.src
  14.5 32.8 %shard_map.55 = bf16[32,2,72,120]{3,2,1,0:T(8,128)(2,1)} custom-call(bf16[32,2,72,120]{3,2,1,0:T(8,128)(2,1)} %maximum_bitcast_fusion.src), custom_call_target="tpu_custom_call" | custom-call | tf_op jit(solution)/shard_map/pallas_call | solution.py:58
  47.3 1.8 fusion.24
  49.1 1.8 copy-done
  51.0 1.2 fusion.23
  52.2 0.0 all-gather.2.cloned.1.call-update
  52.2 0.2 reduce-scatter.2.cloned.1.call-start
  52.4 4.0 %reshape.35 = bf16[32,2,54,160]{3,2,1,0:T(8,128)(2,1)S(1)} reshape(bf16[32,2,72,120]{3,2,1,0:T(8,128)(2,1)} %shard_map.55) | data formatting | bytes 2211840 | tf_op jit(solution)/shard_map/reshape | solution.py:213
  56.5 0.1 fusion.35
  56.6 0.2 copy.15
  56.8 2.3 squeeze.20.up_ref
  59.1 0.2 copy.16
  59.3 2.3 squeeze.21.dn_ref
  61.6 111.5 %shard_map.56 = (bf16[2,8,54,5120]{3,2,1,0:T(8,128)(2,1)}, bf16[2,8,54,5120]{3,2,1,0:T(8,128)(2,1)}) custom-call(bf16[54,5120]{1,0:T(8,128)(2,1)} %squeeze.20.up_ref, bf16[54,5120]{1,0:T(8,128)(2,1)} %squeeze.21.dn_ref), custom_call_target="tpu_custom_call" | custom-call | tf_op jit(solution)/shard_map/pallas_call | solution.py:172
  173.2 8.3 %reshape.36 = bf16[864,5120]{1,0:T(8,128)(2,1)} reshape(bf16[2,8,54,5120]{3,2,1,0:T(8,128)(2,1)} %get-tuple-element.11) | data formatting | bytes 17694720 | tf_op jit(solution)/shard_map/reshape | solution.py:217
  181.5 8.4 %reshape.37 = bf16[864,5120]{1,0:T(8,128)(2,1)} reshape(bf16[2,8,54,5120]{3,2,1,0:T(8,128)(2,1)} %get-tuple-element.12) | data formatting | bytes 17694720 | tf_op jit(solution)/shard_map/reshape | solution.py:218
  189.9 12.7 %all-gather.2.cloned.1.call-done = bf16[1024,5120]{1,0:T(8,128)(2,1)} async-done(((bf16[64,5120]{1,0:T(8,128)(2,1)}), bf16[1024,5120]{1,0:T(8,128)(2,1)}) %all-gather.2.cloned.1.call-update) | async-done | bytes 10485776 | tf_op jit(solution)/shard_map/all_gather | solution.py:212
  202.6 13.6 %fusion.36 = f32[1024,864]{0,1:T(8,128)S(1)} fusion(bf16[1024,5120]{1,0:T(8,128)(2,1)} %all-gather.2.cloned.1.call-done, bf16[864,5120]{1,0:T(8,128)(2,1)} %reshape.36), kind=kOutput, calls=%fused_computation.46 | convolution fusion | flops 9059696640 | bytes 22872064 | tf_op jit(solution)/shard_map/dot_general | solution.py:221
  216.2 14.3 %convolution_convert_fusion = bf16[1024,5120]{1,0:T(8,128)(2,1)} fusion(bf16[864,5120]{1,0:T(8,128)(2,1)S(1)} %copy-done.2, f32[1024,864]{0,1:T(8,128)S(1)} %fusion.36), kind=kOutput, calls=%fused_computation | convolution fusion | flops 9072902144 | bytes 22872064 | tf_op jit(solution)/shard_map/dot_general | solution.py:225
  230.5 0.0 reduce-scatter.2.cloned.1.call-update
  230.5 142.3 %reduce-scatter.2.cloned.1.call-done = bf16[64,5120]{1,0:T(8,128)(2,1)} async-done(((bf16[1024,5120]{1,0:T(8,128)(2,1)}), bf16[64,5120]{1,0:T(8,128)(2,1)}) %reduce-scatter.2.cloned.1.call-update) | async-done | bytes 655376 | tf_op jit(solution)/shard_map/reduce_scatter | solution.py:224
  372.8 2.6 fusion.27
  (12 shorter events, 0.0 us)
Async XLA Ops:
  6.5 5.4 %copy-start.4 = (f32[1728,160]{0,1:T(8,128)S(1)}, f32[1728,160]{0,1:T(8,128)}, u32[]{:S(2)}) copy-start(f32[1728,160]{0,1:T(8,128)} %param.9) | copy-start | bytes 3317764
  6.5 196.1 %all-gather.2.cloned.1.call-start = ((), (), s32[]{:S(2)}) async-start(), calls=%async_computation.1 | async-start | bytes 11141120 | tf_op jit(solution)/shard_map/all_gather | solution.py:212
  12.0 35.3 %copy-start.3 = (f32[1,12,3,5120]{3,0,2,1:T(1,128)S(1)}, f32[1,12,3,5120]{3,0,2,1:T(1,128)}, u32[]{:S(2)}) copy-start(f32[1,12,3,5120]{3,0,2,1:T(1,128)} %param.7) | copy-start | bytes 2211844
  12.0 35.3 %copy-start.5 = (s32[1,64]{1,0:T(1,128)S(1)}, s32[1,64]{1,0:T(1,128)}, u32[]{:S(2)}) copy-start(s32[1,64]{1,0:T(1,128)} %param.6) | copy-start | bytes 772
  14.5 36.5 %copy-start.1 = (bf16[1,64,5120]{2,1,0:T(8,128)(2,1)S(1)}, bf16[1,64,5120]{2,1,0:T(8,128)(2,1)}, u32[]{:S(2)}) copy-start(bf16[1,64,5120]{2,1,0:T(8,128)(2,1)} %param.5) | copy-start | bytes 1966084
  49.1 1.8 copy-start
  52.2 320.6 %reduce-scatter.2.cloned.1.call-start = ((), (), s32[]{:S(2)}) async-start(), calls=%async_computation.2 | async-start | bytes 11141120 | tf_op jit(solution)/shard_map/reduce_scatter | solution.py:224
  202.6 13.6 %copy-start.2 = (bf16[864,5120]{1,0:T(8,128)(2,1)S(1)}, bf16[864,5120]{1,0:T(8,128)(2,1)}, u32[]{:S(2)}) copy-start(bf16[864,5120]{1,0:T(8,128)(2,1)} %reshape.37) | copy-start | bytes 26542084
Sparse Core Ops, SparseCore 0:
  52.3 150.2 all-gather.1
  230.6 142.1 reduce-scatter.1

commit v12 on v11

--- a/solution.py
+++ b/solution.py
@@ -11,8 +11,8 @@
 MESH_ID = pl.DeviceIdType.MESH
 
 
-def exchange_kernel(src, dst, send_sem, recv_sem, local_sem):
-    n = src.shape[0]
+def exchange_kernel(up_src, dn_src, up_dst, dn_dst, send_sem, recv_sem, local_sem):
+    n = up_src.shape[0]
     me = lax.axis_index("mc") * 2 + lax.axis_index("core")
     r = lax.axis_index("rep")
 
@@ -23,50 +23,58 @@
     for k in range(1, n):
         pl.semaphore_signal(barrier, 1, device_id=dev(lax.rem(me + k, n)), device_id_type=MESH_ID)
     pl.semaphore_wait(barrier, n - 1)
-    own = pltpu.make_async_copy(src.at[me], dst.at[me], local_sem.at[0])
-    own.start()
+    pairs = ((up_src, up_dst), (dn_src, dn_dst))
+    owns = []
     sends = []
+    for i, (src, dst) in enumerate(pairs):
+        own = pltpu.make_async_copy(src.at[me], dst.at[me], local_sem.at[i])
+        own.start()
+        owns.append(own)
     for k in range(1, n):
         t = lax.rem(me + k, n)
-        cp = pltpu.make_async_remote_copy(
-            src_ref=src.at[t],
-            dst_ref=dst.at[me],
-            send_sem=send_sem.at[k],
-            recv_sem=recv_sem.at[k],
-            device_id=dev(t),
-            device_id_type=MESH_ID,
-        )
-        cp.start()
-        sends.append(cp)
+        for i, (src, dst) in enumerate(pairs):
+            cp = pltpu.make_async_remote_copy(
+                src_ref=src.at[t],
+                dst_ref=dst.at[me],
+                send_sem=send_sem.at[i, k],
+                recv_sem=recv_sem.at[i, k],
+                device_id=dev(t),
+                device_id_type=MESH_ID,
+            )
+            cp.start()
+            sends.append(cp)
     for k in range(1, n):
         s = lax.rem(me + n - k, n)
-        pltpu.make_async_remote_copy(
-            src_ref=src.at[s],
-            dst_ref=dst.at[s],
-            send_sem=send_sem.at[k],
-            recv_sem=recv_sem.at[k],
-            device_id=dev(s),
-            device_id_type=MESH_ID,
-        ).wait_recv()
+        for i, (src, dst) in enumerate(pairs):
+            pltpu.make_async_remote_copy(
+                src_ref=src.at[s],
+                dst_ref=dst.at[s],
+                send_sem=send_sem.at[i, k],
+                recv_sem=recv_sem.at[i, k],
+                device_id=dev(s),
+                device_id_type=MESH_ID,
+            ).wait_recv()
     for cp in sends:
         cp.wait_send()
-    own.wait()
-
-
-def exchange(pieces):
-    n = pieces.shape[0]
+    for own in owns:
+        own.wait()
+
+
+def exchange(up_pieces, dn_pieces):
+    n = up_pieces.shape[0]
+    shape = jax.ShapeDtypeStruct(up_pieces.shape, up_pieces.dtype)
     return pl.pallas_call(
         exchange_kernel,
-        out_shape=jax.ShapeDtypeStruct(pieces.shape, pieces.dtype),
-        in_specs=[pl.BlockSpec(memory_space=pl.ANY)],
-        out_specs=pl.BlockSpec(memory_space=pl.ANY),
+        out_shape=(shape, shape),
+        in_specs=[pl.BlockSpec(memory_space=pl.ANY)] * 2,
+        out_specs=(pl.BlockSpec(memory_space=pl.ANY),) * 2,
         scratch_shapes=[
-            pltpu.SemaphoreType.DMA((n,)),
-            pltpu.SemaphoreType.DMA((n,)),
-            pltpu.SemaphoreType.DMA((1,)),
+            pltpu.SemaphoreType.DMA((2, n)),
+            pltpu.SemaphoreType.DMA((2, n)),
+            pltpu.SemaphoreType.DMA((2,)),
         ],
         compiler_params=pltpu.CompilerParams(collective_id=1, has_side_effects=True),
-    )(pieces)
+    )(up_pieces, dn_pieces)
 
 
 def handover_kernel(up_ref, dn_ref, up_out, dn_out, send_sem, recv_sem, fwd_send, fwd_recv, local_sem):
@@ -205,14 +213,17 @@
     n_rep = lax.psum(1, "rep")
     rows, cols = trainer_up.shape
     piece = cols // n_mp
-    both = jnp.stack([trainer_up.astype(jnp.bfloat16).T, trainer_down.astype(jnp.bfloat16)])
     flat = (piece * rows // 120, 120)
-    both = exchange(both.reshape(2, n_mp, *flat).transpose(1, 0, 2, 3))
-    xin, both = lax.optimization_barrier((xin, both))
+    up_p = trainer_up.astype(jnp.bfloat16).reshape(rows, n_mp, piece).transpose(1, 2, 0)
+    dn_p = trainer_down.astype(jnp.bfloat16).reshape(n_mp, piece, rows)
+    up_p, dn_p = exchange(up_p.reshape(n_mp, *flat), dn_p.reshape(n_mp, *flat))
+    xin, up_p, dn_p = lax.optimization_barrier((xin, up_p, dn_p))
     x_all = lax.all_gather(xin, "mc", axis=0, tiled=True)
-    both = both.reshape(n_mp, 2, piece, rows).transpose(1, 2, 0, 3)
-    both = both.reshape(2, piece, n_mp * rows)
-    up_all, dn_all = handover(both[0], both[1], n_rep)
+
+    def units_by_d(p):
+        return p.reshape(n_mp, piece, rows).transpose(1, 0, 2).reshape(piece, n_mp * rows)
+
+    up_all, dn_all = handover(units_by_d(up_p), units_by_d(dn_p), n_rep)
     units = 2 * n_rep * piece
     w_up_t = up_all.reshape(units, n_mp * rows)
     w_down = dn_all.reshape(units, n_mp * rows)

time: 382 us -> 389 us (1.018)
  waiting for transfers between devices: 155 us -> 159 us
    reshape x1 -> x6, local copies, waits for them, and re-layouts: 4.03 us -> 10.5 us  [the longest x4 8.52 us: units_by_d(): p.reshape(n_mp, piece, rows).transpose(1, 0, 2).reshape(piece, n_mp * rows)]
    pallas_call x1, Pallas kernels: 32.8 us -> 37.9 us  [exchange(): pl.pallas_call(exchange_kernel, out_shape=(shape, shape), in_specs=[pl.Bl...]
    squeeze x2 -> x0, local copies, waits for them, and re-layouts: 4.6 us -> none  [local(): up_all, dn_all = handover(both[0], both[1], n_rep)]
    pallas_call x1, Pallas kernels: 112 us -> 108 us  [handover(): pl.pallas_call(handover_kernel, out_shape=(shape, shape), in_specs=[pl.Bl...]
  transfers between devices with their start and end apart: 2 -> 2, of which waited for: 2 -> 2; matrix products, arithmetic and copies ran while one was open for 7% -> 7% of each run, Pallas kernels for 29% -> 28%
where the time goes in v12:
time: 389 us
  waiting for transfers between devices  159 us (41%)
  Pallas kernels  146 us (38%)
  local copies, waits for them, and re-layouts  31.9 us (8%)
  matrix products  29.6 us (8%)
  between operations  13.6 us (3%)
  other arithmetic  9.12 us (2%)
    reduce_scatter x1, waiting for transfers between devices, local(): lax.psum_scatter(jnp.dot(hidden, w_down, preferred_element_type=jnp.float...  144 us
    pallas_call x1, Pallas kernels, handover(): pl.pallas_call(handover_kernel, out_shape=(shape, shape), in_specs=[pl.Bl...  108 us
    pallas_call x1, Pallas kernels, exchange(): pl.pallas_call(exchange_kernel, out_shape=(shape, shape), in_specs=[pl.Bl...  37.9 us
    all_gather x1, waiting for transfers between devices, local(): x_all = lax.all_gather(xin, 'mc', axis=0, tiled=True)  14.5 us
    dot_general x1, matrix products, local(): jnp.dot(hidden, w_down, preferred_element_type=jnp.float32)  14.3 us
    dot_general x1, matrix products, local(): lax.dot_general(x_all, w_up_t, (((1,), (1,)), ((), ())), preferred_elemen...  13.6 us
    reshape x4, local copies, waits for them, and re-layouts, units_by_d(): p.reshape(n_mp, piece, rows).transpose(1, 0, 2).reshape(piece, n_mp * rows)  8.52 us
    reshape x1, local copies, waits for them, and re-layouts, local(): w_up_t = up_all.reshape(units, n_mp * rows)  8.43 us
  transfers between devices with their start and end apart: 2, of which 2 were waited for; matrix products, arithmetic and copies ran while one was open for 7% of the time, Pallas kernels for 28%

profile of v12, /device:TPU:1, one launch (start us, length us, event | category | flops | bytes accessed | tf_op | source)
XLA Modules:
  0.0 388.9 jit_solution(17357049246714833664)
XLA Ops:
  6.5 1.3 convert_reduce_fusion
  7.8 1.4 fusion.17
  9.3 1.3 convert_element_type.31
  10.6 0.3 copy.12
  10.9 0.0 copy-start.3
  10.9 0.3 reshape.40
  11.2 1.7 reshape.41.up_src
  13.0 1.3 convert_element_type.32
  14.3 0.3 copy.13
  14.6 0.0 copy-start.1
  14.6 1.7 reshape_reshape.3.dn_src
  16.3 1.8 fusion.24
  18.1 1.8 copy-done
  20.0 1.2 fusion.23
  21.2 37.9 %shard_map.55 = (bf16[32,72,120]{2,1,0:T(8,128)(2,1)}, bf16[32,72,120]{2,1,0:T(8,128)(2,1)}) custom-call(bf16[32,72,120]{2,1,0:T(8,128)(2,1)} %reshape.41.up_src, bf16[32,72,120]{2,1,0:T(8,128)(2,1)} %reshape_reshape.3.dn_src), custom_call_target="tpu_custom_call" | custom-call | tf_op jit(solution)/shard_map/pallas_call | solution.py:66
  59.1 0.0 all-gather.2.cloned.1.call-update
  59.1 0.2 reduce-scatter.2.cloned.1.call-start
  59.3 2.5 reshape.42
  61.9 0.2 copy.14
  62.1 2.3 reshape.43.up_ref
  64.4 1.4 reshape.44
  65.8 0.2 copy.15
  66.0 2.3 reshape.45.dn_ref
  68.3 107.6 %shard_map.56 = (bf16[2,8,54,5120]{3,2,1,0:T(8,128)(2,1)}, bf16[2,8,54,5120]{3,2,1,0:T(8,128)(2,1)}) custom-call(bf16[54,5120]{1,0:T(8,128)(2,1)} %reshape.43.up_ref, bf16[54,5120]{1,0:T(8,128)(2,1)} %reshape.45.dn_ref), custom_call_target="tpu_custom_call" | custom-call | tf_op jit(solution)/shard_map/pallas_call | solution.py:180
  175.9 8.4 %reshape.46 = bf16[864,5120]{1,0:T(8,128)(2,1)} reshape(bf16[2,8,54,5120]{3,2,1,0:T(8,128)(2,1)} %get-tuple-element.17) | data formatting | bytes 17694720 | tf_op jit(solution)/shard_map/reshape | solution.py:228
  184.4 8.3 %reshape.47 = bf16[864,5120]{1,0:T(8,128)(2,1)} reshape(bf16[2,8,54,5120]{3,2,1,0:T(8,128)(2,1)} %get-tuple-element.18) | data formatting | bytes 17694720 | tf_op jit(solution)/shard_map/reshape | solution.py:229
  192.7 14.5 %all-gather.2.cloned.1.call-done = bf16[1024,5120]{1,0:T(8,128)(2,1)} async-done(((bf16[64,5120]{1,0:T(8,128)(2,1)}), bf16[1024,5120]{1,0:T(8,128)(2,1)}) %all-gather.2.cloned.1.call-update) | async-done | bytes 10485776 | tf_op jit(solution)/shard_map/all_gather | solution.py:221
  207.2 13.6 %fusion.35 = f32[1024,864]{0,1:T(8,128)S(1)} fusion(bf16[1024,5120]{1,0:T(8,128)(2,1)} %all-gather.2.cloned.1.call-done, bf16[864,5120]{1,0:T(8,128)(2,1)} %reshape.46), kind=kOutput, calls=%fused_computation.43 | convolution fusion | flops 9059696640 | bytes 22872064 | tf_op jit(solution)/shard_map/dot_general | solution.py:232
  220.7 14.3 %convolution_convert_fusion = bf16[1024,5120]{1,0:T(8,128)(2,1)} fusion(bf16[864,5120]{1,0:T(8,128)(2,1)S(1)} %copy-done.2, f32[1024,864]{0,1:T(8,128)S(1)} %fusion.35), kind=kOutput, calls=%fused_computation | convolution fusion | flops 9072902144 | bytes 22872064 | tf_op jit(solution)/shard_map/dot_general | solution.py:236
  235.1 0.0 reduce-scatter.2.cloned.1.call-update
  235.1 144.4 %reduce-scatter.2.cloned.1.call-done = bf16[64,5120]{1,0:T(8,128)(2,1)} async-done(((bf16[1024,5120]{1,0:T(8,128)(2,1)}), bf16[64,5120]{1,0:T(8,128)(2,1)}) %reduce-scatter.2.cloned.1.call-update) | async-done | bytes 655376 | tf_op jit(solution)/shard_map/reduce_scatter | solution.py:235
  379.5 2.6 fusion.27
  (12 shorter events, 0.0 us)
Async XLA Ops:
  6.5 200.6 %all-gather.2.cloned.1.call-start = ((), (), s32[]{:S(2)}) async-start(), calls=%async_computation.1 | async-start | bytes 11141120 | tf_op jit(solution)/shard_map/all_gather | solution.py:221
  10.9 5.4 %copy-start.3 = (f32[1,12,3,5120]{3,0,2,1:T(1,128)S(1)}, f32[1,12,3,5120]{3,0,2,1:T(1,128)}, u32[]{:S(2)}) copy-start(f32[1,12,3,5120]{3,0,2,1:T(1,128)} %param.7) | copy-start | bytes 2211844
  10.9 5.4 %copy-start.5 = (s32[1,64]{1,0:T(1,128)S(1)}, s32[1,64]{1,0:T(1,128)}, u32[]{:S(2)}) copy-start(s32[1,64]{1,0:T(1,128)} %param.6) | copy-start | bytes 772
  14.6 5.4 %copy-start.1 = (bf16[1,64,5120]{2,1,0:T(8,128)(2,1)S(1)}, bf16[1,64,5120]{2,1,0:T(8,128)(2,1)}, u32[]{:S(2)}) copy-start(bf16[1,64,5120]{2,1,0:T(8,128)(2,1)} %param.5) | copy-start | bytes 1966084
  18.1 1.8 copy-start
  59.1 5.3 %copy-start.4 = (bf16[32,72,120]{2,1,0:T(8,128)(2,1)S(1)}, bf16[32,72,120]{2,1,0:T(8,128)(2,1)}, u32[]{:S(2)}) copy-start(bf16[32,72,120]{2,1,0:T(8,128)(2,1)} %get-tuple-element.16) | copy-start | bytes 1658884
  59.1 320.4 %reduce-scatter.2.cloned.1.call-start = ((), (), s32[]{:S(2)}) async-start(), calls=%async_computation.2 | async-start | bytes 11141120 | tf_op jit(solution)/shard_map/reduce_scatter | solution.py:235
  207.2 13.6 %copy-start.2 = (bf16[864,5120]{1,0:T(8,128)(2,1)S(1)}, bf16[864,5120]{1,0:T(8,128)(2,1)}, u32[]{:S(2)}) copy-start(bf16[864,5120]{1,0:T(8,128)(2,1)} %reshape.47) | copy-start | bytes 26542084
Sparse Core Ops, SparseCore 0:
  59.2 147.8 all-gather.1
  235.2 144.2 reduce-scatter.1

commit v13 on v11

--- a/solution.py
+++ b/solution.py
@@ -206,8 +206,8 @@
     rows, cols = trainer_up.shape
     piece = cols // n_mp
     both = jnp.stack([trainer_up.astype(jnp.bfloat16).T, trainer_down.astype(jnp.bfloat16)])
-    flat = (piece * rows // 120, 120)
-    both = exchange(both.reshape(2, n_mp, *flat).transpose(1, 0, 2, 3))
+    flat = (2 * piece * rows // 128, 128)
+    both = exchange(both.reshape(2, n_mp, piece, rows).transpose(1, 0, 2, 3).reshape(n_mp, *flat))
     xin, both = lax.optimization_barrier((xin, both))
     x_all = lax.all_gather(xin, "mc", axis=0, tiled=True)
     both = both.reshape(n_mp, 2, piece, rows).transpose(1, 2, 0, 3)

time: 382 us -> 384 us (level)
  no operation moved by 1% of the time
where the time goes in v13:
time: 384 us; the launch traced here: 383 us
  waiting for transfers between devices  155 us (40%)
  Pallas kernels  143 us (37%)
  local copies, waits for them, and re-layouts  32.3 us (8%)
  matrix products  29.7 us (8%)
  between operations  13.6 us (4%)
  other arithmetic  9.5 us (2%)
    reduce_scatter x1, waiting for transfers between devices, local(): lax.psum_scatter(jnp.dot(hidden, w_down, preferred_element_type=jnp.float...  142 us
    pallas_call x1, Pallas kernels, handover(): pl.pallas_call(handover_kernel, out_shape=(shape, shape), in_specs=[pl.Bl...  111 us
    pallas_call x1, Pallas kernels, exchange(): pl.pallas_call(exchange_kernel, out_shape=jax.ShapeDtypeStruct(pieces.sha...  31.8 us
    dot_general x1, matrix products, local(): jnp.dot(hidden, w_down, preferred_element_type=jnp.float32)  14.4 us
    dot_general x1, matrix products, local(): lax.dot_general(x_all, w_up_t, (((1,), (1,)), ((), ())), preferred_elemen...  13.6 us
    all_gather x1, waiting for transfers between devices, local(): x_all = lax.all_gather(xin, 'mc', axis=0, tiled=True)  13 us
    reshape x1, local copies, waits for them, and re-layouts, local(): w_down = dn_all.reshape(units, n_mp * rows)  8.39 us
    reshape x1, local copies, waits for them, and re-layouts, local(): w_up_t = up_all.reshape(units, n_mp * rows)  8.3 us
  transfers between devices with their start and end apart: 2, of which 2 were waited for; matrix products, arithmetic and copies ran while one was open for 7% of the time, Pallas kernels for 29%

profile of v13, /device:TPU:1, one launch (start us, length us, event | category | flops | bytes accessed | tf_op | source)
XLA Modules:
  0.0 383.3 jit_solution(13897566157842644894)
XLA Ops:
  6.5 1.3 convert_reduce_fusion
  7.8 1.4 fusion.17
  9.3 1.3 convert_element_type.32
  10.6 0.3 copy.12
  10.9 0.3 stack.10
  11.2 1.3 convert_bitcast_fusion.1
  12.5 0.3 copy.11
  12.8 0.3 stack.9
  13.1 0.4 maximum_bitcast_fusion
  13.5 0.1 copy.13
  13.7 3.7 reshape.38.src
  17.3 31.8 %shard_map.55 = bf16[32,135,128]{2,1,0:T(8,128)(2,1)} custom-call(bf16[32,135,128]{2,1,0:T(8,128)(2,1)} %reshape.38.src), custom_call_target="tpu_custom_call" | custom-call | tf_op jit(solution)/shard_map/pallas_call | solution.py:58
  49.1 1.8 fusion.24
  50.9 1.8 copy-done
  52.8 1.2 fusion.23
  54.0 0.0 all-gather.2.cloned.1.call-update
  54.0 0.2 reduce-scatter.2.cloned.1.call-start
  54.2 3.7 reshape.39
  57.9 0.1 fusion.35
  58.0 0.2 copy.14
  58.2 2.3 squeeze.20.up_ref
  60.5 0.2 copy.15
  60.7 2.3 squeeze.21.dn_ref
  63.0 111.2 %shard_map.56 = (bf16[2,8,54,5120]{3,2,1,0:T(8,128)(2,1)}, bf16[2,8,54,5120]{3,2,1,0:T(8,128)(2,1)}) custom-call(bf16[54,5120]{1,0:T(8,128)(2,1)} %squeeze.20.up_ref, bf16[54,5120]{1,0:T(8,128)(2,1)} %squeeze.21.dn_ref), custom_call_target="tpu_custom_call" | custom-call | tf_op jit(solution)/shard_map/pallas_call | solution.py:172
  174.2 8.3 %reshape.40 = bf16[864,5120]{1,0:T(8,128)(2,1)} reshape(bf16[2,8,54,5120]{3,2,1,0:T(8,128)(2,1)} %get-tuple-element.11) | data formatting | bytes 17694720 | tf_op jit(solution)/shard_map/reshape | solution.py:217
  182.5 8.4 %reshape.41 = bf16[864,5120]{1,0:T(8,128)(2,1)} reshape(bf16[2,8,54,5120]{3,2,1,0:T(8,128)(2,1)} %get-tuple-element.12) | data formatting | bytes 17694720 | tf_op jit(solution)/shard_map/reshape | solution.py:218
  190.9 13.0 %all-gather.2.cloned.1.call-done = bf16[1024,5120]{1,0:T(8,128)(2,1)} async-done(((bf16[64,5120]{1,0:T(8,128)(2,1)}), bf16[1024,5120]{1,0:T(8,128)(2,1)}) %all-gather.2.cloned.1.call-update) | async-done | bytes 10485776 | tf_op jit(solution)/shard_map/all_gather | solution.py:212
  204.0 13.6 %fusion.36 = f32[1024,864]{0,1:T(8,128)S(1)} fusion(bf16[1024,5120]{1,0:T(8,128)(2,1)} %all-gather.2.cloned.1.call-done, bf16[864,5120]{1,0:T(8,128)(2,1)} %reshape.40), kind=kOutput, calls=%fused_computation.46 | convolution fusion | flops 9059696640 | bytes 22872064 | tf_op jit(solution)/shard_map/dot_general | solution.py:221
  217.5 14.4 %convolution_convert_fusion = bf16[1024,5120]{1,0:T(8,128)(2,1)} fusion(bf16[864,5120]{1,0:T(8,128)(2,1)S(1)} %copy-done.2, f32[1024,864]{0,1:T(8,128)S(1)} %fusion.36), kind=kOutput, calls=%fused_computation | convolution fusion | flops 9072902144 | bytes 22872064 | tf_op jit(solution)/shard_map/dot_general | solution.py:225
  231.9 0.0 reduce-scatter.2.cloned.1.call-update
  231.9 142.0 %reduce-scatter.2.cloned.1.call-done = bf16[64,5120]{1,0:T(8,128)(2,1)} async-done(((bf16[1024,5120]{1,0:T(8,128)(2,1)}), bf16[64,5120]{1,0:T(8,128)(2,1)}) %reduce-scatter.2.cloned.1.call-update) | async-done | bytes 655376 | tf_op jit(solution)/shard_map/reduce_scatter | solution.py:224
  373.9 2.6 fusion.27
  (12 shorter events, 0.0 us)
Async XLA Ops:
  6.5 197.4 %all-gather.2.cloned.1.call-start = ((), (), s32[]{:S(2)}) async-start(), calls=%async_computation.1 | async-start | bytes 11141120 | tf_op jit(solution)/shard_map/all_gather | solution.py:212
  13.5 35.6 %copy-start.3 = (f32[1,12,3,5120]{3,0,2,1:T(1,128)S(1)}, f32[1,12,3,5120]{3,0,2,1:T(1,128)}, u32[]{:S(2)}) copy-start(f32[1,12,3,5120]{3,0,2,1:T(1,128)} %param.7) | copy-start | bytes 2211844
  13.5 35.6 %copy-start.4 = (s32[1,64]{1,0:T(1,128)S(1)}, s32[1,64]{1,0:T(1,128)}, u32[]{:S(2)}) copy-start(s32[1,64]{1,0:T(1,128)} %param.6) | copy-start | bytes 772
  17.3 35.5 %copy-start.1 = (bf16[1,64,5120]{2,1,0:T(8,128)(2,1)S(1)}, bf16[1,64,5120]{2,1,0:T(8,128)(2,1)}, u32[]{:S(2)}) copy-start(bf16[1,64,5120]{2,1,0:T(8,128)(2,1)} %param.5) | copy-start | bytes 1966084
  50.9 1.9 copy-start
  54.0 319.9 %reduce-scatter.2.cloned.1.call-start = ((), (), s32[]{:S(2)}) async-start(), calls=%async_computation.2 | async-start | bytes 11141120 | tf_op jit(solution)/shard_map/reduce_scatter | solution.py:224
  204.0 13.6 %copy-start.2 = (bf16[864,5120]{1,0:T(8,128)(2,1)S(1)}, bf16[864,5120]{1,0:T(8,128)(2,1)}, u32[]{:S(2)}) copy-start(bf16[864,5120]{1,0:T(8,128)(2,1)} %reshape.41) | copy-start | bytes 26542084
Sparse Core Ops, SparseCore 0:
  54.1 149.7 all-gather.1
  232.0 141.8 reduce-scatter.1

commit v14 on v11

--- a/solution.py
+++ b/solution.py
@@ -191,11 +191,7 @@
     centred = as_float - average
     variance = jnp.mean(centred * centred, axis=-1, keepdims=True)
     normed = centred / jnp.sqrt(variance + 1e-06)
-    prompts_here = modulation.shape[1]
-    onehot = (prompt_ids[0][:, None] == jnp.arange(prompts_here, dtype=jnp.int32)[None, :]).astype(
-        jnp.float32
-    )
-    chosen = jnp.einsum("tp,pkd->tkd", onehot, modulation[0], precision=lax.Precision.HIGHEST)
+    chosen = jnp.take(modulation[0], prompt_ids[0], axis=0, mode="clip")
     shift = chosen[:, 0]
     scale = chosen[:, 1]
     gate = chosen[:, 2]

time: 382 us -> 408 us (1.068)
  local copies, waits for them, and re-layouts: 30.1 us -> 54.2 us
    slice x0 -> x1, local copies, waits for them, and re-layouts: none -> 10.7 us  [local(): gate = chosen[:, 2]]
    gather x0 -> x1, local copies, waits for them, and re-layouts: none -> 5.65 us  [local(): chosen = jnp.take(modulation[0], prompt_ids[0], axis=0, mode='clip')]
  transfers between devices with their start and end apart: 2 -> 2, of which waited for: 2 -> 2; matrix products, arithmetic and copies ran while one was open for 7% -> 6% of each run, Pallas kernels for 29% -> 27%
where the time goes in v14:
time: 408 us
  waiting for transfers between devices  157 us (38%)
  Pallas kernels  144 us (35%)
  local copies, waits for them, and re-layouts  54.2 us (13%)
  matrix products  27.9 us (7%)
  between operations  13.5 us (3%)
  other arithmetic  10.4 us (3%)
    reduce_scatter x1, waiting for transfers between devices, local(): lax.psum_scatter(jnp.dot(hidden, w_down, preferred_element_type=jnp.float...  144 us
    pallas_call x1, Pallas kernels, handover(): pl.pallas_call(handover_kernel, out_shape=(shape, shape), in_specs=[pl.Bl...  112 us
    pallas_call x1, Pallas kernels, exchange(): pl.pallas_call(exchange_kernel, out_shape=jax.ShapeDtypeStruct(pieces.sha...  32.7 us
    dot_general x1, matrix products, local(): jnp.dot(hidden, w_down, preferred_element_type=jnp.float32)  14.4 us
    dot_general x1, matrix products, local(): lax.dot_general(x_all, w_up_t, (((1,), (1,)), ((), ())), preferred_elemen...  13.6 us
    all_gather x1, waiting for transfers between devices, local(): x_all = lax.all_gather(xin, 'mc', axis=0, tiled=True)  12.7 us
    slice x1, local copies, waits for them, and re-layouts, local(): gate = chosen[:, 2]  10.7 us
    reshape x1, local copies, waits for them, and re-layouts, local(): w_down = dn_all.reshape(units, n_mp * rows)  8.38 us
  transfers between devices with their start and end apart: 2, of which 2 were waited for; matrix products, arithmetic and copies ran while one was open for 6% of the time, Pallas kernels for 27%

profile of v14, /device:TPU:1, one launch (start us, length us, event | category | flops | bytes accessed | tf_op | source)
XLA Modules:
  0.0 407.6 jit_solution(6349311915577792367)
XLA Ops:
  6.5 1.4 copy.42
  7.9 0.7 pad_clamp_fusion
  8.6 5.6 %gather_fusion = f32[64,3,5120]{2,1,0:T(4,128)} fusion(f32[12,3,5120]{2,1,0:T(4,128)S(1)} %bitcast.64, s32[1024]{0:T(1024)S(1)} %pad_clamp_fusion), kind=kCustom, calls=%fused_computation | custom fusion | bytes 7864576 | tf_op jit(solution)/shard_map/jit(_take)/gather | solution.py:194
  14.2 10.7 %fusion.29 = (f32[64,1,5120]{2,1,0:T(1,128)}, f32[64,1,5120]{2,1,0:T(1,128)S(1)}, f32[64,1,5120]{2,1,0:T(1,128)S(1)}) fusion(f32[64,3,5120]{2,1,0:T(4,128)} %gather_fusion), kind=kLoop, calls=%fused_computation.42 | loop fusion | bytes 7864320 | tf_op jit(solution)/shard_map/slice | solution.py:197
  24.9 0.2 convert_reduce_fusion
  25.2 0.3 fusion.17
  25.5 0.7 copy-done.3
  26.2 0.9 convert_bitcast_fusion.1
  27.1 2.3 copy.12
  29.4 2.7 stack.9
  32.0 2.1 convert_element_type.31
  34.1 2.3 copy.13
  36.4 2.7 stack.10
  39.1 2.5 maximum_bitcast_fusion.src
  41.6 32.7 %shard_map.55 = bf16[32,2,72,120]{3,2,1,0:T(8,128)(2,1)} custom-call(bf16[32,2,72,120]{3,2,1,0:T(8,128)(2,1)} %maximum_bitcast_fusion.src), custom_call_target="tpu_custom_call" | custom-call | tf_op jit(solution)/shard_map/pallas_call | solution.py:58
  74.3 1.4 fusion.23
  75.7 0.0 all-gather.2.cloned.1.call-update
  75.7 0.2 reduce-scatter.2.cloned.1.call-start
  76.0 4.0 reshape.35
  80.0 0.1 fusion.30
  80.1 0.2 copy.16
  80.3 2.3 squeeze.21.up_ref
  82.6 0.2 copy.17
  82.8 2.3 squeeze.22.dn_ref
  85.1 111.6 %shard_map.56 = (bf16[2,8,54,5120]{3,2,1,0:T(8,128)(2,1)}, bf16[2,8,54,5120]{3,2,1,0:T(8,128)(2,1)}) custom-call(bf16[54,5120]{1,0:T(8,128)(2,1)} %squeeze.21.up_ref, bf16[54,5120]{1,0:T(8,128)(2,1)} %squeeze.22.dn_ref), custom_call_target="tpu_custom_call" | custom-call | tf_op jit(solution)/shard_map/pallas_call | solution.py:172
  196.8 8.3 %reshape.36 = bf16[864,5120]{1,0:T(8,128)(2,1)} reshape(bf16[2,8,54,5120]{3,2,1,0:T(8,128)(2,1)} %get-tuple-element.11) | data formatting | bytes 17694720 | tf_op jit(solution)/shard_map/reshape | solution.py:213
  205.1 8.4 %reshape.37 = bf16[864,5120]{1,0:T(8,128)(2,1)} reshape(bf16[2,8,54,5120]{3,2,1,0:T(8,128)(2,1)} %get-tuple-element.12) | data formatting | bytes 17694720 | tf_op jit(solution)/shard_map/reshape | solution.py:214
  213.5 12.7 %all-gather.2.cloned.1.call-done = bf16[1024,5120]{1,0:T(8,128)(2,1)} async-done(((bf16[64,5120]{1,0:T(8,128)(2,1)}), bf16[1024,5120]{1,0:T(8,128)(2,1)}) %all-gather.2.cloned.1.call-update) | async-done | bytes 10485776 | tf_op jit(solution)/shard_map/all_gather | solution.py:208
  226.2 13.6 %fusion.31 = f32[1024,864]{0,1:T(8,128)S(1)} fusion(bf16[1024,5120]{1,0:T(8,128)(2,1)} %all-gather.2.cloned.1.call-done, bf16[864,5120]{1,0:T(8,128)(2,1)} %reshape.36), kind=kOutput, calls=%fused_computation.44 | convolution fusion | flops 9059696640 | bytes 22872064 | tf_op jit(solution)/shard_map/dot_general | solution.py:217
  239.8 14.4 %convolution_convert_fusion = bf16[1024,5120]{1,0:T(8,128)(2,1)} fusion(bf16[864,5120]{1,0:T(8,128)(2,1)S(1)} %copy-done.1, f32[1024,864]{0,1:T(8,128)S(1)} %fusion.31), kind=kOutput, calls=%fused_computation.1 | convolution fusion | flops 9072902144 | bytes 22872064 | tf_op jit(solution)/shard_map/dot_general | solution.py:221
  254.2 144.3 %reduce-scatter.2.cloned.1.call-done = bf16[64,5120]{1,0:T(8,128)(2,1)} async-done(((bf16[1024,5120]{1,0:T(8,128)(2,1)}), bf16[64,5120]{1,0:T(8,128)(2,1)}) %reduce-scatter.2.cloned.1.call-update) | async-done | bytes 655376 | tf_op jit(solution)/shard_map/reduce_scatter | solution.py:220
  398.5 2.2 fusion.24
  (11 shorter events, 0.0 us)
Async XLA Ops:
  6.5 219.7 %all-gather.2.cloned.1.call-start = ((), (), s32[]{:S(2)}) async-start(), calls=%async_computation.1 | async-start | bytes 11141120 | tf_op jit(solution)/shard_map/all_gather | solution.py:208
  14.2 10.7 %copy-start = (bf16[1,64,5120]{2,1,0:T(8,128)(2,1)S(1)}, bf16[1,64,5120]{2,1,0:T(8,128)(2,1)}, u32[]{:S(2)}) copy-start(bf16[1,64,5120]{2,1,0:T(8,128)(2,1)} %param.5) | copy-start | bytes 1966084
  24.9 1.3 copy-start.3
  75.7 322.8 %reduce-scatter.2.cloned.1.call-start = ((), (), s32[]{:S(2)}) async-start(), calls=%async_computation.2 | async-start | bytes 11141120 | tf_op jit(solution)/shard_map/reduce_scatter | solution.py:220
  226.2 13.6 %copy-start.1 = (bf16[864,5120]{1,0:T(8,128)(2,1)S(1)}, bf16[864,5120]{1,0:T(8,128)(2,1)}, u32[]{:S(2)}) copy-start(bf16[864,5120]{1,0:T(8,128)(2,1)} %reshape.37) | copy-start | bytes 26542084
  254.2 144.4 %copy-start.2 = (f32[64,1,5120]{2,1,0:T(1,128)S(1)}, f32[64,1,5120]{2,1,0:T(1,128)}, u32[]{:S(2)}) copy-start(f32[64,1,5120]{2,1,0:T(1,128)} %get-tuple-element.13) | copy-start | bytes 3932164
Sparse Core Ops, SparseCore 0:
  75.9 150.3 all-gather.1
  254.3 144.1 reduce-scatter.1

commit v15 on v11

--- a/solution.py
+++ b/solution.py
@@ -11,41 +11,57 @@
 MESH_ID = pl.DeviceIdType.MESH
 
 
+def _offsets(n_zh, n_y):
+    ring = lambda d, n: min(d, n - d)
+    offs = [(dz, dy, dc) for dz in range(n_zh) for dy in range(n_y) for dc in range(2) if (dz, dy, dc) != (0, 0, 0)]
+    return sorted(offs, key=lambda o: -(2 * ring(o[0], n_zh) + ring(o[1], n_y)))
+
+
 def exchange_kernel(src, dst, send_sem, recv_sem, local_sem):
     n = src.shape[0]
-    me = lax.axis_index("mc") * 2 + lax.axis_index("core")
+    n_y = 4
+    n_zh = n // (2 * n_y)
+    mc = lax.axis_index("mc")
+    zh = lax.div(mc, n_y)
+    yy = lax.rem(mc, n_y)
+    c = lax.axis_index("core")
+    me = mc * 2 + c
     r = lax.axis_index("rep")
-
-    def dev(i):
-        return (r, lax.div(i, 2), lax.rem(i, 2))
+    offsets = _offsets(n_zh, n_y)
+
+    def peer(o, sign):
+        z2 = lax.rem(zh + sign * o[0] + n_zh, n_zh)
+        y2 = lax.rem(yy + sign * o[1] + n_y, n_y)
+        c2 = lax.rem(c + sign * o[2] + 2, 2)
+        return (z2 * n_y + y2) * 2 + c2, (r, z2 * n_y + y2, c2)
 
     barrier = pltpu.get_barrier_semaphore()
-    for k in range(1, n):
-        pl.semaphore_signal(barrier, 1, device_id=dev(lax.rem(me + k, n)), device_id_type=MESH_ID)
+    for o in offsets:
+        pl.semaphore_signal(barrier, 1, device_id=peer(o, 1)[1], device_id_type=MESH_ID)
     pl.semaphore_wait(barrier, n - 1)
-    own = pltpu.make_async_copy(src.at[me], dst.at[me], local_sem.at[0])
-    own.start()
     sends = []
-    for k in range(1, n):
-        t = lax.rem(me + k, n)
+    for j, o in enumerate(offsets):
+        t, dev = peer(o, 1)
         cp = pltpu.make_async_remote_copy(
             src_ref=src.at[t],
             dst_ref=dst.at[me],
-            send_sem=send_sem.at[k],
-            recv_sem=recv_sem.at[k],
-            device_id=dev(t),
+            send_sem=send_sem.at[j],
+            recv_sem=recv_sem.at[j],
+            device_id=dev,
             device_id_type=MESH_ID,
         )
         cp.start()
         sends.append(cp)
-    for k in range(1, n):
-        s = lax.rem(me + n - k, n)
+    own = pltpu.make_async_copy(src.at[me], dst.at[me], local_sem.at[0])
+    own.start()
+    for j, o in enumerate(offsets):
+        s, dev = peer(o, -1)
         pltpu.make_async_remote_copy(
             src_ref=src.at[s],
             dst_ref=dst.at[s],
-            send_sem=send_sem.at[k],
-            recv_sem=recv_sem.at[k],
-            device_id=dev(s),
+            send_sem=send_sem.at[j],
+            recv_sem=recv_sem.at[j],
+            device_id=dev,
             device_id_type=MESH_ID,
         ).wait_recv()
     for cp in sends:

time: 382 us -> 379 us (level)
  waiting for transfers between devices: 155 us -> 150 us
    all_gather x1, waiting for transfers between devices: 12.7 us -> 4.6 us  [local(): x_all = lax.all_gather(xin, 'mc', axis=0, tiled=True)]
    pallas_call x1, Pallas kernels: 32.8 us -> 38.4 us  [exchange(): pl.pallas_call(exchange_kernel, out_shape=jax.ShapeDtypeStruct(pieces.sha...]
  transfers between devices with their start and end apart: 2 -> 2, of which waited for: 2 -> 2; matrix products, arithmetic and copies ran while one was open for 7% -> 7% of each run, Pallas kernels for 29% -> 28%
where the time goes in v15:
time: 379 us
  waiting for transfers between devices  150 us (40%)
  Pallas kernels  146 us (39%)
  local copies, waits for them, and re-layouts  30 us (8%)
  matrix products  29.6 us (8%)
  between operations  13.6 us (4%)
  other arithmetic  9.21 us (2%)
    reduce_scatter x1, waiting for transfers between devices, local(): lax.psum_scatter(jnp.dot(hidden, w_down, preferred_element_type=jnp.float...  145 us
    pallas_call x1, Pallas kernels, handover(): pl.pallas_call(handover_kernel, out_shape=(shape, shape), in_specs=[pl.Bl...  108 us
    pallas_call x1, Pallas kernels, exchange(): pl.pallas_call(exchange_kernel, out_shape=jax.ShapeDtypeStruct(pieces.sha...  38.4 us
    dot_general x1, matrix products, local(): jnp.dot(hidden, w_down, preferred_element_type=jnp.float32)  14.3 us
    dot_general x1, matrix products, local(): lax.dot_general(x_all, w_up_t, (((1,), (1,)), ((), ())), preferred_elemen...  13.6 us
    reshape x1, local copies, waits for them, and re-layouts, local(): w_down = dn_all.reshape(units, n_mp * rows)  8.3 us
    reshape x1, local copies, waits for them, and re-layouts, local(): w_up_t = up_all.reshape(units, n_mp * rows)  8.27 us
  transfers between devices with their start and end apart: 2, of which 2 were waited for; matrix products, arithmetic and copies ran while one was open for 7% of the time, Pallas kernels for 28%

profile of v15, /device:TPU:1, one launch (start us, length us, event | category | flops | bytes accessed | tf_op | source)
XLA Modules:
  0.0 379.0 jit_solution(8189221035532325796)
XLA Ops:
  6.5 1.4 convert_reduce_fusion
  7.9 1.4 fusion.17
  9.4 1.3 convert_bitcast_fusion.1
  10.7 0.3 copy.11
  11.0 0.9 stack.9
  11.9 0.1 convert_element_type.32
  12.0 0.0 copy-start.3
  12.0 0.0 copy-start.5
  12.0 0.3 copy.12
  12.3 0.9 stack.10
  13.2 1.2 maximum_bitcast_fusion.src
  14.5 38.4 %shard_map.55 = bf16[32,2,72,120]{3,2,1,0:T(8,128)(2,1)} custom-call(bf16[32,2,72,120]{3,2,1,0:T(8,128)(2,1)} %maximum_bitcast_fusion.src), custom_call_target="tpu_custom_call" | custom-call | tf_op jit(solution)/shard_map/pallas_call | solution.py:74
  53.0 1.8 fusion.24
  54.7 1.8 copy-done
  56.6 1.2 fusion.23
  57.8 0.0 all-gather.2.cloned.1.call-update
  57.8 0.2 reduce-scatter.2.cloned.1.call-start
  58.0 4.0 %reshape.35 = bf16[32,2,54,160]{3,2,1,0:T(8,128)(2,1)S(1)} reshape(bf16[32,2,72,120]{3,2,1,0:T(8,128)(2,1)} %shard_map.55) | data formatting | bytes 2211840 | tf_op jit(solution)/shard_map/reshape | solution.py:229
  62.1 0.1 fusion.35
  62.2 0.2 copy.15
  62.4 2.3 squeeze.20.up_ref
  64.7 0.2 copy.16
  64.9 2.3 squeeze.21.dn_ref
  67.2 107.9 %shard_map.56 = (bf16[2,8,54,5120]{3,2,1,0:T(8,128)(2,1)}, bf16[2,8,54,5120]{3,2,1,0:T(8,128)(2,1)}) custom-call(bf16[54,5120]{1,0:T(8,128)(2,1)} %squeeze.20.up_ref, bf16[54,5120]{1,0:T(8,128)(2,1)} %squeeze.21.dn_ref), custom_call_target="tpu_custom_call" | custom-call | tf_op jit(solution)/shard_map/pallas_call | solution.py:188
  175.1 8.3 %reshape.36 = bf16[864,5120]{1,0:T(8,128)(2,1)} reshape(bf16[2,8,54,5120]{3,2,1,0:T(8,128)(2,1)} %get-tuple-element.11) | data formatting | bytes 17694720 | tf_op jit(solution)/shard_map/reshape | solution.py:233
  183.4 8.3 %reshape.37 = bf16[864,5120]{1,0:T(8,128)(2,1)} reshape(bf16[2,8,54,5120]{3,2,1,0:T(8,128)(2,1)} %get-tuple-element.12) | data formatting | bytes 17694720 | tf_op jit(solution)/shard_map/reshape | solution.py:234
  191.7 4.6 %all-gather.2.cloned.1.call-done = bf16[1024,5120]{1,0:T(8,128)(2,1)} async-done(((bf16[64,5120]{1,0:T(8,128)(2,1)}), bf16[1024,5120]{1,0:T(8,128)(2,1)}) %all-gather.2.cloned.1.call-update) | async-done | bytes 10485776 | tf_op jit(solution)/shard_map/all_gather | solution.py:228
  196.3 13.6 %fusion.36 = f32[1024,864]{0,1:T(8,128)S(1)} fusion(bf16[1024,5120]{1,0:T(8,128)(2,1)} %all-gather.2.cloned.1.call-done, bf16[864,5120]{1,0:T(8,128)(2,1)} %reshape.36), kind=kOutput, calls=%fused_computation.46 | convolution fusion | flops 9059696640 | bytes 22872064 | tf_op jit(solution)/shard_map/dot_general | solution.py:237
  209.8 14.3 %convolution_convert_fusion = bf16[1024,5120]{1,0:T(8,128)(2,1)} fusion(bf16[864,5120]{1,0:T(8,128)(2,1)S(1)} %copy-done.2, f32[1024,864]{0,1:T(8,128)S(1)} %fusion.36), kind=kOutput, calls=%fused_computation | convolution fusion | flops 9072902144 | bytes 22872064 | tf_op jit(solution)/shard_map/dot_general | solution.py:241
  224.2 0.0 reduce-scatter.2.cloned.1.call-update
  224.2 145.4 %reduce-scatter.2.cloned.1.call-done = bf16[64,5120]{1,0:T(8,128)(2,1)} async-done(((bf16[1024,5120]{1,0:T(8,128)(2,1)}), bf16[64,5120]{1,0:T(8,128)(2,1)}) %reduce-scatter.2.cloned.1.call-update) | async-done | bytes 655376 | tf_op jit(solution)/shard_map/reduce_scatter | solution.py:240
  369.6 2.6 fusion.27
  (12 shorter events, 0.0 us)
Async XLA Ops:
  6.5 5.4 %copy-start.4 = (f32[1728,160]{0,1:T(8,128)S(1)}, f32[1728,160]{0,1:T(8,128)}, u32[]{:S(2)}) copy-start(f32[1728,160]{0,1:T(8,128)} %param.9) | copy-start | bytes 3317764
  6.5 189.7 %all-gather.2.cloned.1.call-start = ((), (), s32[]{:S(2)}) async-start(), calls=%async_computation.1 | async-start | bytes 11141120 | tf_op jit(solution)/shard_map/all_gather | solution.py:228
  12.0 40.9 %copy-start.3 = (f32[1,12,3,5120]{3,0,2,1:T(1,128)S(1)}, f32[1,12,3,5120]{3,0,2,1:T(1,128)}, u32[]{:S(2)}) copy-start(f32[1,12,3,5120]{3,0,2,1:T(1,128)} %param.7) | copy-start | bytes 2211844
  12.0 40.9 %copy-start.5 = (s32[1,64]{1,0:T(1,128)S(1)}, s32[1,64]{1,0:T(1,128)}, u32[]{:S(2)}) copy-start(s32[1,64]{1,0:T(1,128)} %param.6) | copy-start | bytes 772
  14.5 42.1 %copy-start.1 = (bf16[1,64,5120]{2,1,0:T(8,128)(2,1)S(1)}, bf16[1,64,5120]{2,1,0:T(8,128)(2,1)}, u32[]{:S(2)}) copy-start(bf16[1,64,5120]{2,1,0:T(8,128)(2,1)} %param.5) | copy-start | bytes 1966084
  54.7 1.8 copy-start
  57.8 311.8 %reduce-scatter.2.cloned.1.call-start = ((), (), s32[]{:S(2)}) async-start(), calls=%async_computation.2 | async-start | bytes 11141120 | tf_op jit(solution)/shard_map/reduce_scatter | solution.py:240
  196.3 13.6 %copy-start.2 = (bf16[864,5120]{1,0:T(8,128)(2,1)S(1)}, bf16[864,5120]{1,0:T(8,128)(2,1)}, u32[]{:S(2)}) copy-start(bf16[864,5120]{1,0:T(8,128)(2,1)} %reshape.37) | copy-start | bytes 26542084
Sparse Core Ops, SparseCore 0:
  57.9 138.2 all-gather.1
  224.3 145.2 reduce-scatter.1

commit v16 on v15

--- a/solution.py
+++ b/solution.py
@@ -95,7 +95,8 @@
     x = lax.div(me, 2)
     zl = lax.rem(me, 2)
     partner = me + 1 - 2 * zl
-    xs = [lax.rem(x + d, n_x) * 2 for d in range(1, n_x)]
+    steps = sorted(range(1, n_x), key=lambda d: -min(d, n_x - d))
+    xs = [lax.rem(x + d, n_x) * 2 for d in steps]
 
     barrier = pltpu.get_barrier_semaphore()
     for t in [partner] + [xo + zl for xo in xs]:

time: 379 us -> 379 us (level)
  no operation moved by 1% of the time
where the time goes in v16:
time: 379 us
  waiting for transfers between devices  151 us (40%)
  Pallas kernels  145 us (38%)
  local copies, waits for them, and re-layouts  30 us (8%)
  matrix products  29.6 us (8%)
  between operations  13.6 us (4%)
  other arithmetic  9.21 us (2%)
    reduce_scatter x1, waiting for transfers between devices, local(): lax.psum_scatter(jnp.dot(hidden, w_down, preferred_element_type=jnp.float...  145 us
    pallas_call x1, Pallas kernels, handover(): pl.pallas_call(handover_kernel, out_shape=(shape, shape), in_specs=[pl.Bl...  107 us
    pallas_call x1, Pallas kernels, exchange(): pl.pallas_call(exchange_kernel, out_shape=jax.ShapeDtypeStruct(pieces.sha...  38.4 us
    dot_general x1, matrix products, local(): jnp.dot(hidden, w_down, preferred_element_type=jnp.float32)  14.3 us
    dot_general x1, matrix products, local(): lax.dot_general(x_all, w_up_t, (((1,), (1,)), ((), ())), preferred_elemen...  13.6 us
    reshape x1, local copies, waits for them, and re-layouts, local(): w_down = dn_all.reshape(units, n_mp * rows)  8.3 us
    reshape x1, local copies, waits for them, and re-layouts, local(): w_up_t = up_all.reshape(units, n_mp * rows)  8.27 us
  transfers between devices with their start and end apart: 2, of which 2 were waited for; matrix products, arithmetic and copies ran while one was open for 7% of the time, Pallas kernels for 28%

profile of v16, /device:TPU:1, one launch (start us, length us, event | category | flops | bytes accessed | tf_op | source)
XLA Modules:
  0.0 379.0 jit_solution(15973278243622455939)
XLA Ops:
  6.5 1.4 convert_reduce_fusion
  7.9 1.4 fusion.17
  9.4 1.3 convert_bitcast_fusion.1
  10.7 0.3 copy.11
  11.0 0.9 stack.9
  11.9 0.1 convert_element_type.32
  12.0 0.0 copy-start.3
  12.0 0.0 copy-start.5
  12.0 0.3 copy.12
  12.3 0.9 stack.10
  13.2 1.2 maximum_bitcast_fusion.src
  14.5 38.4 %shard_map.55 = bf16[32,2,72,120]{3,2,1,0:T(8,128)(2,1)} custom-call(bf16[32,2,72,120]{3,2,1,0:T(8,128)(2,1)} %maximum_bitcast_fusion.src), custom_call_target="tpu_custom_call" | custom-call | tf_op jit(solution)/shard_map/pallas_call | solution.py:74
  53.0 1.8 fusion.24
  54.7 1.8 copy-done
  56.6 1.2 fusion.23
  57.8 0.0 all-gather.2.cloned.1.call-update
  57.8 0.2 reduce-scatter.2.cloned.1.call-start
  58.0 4.0 %reshape.35 = bf16[32,2,54,160]{3,2,1,0:T(8,128)(2,1)S(1)} reshape(bf16[32,2,72,120]{3,2,1,0:T(8,128)(2,1)} %shard_map.55) | data formatting | bytes 2211840 | tf_op jit(solution)/shard_map/reshape | solution.py:230
  62.1 0.1 fusion.35
  62.2 0.2 copy.15
  62.4 2.3 squeeze.20.up_ref
  64.7 0.2 copy.16
  64.9 2.3 squeeze.21.dn_ref
  67.2 106.8 %shard_map.56 = (bf16[2,8,54,5120]{3,2,1,0:T(8,128)(2,1)}, bf16[2,8,54,5120]{3,2,1,0:T(8,128)(2,1)}) custom-call(bf16[54,5120]{1,0:T(8,128)(2,1)} %squeeze.20.up_ref, bf16[54,5120]{1,0:T(8,128)(2,1)} %squeeze.21.dn_ref), custom_call_target="tpu_custom_call" | custom-call | tf_op jit(solution)/shard_map/pallas_call | solution.py:189
  174.0 8.3 %reshape.36 = bf16[864,5120]{1,0:T(8,128)(2,1)} reshape(bf16[2,8,54,5120]{3,2,1,0:T(8,128)(2,1)} %get-tuple-element.11) | data formatting | bytes 17694720 | tf_op jit(solution)/shard_map/reshape | solution.py:234
  182.3 8.3 %reshape.37 = bf16[864,5120]{1,0:T(8,128)(2,1)} reshape(bf16[2,8,54,5120]{3,2,1,0:T(8,128)(2,1)} %get-tuple-element.12) | data formatting | bytes 17694720 | tf_op jit(solution)/shard_map/reshape | solution.py:235
  190.6 5.7 %all-gather.2.cloned.1.call-done = bf16[1024,5120]{1,0:T(8,128)(2,1)} async-done(((bf16[64,5120]{1,0:T(8,128)(2,1)}), bf16[1024,5120]{1,0:T(8,128)(2,1)}) %all-gather.2.cloned.1.call-update) | async-done | bytes 10485776 | tf_op jit(solution)/shard_map/all_gather | solution.py:229
  196.3 13.6 %fusion.36 = f32[1024,864]{0,1:T(8,128)S(1)} fusion(bf16[1024,5120]{1,0:T(8,128)(2,1)} %all-gather.2.cloned.1.call-done, bf16[864,5120]{1,0:T(8,128)(2,1)} %reshape.36), kind=kOutput, calls=%fused_computation.46 | convolution fusion | flops 9059696640 | bytes 22872064 | tf_op jit(solution)/shard_map/dot_general | solution.py:238
  209.8 14.3 %convolution_convert_fusion = bf16[1024,5120]{1,0:T(8,128)(2,1)} fusion(bf16[864,5120]{1,0:T(8,128)(2,1)S(1)} %copy-done.2, f32[1024,864]{0,1:T(8,128)S(1)} %fusion.36), kind=kOutput, calls=%fused_computation | convolution fusion | flops 9072902144 | bytes 22872064 | tf_op jit(solution)/shard_map/dot_general | solution.py:242
  224.2 0.0 reduce-scatter.2.cloned.1.call-update
  224.2 145.4 %reduce-scatter.2.cloned.1.call-done = bf16[64,5120]{1,0:T(8,128)(2,1)} async-done(((bf16[1024,5120]{1,0:T(8,128)(2,1)}), bf16[64,5120]{1,0:T(8,128)(2,1)}) %reduce-scatter.2.cloned.1.call-update) | async-done | bytes 655376 | tf_op jit(solution)/shard_map/reduce_scatter | solution.py:241
  369.6 2.6 fusion.27
  (12 shorter events, 0.0 us)
Async XLA Ops:
  6.5 5.4 %copy-start.4 = (f32[1728,160]{0,1:T(8,128)S(1)}, f32[1728,160]{0,1:T(8,128)}, u32[]{:S(2)}) copy-start(f32[1728,160]{0,1:T(8,128)} %param.9) | copy-start | bytes 3317764
  6.5 189.7 %all-gather.2.cloned.1.call-start = ((), (), s32[]{:S(2)}) async-start(), calls=%async_computation.1 | async-start | bytes 11141120 | tf_op jit(solution)/shard_map/all_gather | solution.py:229
  12.0 40.9 %copy-start.3 = (f32[1,12,3,5120]{3,0,2,1:T(1,128)S(1)}, f32[1,12,3,5120]{3,0,2,1:T(1,128)}, u32[]{:S(2)}) copy-start(f32[1,12,3,5120]{3,0,2,1:T(1,128)} %param.7) | copy-start | bytes 2211844
  12.0 40.9 %copy-start.5 = (s32[1,64]{1,0:T(1,128)S(1)}, s32[1,64]{1,0:T(1,128)}, u32[]{:S(2)}) copy-start(s32[1,64]{1,0:T(1,128)} %param.6) | copy-start | bytes 772
  14.5 42.1 %copy-start.1 = (bf16[1,64,5120]{2,1,0:T(8,128)(2,1)S(1)}, bf16[1,64,5120]{2,1,0:T(8,128)(2,1)}, u32[]{:S(2)}) copy-start(bf16[1,64,5120]{2,1,0:T(8,128)(2,1)} %param.5) | copy-start | bytes 1966084
  54.7 1.8 copy-start
  57.8 311.8 %reduce-scatter.2.cloned.1.call-start = ((), (), s32[]{:S(2)}) async-start(), calls=%async_computation.2 | async-start | bytes 11141120 | tf_op jit(solution)/shard_map/reduce_scatter | solution.py:241
  196.3 13.6 %copy-start.2 = (bf16[864,5120]{1,0:T(8,128)(2,1)S(1)}, bf16[864,5120]{1,0:T(8,128)(2,1)}, u32[]{:S(2)}) copy-start(bf16[864,5120]{1,0:T(8,128)(2,1)} %reshape.37) | copy-start | bytes 26542084
Sparse Core Ops, SparseCore 0:
  57.9 138.2 all-gather.1
  224.3 145.2 reduce-scatter.1

commit v17 on v15

--- a/solution.py
+++ b/solution.py
@@ -17,7 +17,26 @@
     return sorted(offs, key=lambda o: -(2 * ring(o[0], n_zh) + ring(o[1], n_y)))
 
 
-def exchange_kernel(src, dst, send_sem, recv_sem, local_sem):
+def modulate(tok_ref, ids_ref, mod_ref, xin_ref, gate_ref):
+    x = tok_ref[...].astype(jnp.float32)
+    average = jnp.mean(x, axis=-1, keepdims=True)
+    centred = x - average
+    variance = jnp.mean(centred * centred, axis=-1, keepdims=True)
+    normed = centred / jnp.sqrt(variance + 1e-06)
+    ids = ids_ref[...]
+    shift = jnp.zeros_like(normed)
+    scale = jnp.zeros_like(normed)
+    gate = jnp.zeros_like(normed)
+    for p in range(mod_ref.shape[0] // 3):
+        hit = ids == p
+        shift = jnp.where(hit, mod_ref[pl.ds(3 * p, 1), :], shift)
+        scale = jnp.where(hit, mod_ref[pl.ds(3 * p + 1, 1), :], scale)
+        gate = jnp.where(hit, mod_ref[pl.ds(3 * p + 2, 1), :], gate)
+    xin_ref[...] = (normed * (1.0 + scale) + shift).astype(xin_ref.dtype)
+    gate_ref[...] = gate
+
+
+def exchange_kernel(src, tok_ref, ids_ref, mod_ref, dst, xin_ref, gate_ref, send_sem, recv_sem, local_sem):
     n = src.shape[0]
     n_y = 4
     n_zh = n // (2 * n_y)
@@ -54,6 +73,7 @@
         sends.append(cp)
     own = pltpu.make_async_copy(src.at[me], dst.at[me], local_sem.at[0])
     own.start()
+    modulate(tok_ref, ids_ref, mod_ref, xin_ref, gate_ref)
     for j, o in enumerate(offsets):
         s, dev = peer(o, -1)
         pltpu.make_async_remote_copy(
@@ -69,20 +89,25 @@
     own.wait()
 
 
-def exchange(pieces):
+def exchange(pieces, tokens, ids, mod):
     n = pieces.shape[0]
+    vmem = pl.BlockSpec(memory_space=pltpu.VMEM)
     return pl.pallas_call(
         exchange_kernel,
-        out_shape=jax.ShapeDtypeStruct(pieces.shape, pieces.dtype),
-        in_specs=[pl.BlockSpec(memory_space=pl.ANY)],
-        out_specs=pl.BlockSpec(memory_space=pl.ANY),
+        out_shape=(
+            jax.ShapeDtypeStruct(pieces.shape, pieces.dtype),
+            jax.ShapeDtypeStruct(tokens.shape, jnp.bfloat16),
+            jax.ShapeDtypeStruct(tokens.shape, jnp.float32),
+        ),
+        in_specs=[pl.BlockSpec(memory_space=pl.ANY), vmem, vmem, vmem],
+        out_specs=(pl.BlockSpec(memory_space=pl.ANY), vmem, vmem),
         scratch_shapes=[
             pltpu.SemaphoreType.DMA((n,)),
             pltpu.SemaphoreType.DMA((n,)),
             pltpu.SemaphoreType.DMA((1,)),
         ],
         compiler_params=pltpu.CompilerParams(collective_id=1, has_side_effects=True),
-    )(pieces)
+    )(pieces, tokens, ids, mod)
 
 
 def handover_kernel(up_ref, dn_ref, up_out, dn_out, send_sem, recv_sem, fwd_send, fwd_recv, local_sem):
@@ -203,28 +228,16 @@
 
 def local(tokens, prompt_ids, modulation, trainer_up, trainer_down):
     as_float = tokens[0].astype(jnp.float32)
-    average = jnp.mean(as_float, axis=-1, keepdims=True)
-    centred = as_float - average
-    variance = jnp.mean(centred * centred, axis=-1, keepdims=True)
-    normed = centred / jnp.sqrt(variance + 1e-06)
-    prompts_here = modulation.shape[1]
-    onehot = (prompt_ids[0][:, None] == jnp.arange(prompts_here, dtype=jnp.int32)[None, :]).astype(
-        jnp.float32
-    )
-    chosen = jnp.einsum("tp,pkd->tkd", onehot, modulation[0], precision=lax.Precision.HIGHEST)
-    shift = chosen[:, 0]
-    scale = chosen[:, 1]
-    gate = chosen[:, 2]
-    xin = (normed * (1.0 + scale) + shift).astype(jnp.bfloat16)
-
     n_mp = lax.psum(1, MP)
     n_rep = lax.psum(1, "rep")
     rows, cols = trainer_up.shape
     piece = cols // n_mp
     both = jnp.stack([trainer_up.astype(jnp.bfloat16).T, trainer_down.astype(jnp.bfloat16)])
     flat = (piece * rows // 120, 120)
-    both = exchange(both.reshape(2, n_mp, *flat).transpose(1, 0, 2, 3))
-    xin, both = lax.optimization_barrier((xin, both))
+    mod = modulation[0].reshape(-1, modulation.shape[-1])
+    both, xin, gate = exchange(
+        both.reshape(2, n_mp, *flat).transpose(1, 0, 2, 3), tokens[0], prompt_ids[0][:, None], mod
+    )
     x_all = lax.all_gather(xin, "mc", axis=0, tiled=True)
     both = both.reshape(n_mp, 2, piece, rows).transpose(1, 2, 0, 3)
     both = both.reshape(2, piece, n_mp * rows)

time: 379 us -> 378 us (level)
  transfers between devices with their start and end apart: 2 -> 2, of which waited for: 2 -> 2; matrix products, arithmetic and copies ran while one was open for 7% -> 7% of each run, Pallas kernels for 28% -> 29%
where the time goes in v17:
time: 378 us
  waiting for transfers between devices  150 us (40%)
  Pallas kernels  149 us (39%)
  local copies, waits for them, and re-layouts  30.1 us (8%)
  matrix products  27.9 us (7%)
  between operations  13.5 us (4%)
  other arithmetic  6.98 us (2%)
    reduce_scatter x1, waiting for transfers between devices, local(): lax.psum_scatter(jnp.dot(hidden, w_down, preferred_element_type=jnp.float...  145 us
    pallas_call x1, Pallas kernels, handover(): pl.pallas_call(handover_kernel, out_shape=(shape, shape), in_specs=[pl.Bl...  108 us
    pallas_call x1, Pallas kernels, exchange(): pl.pallas_call(exchange_kernel, out_shape=(jax.ShapeDtypeStruct(pieces.sh...  41.1 us
    dot_general x1, matrix products, local(): jnp.dot(hidden, w_down, preferred_element_type=jnp.float32)  14.3 us
    dot_general x1, matrix products, local(): lax.dot_general(x_all, w_up_t, (((1,), (1,)), ((), ())), preferred_elemen...  13.6 us
    reshape x1, local copies, waits for them, and re-layouts, local(): w_up_t = up_all.reshape(units, n_mp * rows)  8.29 us
    reshape x1, local copies, waits for them, and re-layouts, local(): w_down = dn_all.reshape(units, n_mp * rows)  8.29 us
  transfers between devices with their start and end apart: 2, of which 2 were waited for; matrix products, arithmetic and copies ran while one was open for 7% of the time, Pallas kernels for 29%

profile of v17, /device:TPU:1, one launch (start us, length us, event | category | flops | bytes accessed | tf_op | source)
XLA Modules:
  0.0 378.2 jit_solution(12167534648934498882)
XLA Ops:
  6.5 0.0 all-gather.2.cloned.1.call-start
  6.5 1.4 convert_bitcast_fusion
  8.0 0.0 copy-start.4
  8.0 0.3 copy.10
  8.3 0.9 stack.9
  9.2 0.1 convert_element_type.23
  9.3 0.0 copy-start.5
  9.3 0.3 copy.11
  9.6 0.9 stack.10
  10.5 0.0 copy-done.4
  10.5 2.1 reduce
  12.6 1.3 reshape_squeeze.3.mod_ref
  13.9 0.7 copy.14.ids_ref
  14.6 1.3 maximum_bitcast_fusion.src
  15.9 41.1 %shard_map.55 = (bf16[32,2,72,120]{3,2,1,0:T(8,128)(2,1)}, bf16[64,5120]{1,0:T(8,128)(2,1)}, f32[64,5120]{1,0:T(8,128)}) custom-call(bf16[32,2,72,120]{3,2,1,0:T(8,128)(2,1)} %maximum_bitcast_fusion.src, bf16[64,5120]{1,0:T(8,128)(2,1)} %bitcast.22, s32[64,1]{1,0:T(8,128)} %copy.14.ids_ref, f32[36,5120]{1,0:T(8,128)} %reshape_squeeze.3.mod_ref), custom_call_target="tpu_custom_call" | custom-call | tf_op jit(solution)/shard_map/pallas_call | solution.py:95
  57.0 0.0 all-gather.2.cloned.1.call-update
  57.0 0.2 reduce-scatter.2.cloned.1.call-start
  57.2 4.0 %reshape.19 = bf16[32,2,54,160]{3,2,1,0:T(8,128)(2,1)S(1)} reshape(bf16[32,2,72,120]{3,2,1,0:T(8,128)(2,1)} %get-tuple-element.12) | data formatting | bytes 2211840 | tf_op jit(solution)/shard_map/reshape | solution.py:242
  61.3 0.1 fusion.18
  61.4 0.2 copy.15
  61.6 2.3 squeeze.11.up_ref
  63.9 0.2 copy.16
  64.1 2.3 squeeze.12.dn_ref
  66.4 107.9 %shard_map.56 = (bf16[2,8,54,5120]{3,2,1,0:T(8,128)(2,1)}, bf16[2,8,54,5120]{3,2,1,0:T(8,128)(2,1)}) custom-call(bf16[54,5120]{1,0:T(8,128)(2,1)} %squeeze.11.up_ref, bf16[54,5120]{1,0:T(8,128)(2,1)} %squeeze.12.dn_ref), custom_call_target="tpu_custom_call" | custom-call | tf_op jit(solution)/shard_map/pallas_call | solution.py:213
  174.3 8.3 %reshape.20 = bf16[864,5120]{1,0:T(8,128)(2,1)} reshape(bf16[2,8,54,5120]{3,2,1,0:T(8,128)(2,1)} %get-tuple-element.13) | data formatting | bytes 17694720 | tf_op jit(solution)/shard_map/reshape | solution.py:246
  182.6 8.3 %reshape.21 = bf16[864,5120]{1,0:T(8,128)(2,1)} reshape(bf16[2,8,54,5120]{3,2,1,0:T(8,128)(2,1)} %get-tuple-element.14) | data formatting | bytes 17694720 | tf_op jit(solution)/shard_map/reshape | solution.py:247
  190.8 5.0 %all-gather.2.cloned.1.call-done = bf16[1024,5120]{1,0:T(8,128)(2,1)} async-done(((bf16[64,5120]{1,0:T(8,128)(2,1)}), bf16[1024,5120]{1,0:T(8,128)(2,1)}) %all-gather.2.cloned.1.call-update) | async-done | bytes 10485776 | tf_op jit(solution)/shard_map/all_gather | solution.py:241
  195.9 13.6 %fusion.19 = f32[1024,864]{0,1:T(8,128)S(1)} fusion(bf16[1024,5120]{1,0:T(8,128)(2,1)} %all-gather.2.cloned.1.call-done, bf16[864,5120]{1,0:T(8,128)(2,1)} %reshape.20), kind=kOutput, calls=%fused_computation.23 | convolution fusion | flops 9059696640 | bytes 22872064 | tf_op jit(solution)/shard_map/dot_general | solution.py:250
  209.4 14.3 %convolution_convert_fusion = bf16[1024,5120]{1,0:T(8,128)(2,1)} fusion(bf16[864,5120]{1,0:T(8,128)(2,1)S(1)} %copy-done, f32[1024,864]{0,1:T(8,128)S(1)} %fusion.19), kind=kOutput, calls=%fused_computation | convolution fusion | flops 9072902144 | bytes 22872064 | tf_op jit(solution)/shard_map/dot_general | solution.py:254
  223.8 0.0 reduce-scatter.2.cloned.1.call-update
  223.8 145.4 %reduce-scatter.2.cloned.1.call-done = bf16[64,5120]{1,0:T(8,128)(2,1)} async-done(((bf16[1024,5120]{1,0:T(8,128)(2,1)}), bf16[64,5120]{1,0:T(8,128)(2,1)}) %reduce-scatter.2.cloned.1.call-update) | async-done | bytes 655376 | tf_op jit(solution)/shard_map/reduce_scatter | solution.py:253
  369.2 2.1 fusion.13
  (9 shorter events, 0.0 us)
Async XLA Ops:
  6.5 2.7 copy-start.3
  6.5 189.3 %all-gather.2.cloned.1.call-start = ((), (), s32[]{:S(2)}) async-start(), calls=%async_computation.1 | async-start | bytes 11141120 | tf_op jit(solution)/shard_map/all_gather | solution.py:241
  8.0 2.5 copy-start.4
  9.3 4.7 %copy-start.5 = (s32[1,64]{1,0:T(1,128)S(1)}, s32[1,64]{1,0:T(1,128)}, u32[]{:S(2)}) copy-start(s32[1,64]{1,0:T(1,128)} %param.6) | copy-start | bytes 772
  57.0 312.2 %reduce-scatter.2.cloned.1.call-start = ((), (), s32[]{:S(2)}) async-start(), calls=%async_computation.2 | async-start | bytes 11141120 | tf_op jit(solution)/shard_map/reduce_scatter | solution.py:253
  195.9 13.6 %copy-start = (bf16[864,5120]{1,0:T(8,128)(2,1)S(1)}, bf16[864,5120]{1,0:T(8,128)(2,1)}, u32[]{:S(2)}) copy-start(bf16[864,5120]{1,0:T(8,128)(2,1)} %reshape.21) | copy-start | bytes 26542084
  223.8 145.4 %copy-start.1 = (bf16[1,64,5120]{2,1,0:T(8,128)(2,1)S(1)}, bf16[1,64,5120]{2,1,0:T(8,128)(2,1)}, u32[]{:S(2)}) copy-start(bf16[1,64,5120]{2,1,0:T(8,128)(2,1)} %param.5) | copy-start | bytes 1966084
  223.8 145.4 %copy-start.2 = (f32[64,5120]{1,0:T(8,128)S(1)}, f32[64,5120]{1,0:T(8,128)}, u32[]{:S(2)}) copy-start(f32[64,5120]{1,0:T(8,128)} %get-tuple-element.10) | copy-start | bytes 3932164
Sparse Core Ops, SparseCore 0:
  57.1 138.6 all-gather.1
  223.9 145.2 reduce-scatter.1

commit v18 on v17

--- a/solution.py
+++ b/solution.py
@@ -27,11 +27,11 @@
     shift = jnp.zeros_like(normed)
     scale = jnp.zeros_like(normed)
     gate = jnp.zeros_like(normed)
-    for p in range(mod_ref.shape[0] // 3):
+    for p in range(mod_ref.shape[1]):
         hit = ids == p
-        shift = jnp.where(hit, mod_ref[pl.ds(3 * p, 1), :], shift)
-        scale = jnp.where(hit, mod_ref[pl.ds(3 * p + 1, 1), :], scale)
-        gate = jnp.where(hit, mod_ref[pl.ds(3 * p + 2, 1), :], gate)
+        shift = jnp.where(hit, mod_ref[0, p, pl.ds(0, 1), :], shift)
+        scale = jnp.where(hit, mod_ref[0, p, pl.ds(1, 1), :], scale)
+        gate = jnp.where(hit, mod_ref[0, p, pl.ds(2, 1), :], gate)
     xin_ref[...] = (normed * (1.0 + scale) + shift).astype(xin_ref.dtype)
     gate_ref[...] = gate
 
@@ -234,9 +234,8 @@
     piece = cols // n_mp
     both = jnp.stack([trainer_up.astype(jnp.bfloat16).T, trainer_down.astype(jnp.bfloat16)])
     flat = (piece * rows // 120, 120)
-    mod = modulation[0].reshape(-1, modulation.shape[-1])
     both, xin, gate = exchange(
-        both.reshape(2, n_mp, *flat).transpose(1, 0, 2, 3), tokens[0], prompt_ids[0][:, None], mod
+        both.reshape(2, n_mp, *flat).transpose(1, 0, 2, 3), tokens[0], prompt_ids[0][:, None], modulation
     )
     x_all = lax.all_gather(xin, "mc", axis=0, tiled=True)
     both = both.reshape(n_mp, 2, piece, rows).transpose(1, 2, 0, 3)

time: 378 us -> 376 us (level)
  no operation moved by 1% of the time
where the time goes in v18:
time: 376 us
  waiting for transfers between devices  151 us (40%)
  Pallas kernels  149 us (40%)
  local copies, waits for them, and re-layouts  30.1 us (8%)
  matrix products  27.8 us (7%)
  between operations  13.5 us (4%)
  other arithmetic  4.86 us (1%)
    reduce_scatter x1, waiting for transfers between devices, local(): lax.psum_scatter(jnp.dot(hidden, w_down, preferred_element_type=jnp.float...  146 us
    pallas_call x1, Pallas kernels, handover(): pl.pallas_call(handover_kernel, out_shape=(shape, shape), in_specs=[pl.Bl...  108 us
    pallas_call x1, Pallas kernels, exchange(): pl.pallas_call(exchange_kernel, out_shape=(jax.ShapeDtypeStruct(pieces.sh...  41.1 us
    dot_general x1, matrix products, local(): jnp.dot(hidden, w_down, preferred_element_type=jnp.float32)  14.3 us
    dot_general x1, matrix products, local(): lax.dot_general(x_all, w_up_t, (((1,), (1,)), ((), ())), preferred_elemen...  13.6 us
    reshape x1, local copies, waits for them, and re-layouts, local(): w_up_t = up_all.reshape(units, n_mp * rows)  8.31 us
    reshape x1, local copies, waits for them, and re-layouts, local(): w_down = dn_all.reshape(units, n_mp * rows)  8.29 us
  transfers between devices with their start and end apart: 2, of which 2 were waited for; matrix products, arithmetic and copies ran while one was open for 7% of the time, Pallas kernels for 29%

profile of v18, /device:TPU:1, one launch (start us, length us, event | category | flops | bytes accessed | tf_op | source)
XLA Modules:
  0.0 376.2 jit_solution(11428577806334514893)
XLA Ops:
  6.5 0.0 all-gather.2.cloned.1.call-start
  6.5 1.4 convert_bitcast_fusion
  8.0 0.0 copy-start.4
  8.0 0.3 copy.11
  8.3 0.9 stack.9
  9.2 0.0 copy-done.3
  9.2 0.0 copy-start.5
  9.2 0.1 convert_element_type.23
  9.3 0.3 copy.12
  9.6 0.9 stack.10
  10.5 1.2 copy.16.mod_ref
  11.7 0.7 copy.15.ids_ref
  12.4 1.3 maximum_bitcast_fusion.src
  13.7 41.1 %shard_map.55 = (bf16[32,2,72,120]{3,2,1,0:T(8,128)(2,1)}, bf16[64,5120]{1,0:T(8,128)(2,1)}, f32[64,5120]{1,0:T(8,128)}) custom-call(bf16[32,2,72,120]{3,2,1,0:T(8,128)(2,1)} %maximum_bitcast_fusion.src, bf16[64,5120]{1,0:T(8,128)(2,1)} %bitcast.22, s32[64,1]{1,0:T(8,128)} %copy.15.ids_ref, f32[1,12,3,5120]{3,2,1,0:T(4,128)} %copy.16.mod_ref), custom_call_target="tpu_custom_call" | custom-call | tf_op jit(solution)/shard_map/pallas_call | solution.py:95
  54.8 0.0 all-gather.2.cloned.1.call-update
  54.9 0.2 reduce-scatter.2.cloned.1.call-start
  55.1 4.0 %reshape.19 = bf16[32,2,54,160]{3,2,1,0:T(8,128)(2,1)S(1)} reshape(bf16[32,2,72,120]{3,2,1,0:T(8,128)(2,1)} %get-tuple-element.12) | data formatting | bytes 2211840 | tf_op jit(solution)/shard_map/reshape | solution.py:241
  59.1 0.1 fusion.18
  59.3 0.2 copy.17
  59.5 2.3 squeeze.11.up_ref
  61.7 0.2 copy.18
  62.0 2.3 squeeze.12.dn_ref
  64.3 107.9 %shard_map.56 = (bf16[2,8,54,5120]{3,2,1,0:T(8,128)(2,1)}, bf16[2,8,54,5120]{3,2,1,0:T(8,128)(2,1)}) custom-call(bf16[54,5120]{1,0:T(8,128)(2,1)} %squeeze.11.up_ref, bf16[54,5120]{1,0:T(8,128)(2,1)} %squeeze.12.dn_ref), custom_call_target="tpu_custom_call" | custom-call | tf_op jit(solution)/shard_map/pallas_call | solution.py:213
  172.1 8.3 %reshape.20 = bf16[864,5120]{1,0:T(8,128)(2,1)} reshape(bf16[2,8,54,5120]{3,2,1,0:T(8,128)(2,1)} %get-tuple-element.13) | data formatting | bytes 17694720 | tf_op jit(solution)/shard_map/reshape | solution.py:245
  180.4 8.3 %reshape.21 = bf16[864,5120]{1,0:T(8,128)(2,1)} reshape(bf16[2,8,54,5120]{3,2,1,0:T(8,128)(2,1)} %get-tuple-element.14) | data formatting | bytes 17694720 | tf_op jit(solution)/shard_map/reshape | solution.py:246
  188.7 5.0 %all-gather.2.cloned.1.call-done = bf16[1024,5120]{1,0:T(8,128)(2,1)} async-done(((bf16[64,5120]{1,0:T(8,128)(2,1)}), bf16[1024,5120]{1,0:T(8,128)(2,1)}) %all-gather.2.cloned.1.call-update) | async-done | bytes 10485776 | tf_op jit(solution)/shard_map/all_gather | solution.py:240
  193.7 13.6 %fusion.19 = f32[1024,864]{0,1:T(8,128)S(1)} fusion(bf16[1024,5120]{1,0:T(8,128)(2,1)} %all-gather.2.cloned.1.call-done, bf16[864,5120]{1,0:T(8,128)(2,1)} %reshape.20), kind=kOutput, calls=%fused_computation.23 | convolution fusion | flops 9059696640 | bytes 22872064 | tf_op jit(solution)/shard_map/dot_general | solution.py:249
  207.3 0.0 copy-done
  207.3 14.3 %convolution_convert_fusion = bf16[1024,5120]{1,0:T(8,128)(2,1)} fusion(bf16[864,5120]{1,0:T(8,128)(2,1)S(1)} %copy-done, f32[1024,864]{0,1:T(8,128)S(1)} %fusion.19), kind=kOutput, calls=%fused_computation | convolution fusion | flops 9072902144 | bytes 22872064 | tf_op jit(solution)/shard_map/dot_general | solution.py:253
  221.6 0.0 reduce-scatter.2.cloned.1.call-update
  221.6 145.6 %reduce-scatter.2.cloned.1.call-done = bf16[64,5120]{1,0:T(8,128)(2,1)} async-done(((bf16[1024,5120]{1,0:T(8,128)(2,1)}), bf16[64,5120]{1,0:T(8,128)(2,1)}) %reduce-scatter.2.cloned.1.call-update) | async-done | bytes 655376 | tf_op jit(solution)/shard_map/reduce_scatter | solution.py:252
  367.2 2.1 fusion.13
  (8 shorter events, 0.0 us)
Async XLA Ops:
  6.5 2.7 copy-start.3
  6.5 187.2 %all-gather.2.cloned.1.call-start = ((), (), s32[]{:S(2)}) async-start(), calls=%async_computation.1 | async-start | bytes 11141120 | tf_op jit(solution)/shard_map/all_gather | solution.py:240
  8.0 2.5 copy-start.4
  9.2 2.5 copy-start.5
  54.9 312.3 %reduce-scatter.2.cloned.1.call-start = ((), (), s32[]{:S(2)}) async-start(), calls=%async_computation.2 | async-start | bytes 11141120 | tf_op jit(solution)/shard_map/reduce_scatter | solution.py:252
  193.7 13.6 %copy-start = (bf16[864,5120]{1,0:T(8,128)(2,1)S(1)}, bf16[864,5120]{1,0:T(8,128)(2,1)}, u32[]{:S(2)}) copy-start(bf16[864,5120]{1,0:T(8,128)(2,1)} %reshape.21) | copy-start | bytes 26542084
  221.6 145.6 %copy-start.1 = (bf16[1,64,5120]{2,1,0:T(8,128)(2,1)S(1)}, bf16[1,64,5120]{2,1,0:T(8,128)(2,1)}, u32[]{:S(2)}) copy-start(bf16[1,64,5120]{2,1,0:T(8,128)(2,1)} %param.5) | copy-start | bytes 1966084
  221.6 145.6 %copy-start.2 = (f32[64,5120]{1,0:T(8,128)S(1)}, f32[64,5120]{1,0:T(8,128)}, u32[]{:S(2)}) copy-start(f32[64,5120]{1,0:T(8,128)} %get-tuple-element.10) | copy-start | bytes 3932164
Sparse Core Ops, SparseCore 0:
  55.0 138.6 all-gather.1
  221.7 145.4 reduce-scatter.1

commit v19 on v18

--- a/solution.py
+++ b/solution.py
@@ -23,15 +23,14 @@
     centred = x - average
     variance = jnp.mean(centred * centred, axis=-1, keepdims=True)
     normed = centred / jnp.sqrt(variance + 1e-06)
-    ids = ids_ref[...]
-    shift = jnp.zeros_like(normed)
-    scale = jnp.zeros_like(normed)
-    gate = jnp.zeros_like(normed)
-    for p in range(mod_ref.shape[1]):
-        hit = ids == p
-        shift = jnp.where(hit, mod_ref[0, p, pl.ds(0, 1), :], shift)
-        scale = jnp.where(hit, mod_ref[0, p, pl.ds(1, 1), :], scale)
-        gate = jnp.where(hit, mod_ref[0, p, pl.ds(2, 1), :], gate)
+    prompts = mod_ref.shape[1]
+    onehot = (ids_ref[...] == lax.broadcasted_iota(jnp.int32, (1, prompts), 1)).astype(jnp.float32)
+
+    def pick(k):
+        rows = mod_ref[0, :, pl.ds(k, 1), :].reshape(prompts, -1)
+        return jnp.dot(onehot, rows, precision=lax.Precision.HIGHEST, preferred_element_type=jnp.float32)
+
+    shift, scale, gate = pick(0), pick(1), pick(2)
     xin_ref[...] = (normed * (1.0 + scale) + shift).astype(xin_ref.dtype)
     gate_ref[...] = gate
 

time: 376 us -> 377 us (level)
  no operation moved by 1% of the time
where the time goes in v19:
time: 377 us; the launch traced here: 376 us
  waiting for transfers between devices  151 us (40%)
  Pallas kernels  149 us (40%)
  local copies, waits for them, and re-layouts  30.1 us (8%)
  matrix products  27.8 us (7%)
  between operations  13.5 us (4%)
  other arithmetic  4.86 us (1%)
    reduce_scatter x1, waiting for transfers between devices, local(): lax.psum_scatter(jnp.dot(hidden, w_down, preferred_element_type=jnp.float...  146 us
    pallas_call x1, Pallas kernels, handover(): pl.pallas_call(handover_kernel, out_shape=(shape, shape), in_specs=[pl.Bl...  108 us
    pallas_call x1, Pallas kernels, exchange(): pl.pallas_call(exchange_kernel, out_shape=(jax.ShapeDtypeStruct(pieces.sh...  41.1 us
    dot_general x1, matrix products, local(): jnp.dot(hidden, w_down, preferred_element_type=jnp.float32)  14.3 us
    dot_general x1, matrix products, local(): lax.dot_general(x_all, w_up_t, (((1,), (1,)), ((), ())), preferred_elemen...  13.6 us
    reshape x1, local copies, waits for them, and re-layouts, local(): w_up_t = up_all.reshape(units, n_mp * rows)  8.31 us
    reshape x1, local copies, waits for them, and re-layouts, local(): w_down = dn_all.reshape(units, n_mp * rows)  8.29 us
  transfers between devices with their start and end apart: 2, of which 2 were waited for; matrix products, arithmetic and copies ran while one was open for 7% of the time, Pallas kernels for 29%

profile of v19, /device:TPU:1, one launch (start us, length us, event | category | flops | bytes accessed | tf_op | source)
XLA Modules:
  0.0 376.4 jit_solution(268875881479975476)
XLA Ops:
  6.5 0.0 all-gather.2.cloned.1.call-start
  6.5 1.4 convert_bitcast_fusion
  8.0 0.0 copy-start.4
  8.0 0.3 copy.11
  8.3 0.9 stack.9
  9.2 0.0 copy-done.3
  9.2 0.0 copy-start.5
  9.2 0.1 convert_element_type.23
  9.3 0.3 copy.12
  9.6 0.9 stack.10
  10.5 1.2 copy.16.mod_ref
  11.7 0.0 copy-done.5
  11.7 0.7 copy.15.ids_ref
  12.4 1.3 maximum_bitcast_fusion.src
  13.7 41.1 %shard_map.55 = (bf16[32,2,72,120]{3,2,1,0:T(8,128)(2,1)}, bf16[64,5120]{1,0:T(8,128)(2,1)}, f32[64,5120]{1,0:T(8,128)}) custom-call(bf16[32,2,72,120]{3,2,1,0:T(8,128)(2,1)} %maximum_bitcast_fusion.src, bf16[64,5120]{1,0:T(8,128)(2,1)} %bitcast.22, s32[64,1]{1,0:T(8,128)} %copy.15.ids_ref, f32[1,12,3,5120]{3,2,1,0:T(4,128)} %copy.16.mod_ref), custom_call_target="tpu_custom_call" | custom-call | tf_op jit(solution)/shard_map/pallas_call | solution.py:94
  54.8 0.0 all-gather.2.cloned.1.call-update
  54.9 0.2 reduce-scatter.2.cloned.1.call-start
  55.1 4.0 %reshape.19 = bf16[32,2,54,160]{3,2,1,0:T(8,128)(2,1)S(1)} reshape(bf16[32,2,72,120]{3,2,1,0:T(8,128)(2,1)} %get-tuple-element.12) | data formatting | bytes 2211840 | tf_op jit(solution)/shard_map/reshape | solution.py:240
  59.1 0.1 fusion.18
  59.3 0.2 copy.17
  59.5 2.3 squeeze.11.up_ref
  61.8 0.2 copy.18
  62.0 2.3 squeeze.12.dn_ref
  64.3 107.9 %shard_map.56 = (bf16[2,8,54,5120]{3,2,1,0:T(8,128)(2,1)}, bf16[2,8,54,5120]{3,2,1,0:T(8,128)(2,1)}) custom-call(bf16[54,5120]{1,0:T(8,128)(2,1)} %squeeze.11.up_ref, bf16[54,5120]{1,0:T(8,128)(2,1)} %squeeze.12.dn_ref), custom_call_target="tpu_custom_call" | custom-call | tf_op jit(solution)/shard_map/pallas_call | solution.py:212
  172.1 8.3 %reshape.20 = bf16[864,5120]{1,0:T(8,128)(2,1)} reshape(bf16[2,8,54,5120]{3,2,1,0:T(8,128)(2,1)} %get-tuple-element.13) | data formatting | bytes 17694720 | tf_op jit(solution)/shard_map/reshape | solution.py:244
  180.4 8.3 %reshape.21 = bf16[864,5120]{1,0:T(8,128)(2,1)} reshape(bf16[2,8,54,5120]{3,2,1,0:T(8,128)(2,1)} %get-tuple-element.14) | data formatting | bytes 17694720 | tf_op jit(solution)/shard_map/reshape | solution.py:245
  188.7 5.0 %all-gather.2.cloned.1.call-done = bf16[1024,5120]{1,0:T(8,128)(2,1)} async-done(((bf16[64,5120]{1,0:T(8,128)(2,1)}), bf16[1024,5120]{1,0:T(8,128)(2,1)}) %all-gather.2.cloned.1.call-update) | async-done | bytes 10485776 | tf_op jit(solution)/shard_map/all_gather | solution.py:239
  193.7 13.6 %fusion.19 = f32[1024,864]{0,1:T(8,128)S(1)} fusion(bf16[1024,5120]{1,0:T(8,128)(2,1)} %all-gather.2.cloned.1.call-done, bf16[864,5120]{1,0:T(8,128)(2,1)} %reshape.20), kind=kOutput, calls=%fused_computation.23 | convolution fusion | flops 9059696640 | bytes 22872064 | tf_op jit(solution)/shard_map/dot_general | solution.py:248
  207.3 14.3 %convolution_convert_fusion = bf16[1024,5120]{1,0:T(8,128)(2,1)} fusion(bf16[864,5120]{1,0:T(8,128)(2,1)S(1)} %copy-done, f32[1024,864]{0,1:T(8,128)S(1)} %fusion.19), kind=kOutput, calls=%fused_computation | convolution fusion | flops 9072902144 | bytes 22872064 | tf_op jit(solution)/shard_map/dot_general | solution.py:252
  221.6 0.0 reduce-scatter.2.cloned.1.call-update
  221.6 145.8 %reduce-scatter.2.cloned.1.call-done = bf16[64,5120]{1,0:T(8,128)(2,1)} async-done(((bf16[1024,5120]{1,0:T(8,128)(2,1)}), bf16[64,5120]{1,0:T(8,128)(2,1)}) %reduce-scatter.2.cloned.1.call-update) | async-done | bytes 655376 | tf_op jit(solution)/shard_map/reduce_scatter | solution.py:251
  367.4 2.1 fusion.13
  (8 shorter events, 0.0 us)
Async XLA Ops:
  6.5 2.7 copy-start.3
  6.5 187.2 %all-gather.2.cloned.1.call-start = ((), (), s32[]{:S(2)}) async-start(), calls=%async_computation.1 | async-start | bytes 11141120 | tf_op jit(solution)/shard_map/all_gather | solution.py:239
  8.0 2.5 copy-start.4
  9.2 2.5 copy-start.5
  54.9 312.6 %reduce-scatter.2.cloned.1.call-start = ((), (), s32[]{:S(2)}) async-start(), calls=%async_computation.2 | async-start | bytes 11141120 | tf_op jit(solution)/shard_map/reduce_scatter | solution.py:251
  193.7 13.6 %copy-start = (bf16[864,5120]{1,0:T(8,128)(2,1)S(1)}, bf16[864,5120]{1,0:T(8,128)(2,1)}, u32[]{:S(2)}) copy-start(bf16[864,5120]{1,0:T(8,128)(2,1)} %reshape.21) | copy-start | bytes 26542084
  221.6 145.9 %copy-start.1 = (bf16[1,64,5120]{2,1,0:T(8,128)(2,1)S(1)}, bf16[1,64,5120]{2,1,0:T(8,128)(2,1)}, u32[]{:S(2)}) copy-start(bf16[1,64,5120]{2,1,0:T(8,128)(2,1)} %param.5) | copy-start | bytes 1966084
  221.6 145.9 %copy-start.2 = (f32[64,5120]{1,0:T(8,128)S(1)}, f32[64,5120]{1,0:T(8,128)}, u32[]{:S(2)}) copy-start(f32[64,5120]{1,0:T(8,128)} %get-tuple-element.10) | copy-start | bytes 3932164
Sparse Core Ops, SparseCore 0:
  55.0 138.6 all-gather.1
  221.7 145.6 reduce-scatter.1

commit v20 on v19

--- a/solution.py
+++ b/solution.py
@@ -24,11 +24,14 @@
     variance = jnp.mean(centred * centred, axis=-1, keepdims=True)
     normed = centred / jnp.sqrt(variance + 1e-06)
     prompts = mod_ref.shape[1]
-    onehot = (ids_ref[...] == lax.broadcasted_iota(jnp.int32, (1, prompts), 1)).astype(jnp.float32)
+    onehot_t = (lax.broadcasted_iota(jnp.int32, (prompts, 1), 0) == ids_ref[...]).astype(jnp.float32)
 
     def pick(k):
         rows = mod_ref[0, :, pl.ds(k, 1), :].reshape(prompts, -1)
-        return jnp.dot(onehot, rows, precision=lax.Precision.HIGHEST, preferred_element_type=jnp.float32)
+        return lax.dot_general(
+            onehot_t, rows, (((0,), (0,)), ((), ())),
+            precision=lax.Precision.HIGHEST, preferred_element_type=jnp.float32,
+        )
 
     shift, scale, gate = pick(0), pick(1), pick(2)
     xin_ref[...] = (normed * (1.0 + scale) + shift).astype(xin_ref.dtype)
@@ -234,7 +237,7 @@
     both = jnp.stack([trainer_up.astype(jnp.bfloat16).T, trainer_down.astype(jnp.bfloat16)])
     flat = (piece * rows // 120, 120)
     both, xin, gate = exchange(
-        both.reshape(2, n_mp, *flat).transpose(1, 0, 2, 3), tokens[0], prompt_ids[0][:, None], modulation
+        both.reshape(2, n_mp, *flat).transpose(1, 0, 2, 3), tokens[0], prompt_ids, modulation
     )
     x_all = lax.all_gather(xin, "mc", axis=0, tiled=True)
     both = both.reshape(n_mp, 2, piece, rows).transpose(1, 2, 0, 3)

time: 377 us -> 378 us (level)
  no operation moved by 1% of the time
where the time goes in v20:
time: 378 us
  waiting for transfers between devices  152 us (40%)
  Pallas kernels  149 us (39%)
  local copies, waits for them, and re-layouts  30.5 us (8%)
  matrix products  27.9 us (7%)
  between operations  13.5 us (4%)
  other arithmetic  4.84 us (1%)
    reduce_scatter x1, waiting for transfers between devices, local(): lax.psum_scatter(jnp.dot(hidden, w_down, preferred_element_type=jnp.float...  147 us
    pallas_call x1, Pallas kernels, handover(): pl.pallas_call(handover_kernel, out_shape=(shape, shape), in_specs=[pl.Bl...  108 us
    pallas_call x1, Pallas kernels, exchange(): pl.pallas_call(exchange_kernel, out_shape=(jax.ShapeDtypeStruct(pieces.sh...  41.1 us
    dot_general x1, matrix products, local(): jnp.dot(hidden, w_down, preferred_element_type=jnp.float32)  14.3 us
    dot_general x1, matrix products, local(): lax.dot_general(x_all, w_up_t, (((1,), (1,)), ((), ())), preferred_elemen...  13.6 us
    reshape x1, local copies, waits for them, and re-layouts, local(): w_up_t = up_all.reshape(units, n_mp * rows)  8.29 us
    reshape x1, local copies, waits for them, and re-layouts, local(): w_down = dn_all.reshape(units, n_mp * rows)  8.28 us
  transfers between devices with their start and end apart: 2, of which 2 were waited for; matrix products, arithmetic and copies ran while one was open for 7% of the time, Pallas kernels for 29%

profile of v20, /device:TPU:1, one launch (start us, length us, event | category | flops | bytes accessed | tf_op | source)
XLA Modules:
  0.0 378.1 jit_solution(7508620862448815831)
XLA Ops:
  6.5 0.0 copy-start.3
  6.5 0.0 all-gather.2.cloned.1.call-start
  6.5 1.4 convert_bitcast_fusion
  8.0 0.3 copy.10
  8.3 0.9 stack.9
  9.2 0.0 copy-done.3
  9.2 0.1 convert_element_type.23
  9.3 0.3 copy.11
  9.6 0.9 stack.10
  10.5 2.4 copy.14.mod_ref
  12.8 1.3 maximum_bitcast_fusion.src
  14.1 41.1 %shard_map.55 = (bf16[32,2,72,120]{3,2,1,0:T(8,128)(2,1)}, bf16[64,5120]{1,0:T(8,128)(2,1)}, f32[64,5120]{1,0:T(8,128)}) custom-call(bf16[32,2,72,120]{3,2,1,0:T(8,128)(2,1)} %maximum_bitcast_fusion.src, bf16[64,5120]{1,0:T(8,128)(2,1)} %bitcast.21, s32[1,64]{1,0:T(1,128)} %ids_ref.1, f32[1,12,3,5120]{3,2,1,0:T(4,128)} %copy.14.mod_ref), custom_call_target="tpu_custom_call" | custom-call | tf_op jit(solution)/shard_map/pallas_call | solution.py:97
  55.2 0.0 all-gather.2.cloned.1.call-update
  55.2 0.2 reduce-scatter.2.cloned.1.call-start
  55.5 4.0 %reshape.19 = bf16[32,2,54,160]{3,2,1,0:T(8,128)(2,1)S(1)} reshape(bf16[32,2,72,120]{3,2,1,0:T(8,128)(2,1)} %get-tuple-element.12) | data formatting | bytes 2211840 | tf_op jit(solution)/shard_map/reshape | solution.py:243
  59.5 0.1 fusion.18
  59.6 0.2 copy.15
  59.8 2.3 squeeze.11.up_ref
  62.1 0.2 copy.16
  62.3 2.3 squeeze.12.dn_ref
  64.6 107.9 %shard_map.56 = (bf16[2,8,54,5120]{3,2,1,0:T(8,128)(2,1)}, bf16[2,8,54,5120]{3,2,1,0:T(8,128)(2,1)}) custom-call(bf16[54,5120]{1,0:T(8,128)(2,1)} %squeeze.11.up_ref, bf16[54,5120]{1,0:T(8,128)(2,1)} %squeeze.12.dn_ref), custom_call_target="tpu_custom_call" | custom-call | tf_op jit(solution)/shard_map/pallas_call | solution.py:215
  172.5 8.3 %reshape.20 = bf16[864,5120]{1,0:T(8,128)(2,1)} reshape(bf16[2,8,54,5120]{3,2,1,0:T(8,128)(2,1)} %get-tuple-element.13) | data formatting | bytes 17694720 | tf_op jit(solution)/shard_map/reshape | solution.py:247
  180.8 8.3 %reshape.21 = bf16[864,5120]{1,0:T(8,128)(2,1)} reshape(bf16[2,8,54,5120]{3,2,1,0:T(8,128)(2,1)} %get-tuple-element.14) | data formatting | bytes 17694720 | tf_op jit(solution)/shard_map/reshape | solution.py:248
  189.1 5.0 %all-gather.2.cloned.1.call-done = bf16[1024,5120]{1,0:T(8,128)(2,1)} async-done(((bf16[64,5120]{1,0:T(8,128)(2,1)}), bf16[1024,5120]{1,0:T(8,128)(2,1)}) %all-gather.2.cloned.1.call-update) | async-done | bytes 10485776 | tf_op jit(solution)/shard_map/all_gather | solution.py:242
  194.1 13.6 %fusion.19 = f32[1024,864]{0,1:T(8,128)S(1)} fusion(bf16[1024,5120]{1,0:T(8,128)(2,1)} %all-gather.2.cloned.1.call-done, bf16[864,5120]{1,0:T(8,128)(2,1)} %reshape.20), kind=kOutput, calls=%fused_computation.23 | convolution fusion | flops 9059696640 | bytes 22872064 | tf_op jit(solution)/shard_map/dot_general | solution.py:251
  207.7 0.0 copy-done
  207.7 14.3 %convolution_convert_fusion = bf16[1024,5120]{1,0:T(8,128)(2,1)} fusion(bf16[864,5120]{1,0:T(8,128)(2,1)S(1)} %copy-done, f32[1024,864]{0,1:T(8,128)S(1)} %fusion.19), kind=kOutput, calls=%fused_computation | convolution fusion | flops 9072902144 | bytes 22872064 | tf_op jit(solution)/shard_map/dot_general | solution.py:255
  222.0 0.0 reduce-scatter.2.cloned.1.call-update
  222.0 147.1 %reduce-scatter.2.cloned.1.call-done = bf16[64,5120]{1,0:T(8,128)(2,1)} async-done(((bf16[1024,5120]{1,0:T(8,128)(2,1)}), bf16[64,5120]{1,0:T(8,128)(2,1)}) %reduce-scatter.2.cloned.1.call-update) | async-done | bytes 655376 | tf_op jit(solution)/shard_map/reduce_scatter | solution.py:254
  369.1 0.0 copy-done.1
  369.1 0.0 copy-done.2
  369.1 2.1 fusion.13
  (3 shorter events, 0.0 us)
Async XLA Ops:
  6.5 2.6 copy-start.3
  6.5 187.5 %all-gather.2.cloned.1.call-start = ((), (), s32[]{:S(2)}) async-start(), calls=%async_computation.1 | async-start | bytes 11141120 | tf_op jit(solution)/shard_map/all_gather | solution.py:242
  55.2 313.9 %reduce-scatter.2.cloned.1.call-start = ((), (), s32[]{:S(2)}) async-start(), calls=%async_computation.2 | async-start | bytes 11141120 | tf_op jit(solution)/shard_map/reduce_scatter | solution.py:254
  194.1 13.6 %copy-start = (bf16[864,5120]{1,0:T(8,128)(2,1)S(1)}, bf16[864,5120]{1,0:T(8,128)(2,1)}, u32[]{:S(2)}) copy-start(bf16[864,5120]{1,0:T(8,128)(2,1)} %reshape.21) | copy-start | bytes 26542084
  222.0 147.1 %copy-start.1 = (bf16[1,64,5120]{2,1,0:T(8,128)(2,1)S(1)}, bf16[1,64,5120]{2,1,0:T(8,128)(2,1)}, u32[]{:S(2)}) copy-start(bf16[1,64,5120]{2,1,0:T(8,128)(2,1)} %param.5) | copy-start | bytes 1966084
  222.0 147.1 %copy-start.2 = (f32[64,5120]{1,0:T(8,128)S(1)}, f32[64,5120]{1,0:T(8,128)}, u32[]{:S(2)}) copy-start(f32[64,5120]{1,0:T(8,128)} %get-tuple-element.10) | copy-start | bytes 3932164
Sparse Core Ops, SparseCore 0:
  55.4 138.6 all-gather.1
  222.1 146.9 reduce-scatter.1
